TPU v7x, 32 devices: a whole 2x2x4 slice. The times are simulated.
32 devices in a mesh: row: 8 (over z, core), col: 4 (over y, x).
Axes of the slice: x: 2, y: 2, z: 4, core: 2. Of those that a mesh axis runs over, the one named last changes fastest.
Arguments:
- running_cost: float32 [2048, 2048], P('row', 'col'), may hold values from 0.5 to 7.5, as said below
- control_x: float32 [2048, 2048], P('row', 'col'), may hold values from -6 to 6
- control_y: float32 [2048, 2048], P('row', 'col'), may hold values from -6 to 6
- prior_density: float32 [2048, 2048], P('row', 'col'), may hold values from 0.5 to 2
Outputs:
- value_field: float32 [2048, 2048], P('row', 'col')
- density: float32 [2048, 2048], P('row', 'col')
- ergodic: float32 [], replicated
Inputs may be any that keep to these rules, and one draw needn't show every extreme that they name: `running_cost`: strictly positive.
All inputs are finite; a program needn't handle non-finite values.
Results may differ from a plain program's by a relative error of at most 0.0003.
Values sent between devices are 32-bit elements; how exact they have to be, the bound alone decides.
No kernel may reach another device: no remote copies, remote signals or barrier semaphores. Data moves between devices by JAX's collectives and lax.ppermute only.
A program may use at most 64 MiB of HBM per device.

v0:
```python
import jax
import jax.numpy as jnp
from jax import lax
from jax.sharding import PartitionSpec as P

ITERS = 3


discount_rate = 0.05
diffusion = 0.25


def padded_2(cells, sides, width):
    for axis, dim in sides:
        count = lax.axis_size(axis)
        ends = count - 1
        head = lax.slice_in_dim(cells, 0, width, axis=dim)
        tail = lax.slice_in_dim(cells, cells.shape[dim] - width, cells.shape[dim], axis=dim)
        cells = jnp.concatenate(
            [
                lax.ppermute(tail, axis, [(i, (i + 1) % count) for i in range(ends)]),
                cells,
                lax.ppermute(head, axis, [((i + 1) % count, i) for i in range(ends)]),
            ],
            axis=dim,
        )
    return cells


def interior(padded):
    return padded[1:-1, 1:-1]


def neighbours(padded):
    return (padded[2:, 1:-1], padded[:-2, 1:-1], padded[1:-1, 2:], padded[1:-1, :-2])


def coefficients(conduct, padded_conduct, zeroth):
    weights = tuple(
        (diffusion * 0.5 * (conduct + outside) for outside in neighbours(padded_conduct))
    )
    center = zeroth + (weights[0] + weights[1] + (weights[2] + weights[3]))
    return (center,) + weights


def operator_apply(padded, coeffs):
    beside = neighbours(padded)
    inflow = (
        coeffs[1] * beside[0]
        + coeffs[2] * beside[1]
        + (coeffs[3] * beside[2] + coeffs[4] * beside[3])
    )
    return coeffs[0] * interior(padded) - inflow


def operate(source, coeffs):
    padded = padded_2(source, (("row", 0), ("col", 1)), 1)
    return (padded, operator_apply(padded, coeffs))


def products(residual, applied):
    return lax.psum((jnp.sum(residual * residual), jnp.sum(residual * applied)), ("row", "col"))


def conjugate(coeffs, forcing):
    solution = jnp.zeros_like(forcing)
    padded_solution = jnp.zeros((forcing.shape[0] + 2, forcing.shape[1] + 2), jnp.float32)
    residual = forcing
    padded_res, applied = operate(residual, coeffs)
    norm_now, product = products(residual, applied)
    step_size = norm_now / product
    direction, image_dir, padded_dir = (residual, applied, padded_res)
    for iteration in range(ITERS):
        solution = solution + step_size * direction
        if iteration + 1 < ITERS:
            residual = residual - step_size * image_dir
            padded_res, applied = operate(residual, coeffs)
            norm_next, product = products(residual, applied)
            beta_ratio = norm_next / norm_now
            step_size = norm_next / (product - beta_ratio * norm_next / step_size)
            direction = residual + beta_ratio * direction
            image_dir = applied + beta_ratio * image_dir
            norm_now = norm_next
    return (solution, padded_solution)


def body(running_cost, control_x, control_y, prior_density):
    control_cost = 0.5 * (control_x * control_x + control_y * control_y)
    conduct = 1.0 + control_cost
    forcing = running_cost + control_cost
    padded_conduct = padded_2(conduct, (("row", 0), ("col", 1)), 1)
    bellman = coefficients(conduct, padded_conduct, discount_rate)
    value_field, padded_solution = conjugate(bellman, forcing)
    padded_value = padded_2(value_field, (("row", 0), ("col", 1)), 1)
    beside = neighbours(padded_value)
    slope_row = 0.5 * (beside[0] - beside[1])
    slope_col = 0.5 * (beside[2] - beside[3])
    congestion = (slope_row * slope_row + slope_col * slope_col) / (2.0 * diffusion)
    planck = coefficients(conduct, padded_conduct, discount_rate + congestion)
    weighted = jnp.sum(prior_density * (forcing - discount_rate * value_field))
    weight_total = jnp.sum(prior_density)
    density, unused = conjugate(planck, prior_density)
    totals = lax.psum((weighted, weight_total), ("row", "col"))
    ergodic = totals[0] / totals[1]
    return (value_field, density, ergodic)


def solution(mesh):
    in_specs = (P("row", "col"), P("row", "col"), P("row", "col"), P("row", "col"))
    out_specs = (P("row", "col"), P("row", "col"), P())
    return jax.shard_map(body, mesh=mesh, in_specs=in_specs, out_specs=out_specs, check_vma=False)
```

profile of v0, /device:TPU:0, one launch (start us, length us, event | category | flops | bytes accessed | tf_op | source)
XLA Modules:
  0.0 410.6 jit_solution(13232752948674389063)
XLA Ops:
  0.6 1.5 broadcast_add_fusion
  2.2 2.4 collective-permute-start.5
  5.9 5.2 %collective-permute-start.1 = (f32[1,512]{1,0:T(1,128)S(1)}, f32[1,512]{1,0:T(1,128)S(1)}, u32[]{:S(2)}, u32[]{:S(2)}) collective-permute-start(f32[1,512]{1,0:T(1,128)S(1)} %get-tuple-element.65), channel_id=1, source_target_pairs={{0,4},{4,8},{8,12},{12,16},{16,20},{20,24},{24,28},{1,5},{5,9},{9,... | collective-permute-start | bytes 6152 | tf_op jit(solution)/shard_map/ppermute | solution.py:21
  13.8 4.6 %collective-permute-start.7 = (f32[258,1]{1,0:T(8,128)S(1)}, f32[258,1]{1,0:T(8,128)S(1)}, u32[]{:S(2)}, u32[]{:S(2)}) collective-permute-start(f32[258,1]{1,0:T(8,128)S(1)} %get-tuple-element.52), channel_id=1, source_target_pairs={{0,1},{1,2},{2,3},{4,5},{5,6},{6,7},{8,9},{9,10},{10,11},{12,13},{... | collective-permute-start | bytes 3104 | tf_op jit(solution)/shard_map/ppermute | solution.py:21
  19.9 4.9 %collective-permute-start.3 = (f32[258,1]{1,0:T(8,128)S(1)}, f32[258,1]{1,0:T(8,128)S(1)}, u32[]{:S(2)}, u32[]{:S(2)}) collective-permute-start(f32[258,1]{1,0:T(8,128)S(1)} %get-tuple-element.50), channel_id=1, source_target_pairs={{0,1},{1,2},{2,3},{4,5},{5,6},{6,7},{8,9},{9,10},{10,11},{12,13},{... | collective-permute-start | bytes 3104 | tf_op jit(solution)/shard_map/ppermute | solution.py:21
  24.8 2.5 collective-permute-done.2
  29.3 44.4 %all-reduce.5 = (f32[]{:T(128)}, f32[]{:T(128)}) all-reduce(f32[]{:T(128)} %get-tuple-element.12, f32[]{:T(128)} %get-tuple-element.11), channel_id=1, replica_groups=mesh['row'=8,'col'=4] {'row','col'}, use_global_device_ids=true, to_apply=%region_1.0 | all-reduce | flops 2 | bytes 16 | tf_op jit(solution)/shard_map/psum | solution.py:62
  77.8 3.4 collective-permute-done.8
  82.7 4.8 %collective-permute-start.11 = (f32[258,1]{1,0:T(8,128)S(1)}, f32[258,1]{1,0:T(8,128)S(1)}, u32[]{:S(2)}, u32[]{:S(2)}) collective-permute-start(f32[258,1]{1,0:T(8,128)S(1)} %get-tuple-element.48), channel_id=1, source_target_pairs={{0,1},{1,2},{2,3},{4,5},{5,6},{6,7},{8,9},{9,10},{10,11},{12,13},{... | collective-permute-start | bytes 3104 | tf_op jit(solution)/shard_map/ppermute | solution.py:21
  88.5 1.5 collective-permute-done.11
  90.0 1.4 multiply_reduce_fusion.7
  91.4 44.4 %all-reduce.4 = (f32[]{:T(128)}, f32[]{:T(128)}) all-reduce(f32[]{:T(128)} %get-tuple-element.10, f32[]{:T(128)} %get-tuple-element.9), channel_id=1, replica_groups=mesh['row'=8,'col'=4] {'row','col'}, use_global_device_ids=true, to_apply=%region_5.0 | all-reduce | flops 2 | bytes 16 | tf_op jit(solution)/shard_map/psum | solution.py:62
  143.7 1.9 collective-permute-done.12
  147.0 4.8 %collective-permute-start.15 = (f32[258,1]{1,0:T(8,128)S(1)}, f32[258,1]{1,0:T(8,128)S(1)}, u32[]{:S(2)}, u32[]{:S(2)}) collective-permute-start(f32[258,1]{1,0:T(8,128)S(1)} %get-tuple-element.46), channel_id=1, source_target_pairs={{0,1},{1,2},{2,3},{4,5},{5,6},{6,7},{8,9},{9,10},{10,11},{12,13},{... | collective-permute-start | bytes 3104 | tf_op jit(solution)/shard_map/ppermute | solution.py:21
  151.9 3.9 collective-permute-start.21
  158.6 41.7 %all-reduce.3 = (f32[]{:T(128)}, f32[]{:T(128)}) all-reduce(f32[]{:T(128)} %get-tuple-element.31, f32[]{:T(128)} %fusion.41), channel_id=1, replica_groups=mesh['row'=8,'col'=4] {'row','col'}, use_global_device_ids=true, to_apply=%region_9.0 | all-reduce | flops 2 | bytes 16 | tf_op jit(solution)/shard_map/psum | solution.py:62
  208.8 5.0 %collective-permute-start.23 = (f32[258,1]{1,0:T(8,128)S(1)}, f32[258,1]{1,0:T(8,128)S(1)}, u32[]{:S(2)}, u32[]{:S(2)}) collective-permute-start(f32[258,1]{1,0:T(8,128)S(1)} %get-tuple-element.44), channel_id=1, source_target_pairs={{0,1},{1,2},{2,3},{4,5},{5,6},{6,7},{8,9},{9,10},{10,11},{12,13},{... | collective-permute-start | bytes 3104 | tf_op jit(solution)/shard_map/ppermute | solution.py:21
  215.3 5.4 %collective-permute-start.19 = (f32[258,1]{1,0:T(8,128)S(1)}, f32[258,1]{1,0:T(8,128)S(1)}, u32[]{:S(2)}, u32[]{:S(2)}) collective-permute-start(f32[258,1]{1,0:T(8,128)S(1)} %get-tuple-element.42), channel_id=1, source_target_pairs={{0,1},{1,2},{2,3},{4,5},{5,6},{6,7},{8,9},{9,10},{10,11},{12,13},{... | collective-permute-start | bytes 3104 | tf_op jit(solution)/shard_map/ppermute | solution.py:21
  220.8 2.5 collective-permute-done.18
  223.6 3.4 fusion.71
  227.0 44.8 %all-reduce.2 = (f32[]{:T(128)}, f32[]{:T(128)}) all-reduce(f32[]{:T(128)} %get-tuple-element.5, f32[]{:T(128)} %get-tuple-element.4), channel_id=1, replica_groups=mesh['row'=8,'col'=4] {'row','col'}, use_global_device_ids=true, to_apply=%region_13.0 | all-reduce | flops 2 | bytes 16 | tf_op jit(solution)/shard_map/psum | solution.py:62
  275.9 2.3 collective-permute-done.24
  279.6 4.8 %collective-permute-start.27 = (f32[258,1]{1,0:T(8,128)S(1)}, f32[258,1]{1,0:T(8,128)S(1)}, u32[]{:S(2)}, u32[]{:S(2)}) collective-permute-start(f32[258,1]{1,0:T(8,128)S(1)} %get-tuple-element.40), channel_id=1, source_target_pairs={{0,1},{1,2},{2,3},{4,5},{5,6},{6,7},{8,9},{9,10},{10,11},{12,13},{... | collective-permute-start | bytes 3104 | tf_op jit(solution)/shard_map/ppermute | solution.py:21
  285.5 1.5 collective-permute-done.27
  287.0 3.9 multiply_reduce_fusion.2
  290.9 44.6 %all-reduce.1 = (f32[]{:T(128)}, f32[]{:T(128)}) all-reduce(f32[]{:T(128)} %get-tuple-element.8, f32[]{:T(128)} %get-tuple-element.7), channel_id=1, replica_groups=mesh['row'=8,'col'=4] {'row','col'}, use_global_device_ids=true, to_apply=%region_17.0 | all-reduce | flops 2 | bytes 16 | tf_op jit(solution)/shard_map/psum | solution.py:62
  339.9 1.8 multiply_reduce_fusion.1
  344.5 2.4 collective-permute-done.28
  348.3 4.8 %collective-permute-start.31 = (f32[258,1]{1,0:T(8,128)S(1)}, f32[258,1]{1,0:T(8,128)S(1)}, u32[]{:S(2)}, u32[]{:S(2)}) collective-permute-start(f32[258,1]{1,0:T(8,128)S(1)} %get-tuple-element.38), channel_id=1, source_target_pairs={{0,1},{1,2},{2,3},{4,5},{5,6},{6,7},{8,9},{9,10},{10,11},{12,13},{... | collective-permute-start | bytes 3104 | tf_op jit(solution)/shard_map/ppermute | solution.py:21
  354.2 1.5 collective-permute-done.31
  355.7 3.1 fusion.5
  358.8 44.5 %all-reduce = (f32[]{:T(128)}, f32[]{:T(128)}, f32[]{:T(128)}, f32[]{:T(128)}) all-reduce(f32[]{:T(128)} %get-tuple-element.27, f32[]{:T(128)} %fusion.5, f32[]{:T(128)} %get-tuple-element.6, f32[]{:T(128)} %get-tuple-element.3), channel_id=1, replica_groups=mesh['row'=8,'col'=4] {'row','col'}, use_global_device_ids=true, to_apply=%region_21.0 | all-reduce | flops 4 | bytes 32 | tf_op jit(solution)/shard_map/psum | solution.py:62
  (97 shorter events, 37.8 us)
Async XLA Ops:
  2.2 10.2 %collective-permute-start.5 = (f32[1,512]{1,0:T(1,128)S(1)}, f32[1,512]{1,0:T(1,128)S(1)}, u32[]{:S(2)}, u32[]{:S(2)}) collective-permute-start(f32[1,512]{1,0:T(1,128)S(1)} %get-tuple-element.67), channel_id=1, source_target_pairs={{0,4},{4,8},{8,12},{12,16},{16,20},{20,24},{24,28},{1,5},{5,9},{9,... | collective-permute-start | bytes 6152 | tf_op jit(solution)/shard_map/ppermute | solution.py:21
  4.6 7.8 %collective-permute-start.4 = (f32[1,512]{1,0:T(1,128)S(1)}, f32[1,512]{1,0:T(1,128)S(1)}, u32[]{:S(2)}, u32[]{:S(2)}) collective-permute-start(f32[1,512]{1,0:T(1,128)S(1)} %get-tuple-element.68), channel_id=1, source_target_pairs={{4,0},{8,4},{12,8},{16,12},{20,16},{24,20},{28,24},{5,1},{9,5},{13... | collective-permute-start | bytes 6152 | tf_op jit(solution)/shard_map/ppermute | solution.py:23
  5.9 12.5 %collective-permute-start.1 = (f32[1,512]{1,0:T(1,128)S(1)}, f32[1,512]{1,0:T(1,128)S(1)}, u32[]{:S(2)}, u32[]{:S(2)}) collective-permute-start(f32[1,512]{1,0:T(1,128)S(1)} %get-tuple-element.65), channel_id=1, source_target_pairs={{0,4},{4,8},{8,12},{12,16},{16,20},{20,24},{24,28},{1,5},{5,9},{9,... | collective-permute-start | bytes 6152 | tf_op jit(solution)/shard_map/ppermute | solution.py:21
  11.1 7.3 %collective-permute-start = (f32[1,512]{1,0:T(1,128)S(1)}, f32[1,512]{1,0:T(1,128)S(1)}, u32[]{:S(2)}, u32[]{:S(2)}) collective-permute-start(f32[1,512]{1,0:T(1,128)S(1)} %get-tuple-element.66), channel_id=1, source_target_pairs={{4,0},{8,4},{12,8},{16,12},{20,16},{24,20},{28,24},{5,1},{9,5},{13... | collective-permute-start | bytes 6152 | tf_op jit(solution)/shard_map/ppermute | solution.py:23
  12.5 12.2 %collective-permute-start.6 = (f32[258,1]{1,0:T(8,128)S(1)}, f32[258,1]{1,0:T(8,128)S(1)}, u32[]{:S(2)}, u32[]{:S(2)}) collective-permute-start(f32[258,1]{1,0:T(8,128)S(1)} %get-tuple-element.51), channel_id=1, source_target_pairs={{1,0},{2,1},{3,2},{5,4},{6,5},{7,6},{9,8},{10,9},{11,10},{13,12},{... | collective-permute-start | bytes 3104 | tf_op jit(solution)/shard_map/ppermute | solution.py:23
  13.8 11.0 %collective-permute-start.7 = (f32[258,1]{1,0:T(8,128)S(1)}, f32[258,1]{1,0:T(8,128)S(1)}, u32[]{:S(2)}, u32[]{:S(2)}) collective-permute-start(f32[258,1]{1,0:T(8,128)S(1)} %get-tuple-element.52), channel_id=1, source_target_pairs={{0,1},{1,2},{2,3},{4,5},{5,6},{6,7},{8,9},{9,10},{10,11},{12,13},{... | collective-permute-start | bytes 3104 | tf_op jit(solution)/shard_map/ppermute | solution.py:21
  18.6 8.7 %collective-permute-start.2 = (f32[258,1]{1,0:T(8,128)S(1)}, f32[258,1]{1,0:T(8,128)S(1)}, u32[]{:S(2)}, u32[]{:S(2)}) collective-permute-start(f32[258,1]{1,0:T(8,128)S(1)} %get-tuple-element.49), channel_id=1, source_target_pairs={{1,0},{2,1},{3,2},{5,4},{6,5},{7,6},{9,8},{10,9},{11,10},{13,12},{... | collective-permute-start | bytes 3104 | tf_op jit(solution)/shard_map/ppermute | solution.py:23
  19.9 8.0 %collective-permute-start.3 = (f32[258,1]{1,0:T(8,128)S(1)}, f32[258,1]{1,0:T(8,128)S(1)}, u32[]{:S(2)}, u32[]{:S(2)}) collective-permute-start(f32[258,1]{1,0:T(8,128)S(1)} %get-tuple-element.50), channel_id=1, source_target_pairs={{0,1},{1,2},{2,3},{4,5},{5,6},{6,7},{8,9},{9,10},{10,11},{12,13},{... | collective-permute-start | bytes 3104 | tf_op jit(solution)/shard_map/ppermute | solution.py:21
  75.2 2.6 collective-permute-start.9
  76.5 4.7 %collective-permute-start.8 = (f32[1,512]{1,0:T(1,128)S(1)}, f32[1,512]{1,0:T(1,128)S(1)}, u32[]{:S(2)}, u32[]{:S(2)}) collective-permute-start(f32[1,512]{1,0:T(1,128)S(1)} %get-tuple-element.64), channel_id=1, source_target_pairs={{4,0},{8,4},{12,8},{16,12},{20,16},{24,20},{28,24},{5,1},{9,5},{13... | collective-permute-start | bytes 6152 | tf_op jit(solution)/shard_map/ppermute | solution.py:23
  81.4 7.2 %collective-permute-start.10 = (f32[258,1]{1,0:T(8,128)S(1)}, f32[258,1]{1,0:T(8,128)S(1)}, u32[]{:S(2)}, u32[]{:S(2)}) collective-permute-start(f32[258,1]{1,0:T(8,128)S(1)} %get-tuple-element.47), channel_id=1, source_target_pairs={{1,0},{2,1},{3,2},{5,4},{6,5},{7,6},{9,8},{10,9},{11,10},{13,12},{... | collective-permute-start | bytes 3104 | tf_op jit(solution)/shard_map/ppermute | solution.py:23
  82.7 7.4 %collective-permute-start.11 = (f32[258,1]{1,0:T(8,128)S(1)}, f32[258,1]{1,0:T(8,128)S(1)}, u32[]{:S(2)}, u32[]{:S(2)}) collective-permute-start(f32[258,1]{1,0:T(8,128)S(1)} %get-tuple-element.48), channel_id=1, source_target_pairs={{0,1},{1,2},{2,3},{4,5},{5,6},{6,7},{8,9},{9,10},{10,11},{12,13},{... | collective-permute-start | bytes 3104 | tf_op jit(solution)/shard_map/ppermute | solution.py:21
  141.0 2.7 collective-permute-start.13
  142.4 3.2 collective-permute-start.12
  145.7 11.4 %collective-permute-start.14 = (f32[258,1]{1,0:T(8,128)S(1)}, f32[258,1]{1,0:T(8,128)S(1)}, u32[]{:S(2)}, u32[]{:S(2)}) collective-permute-start(f32[258,1]{1,0:T(8,128)S(1)} %get-tuple-element.45), channel_id=1, source_target_pairs={{1,0},{2,1},{3,2},{5,4},{6,5},{7,6},{9,8},{10,9},{11,10},{13,12},{... | collective-permute-start | bytes 3104 | tf_op jit(solution)/shard_map/ppermute | solution.py:23
  147.0 10.1 %collective-permute-start.15 = (f32[258,1]{1,0:T(8,128)S(1)}, f32[258,1]{1,0:T(8,128)S(1)}, u32[]{:S(2)}, u32[]{:S(2)}) collective-permute-start(f32[258,1]{1,0:T(8,128)S(1)} %get-tuple-element.46), channel_id=1, source_target_pairs={{0,1},{1,2},{2,3},{4,5},{5,6},{6,7},{8,9},{9,10},{10,11},{12,13},{... | collective-permute-start | bytes 3104 | tf_op jit(solution)/shard_map/ppermute | solution.py:21
  151.9 55.0 %collective-permute-start.21 = (f32[1,512]{1,0:T(1,128)S(1)}, f32[1,512]{1,0:T(1,128)S(1)}, u32[]{:S(2)}, u32[]{:S(2)}) collective-permute-start(f32[1,512]{1,0:T(1,128)S(1)} %get-tuple-element.59), channel_id=1, source_target_pairs={{0,4},{4,8},{8,12},{12,16},{16,20},{20,24},{24,28},{1,5},{5,9},{9,... | collective-permute-start | bytes 6152 | tf_op jit(solution)/shard_map/ppermute | solution.py:21
  155.8 51.1 %collective-permute-start.20 = (f32[1,512]{1,0:T(1,128)S(1)}, f32[1,512]{1,0:T(1,128)S(1)}, u32[]{:S(2)}, u32[]{:S(2)}) collective-permute-start(f32[1,512]{1,0:T(1,128)S(1)} %get-tuple-element.60), channel_id=1, source_target_pairs={{4,0},{8,4},{12,8},{16,12},{20,16},{24,20},{28,24},{5,1},{9,5},{13... | collective-permute-start | bytes 6152 | tf_op jit(solution)/shard_map/ppermute | solution.py:23
  204.3 9.6 %collective-permute-start.17 = (f32[1,512]{1,0:T(1,128)S(1)}, f32[1,512]{1,0:T(1,128)S(1)}, u32[]{:S(2)}, u32[]{:S(2)}) collective-permute-start(f32[1,512]{1,0:T(1,128)S(1)} %get-tuple-element.57), channel_id=1, source_target_pairs={{0,4},{4,8},{8,12},{12,16},{16,20},{20,24},{24,28},{1,5},{5,9},{9,... | collective-permute-start | bytes 6152 | tf_op jit(solution)/shard_map/ppermute | solution.py:21
  205.6 8.3 %collective-permute-start.16 = (f32[1,512]{1,0:T(1,128)S(1)}, f32[1,512]{1,0:T(1,128)S(1)}, u32[]{:S(2)}, u32[]{:S(2)}) collective-permute-start(f32[1,512]{1,0:T(1,128)S(1)} %get-tuple-element.58), channel_id=1, source_target_pairs={{4,0},{8,4},{12,8},{16,12},{20,16},{24,20},{28,24},{5,1},{9,5},{13... | collective-permute-start | bytes 6152 | tf_op jit(solution)/shard_map/ppermute | solution.py:23
  207.5 13.3 %collective-permute-start.22 = (f32[258,1]{1,0:T(8,128)S(1)}, f32[258,1]{1,0:T(8,128)S(1)}, u32[]{:S(2)}, u32[]{:S(2)}) collective-permute-start(f32[258,1]{1,0:T(8,128)S(1)} %get-tuple-element.43), channel_id=1, source_target_pairs={{1,0},{2,1},{3,2},{5,4},{6,5},{7,6},{9,8},{10,9},{11,10},{13,12},{... | collective-permute-start | bytes 3104 | tf_op jit(solution)/shard_map/ppermute | solution.py:23
  208.8 12.0 %collective-permute-start.23 = (f32[258,1]{1,0:T(8,128)S(1)}, f32[258,1]{1,0:T(8,128)S(1)}, u32[]{:S(2)}, u32[]{:S(2)}) collective-permute-start(f32[258,1]{1,0:T(8,128)S(1)} %get-tuple-element.44), channel_id=1, source_target_pairs={{0,1},{1,2},{2,3},{4,5},{5,6},{6,7},{8,9},{9,10},{10,11},{12,13},{... | collective-permute-start | bytes 3104 | tf_op jit(solution)/shard_map/ppermute | solution.py:21
  214.0 9.2 %collective-permute-start.18 = (f32[258,1]{1,0:T(8,128)S(1)}, f32[258,1]{1,0:T(8,128)S(1)}, u32[]{:S(2)}, u32[]{:S(2)}) collective-permute-start(f32[258,1]{1,0:T(8,128)S(1)} %get-tuple-element.41), channel_id=1, source_target_pairs={{1,0},{2,1},{3,2},{5,4},{6,5},{7,6},{9,8},{10,9},{11,10},{13,12},{... | collective-permute-start | bytes 3104 | tf_op jit(solution)/shard_map/ppermute | solution.py:23
  215.3 8.2 %collective-permute-start.19 = (f32[258,1]{1,0:T(8,128)S(1)}, f32[258,1]{1,0:T(8,128)S(1)}, u32[]{:S(2)}, u32[]{:S(2)}) collective-permute-start(f32[258,1]{1,0:T(8,128)S(1)} %get-tuple-element.42), channel_id=1, source_target_pairs={{0,1},{1,2},{2,3},{4,5},{5,6},{6,7},{8,9},{9,10},{10,11},{12,13},{... | collective-permute-start | bytes 3104 | tf_op jit(solution)/shard_map/ppermute | solution.py:21
  273.2 2.6 collective-permute-start.25
  274.5 3.7 collective-permute-start.24
  278.3 7.2 %collective-permute-start.26 = (f32[258,1]{1,0:T(8,128)S(1)}, f32[258,1]{1,0:T(8,128)S(1)}, u32[]{:S(2)}, u32[]{:S(2)}) collective-permute-start(f32[258,1]{1,0:T(8,128)S(1)} %get-tuple-element.39), channel_id=1, source_target_pairs={{1,0},{2,1},{3,2},{5,4},{6,5},{7,6},{9,8},{10,9},{11,10},{13,12},{... | collective-permute-start | bytes 3104 | tf_op jit(solution)/shard_map/ppermute | solution.py:23
  279.6 7.4 %collective-permute-start.27 = (f32[258,1]{1,0:T(8,128)S(1)}, f32[258,1]{1,0:T(8,128)S(1)}, u32[]{:S(2)}, u32[]{:S(2)}) collective-permute-start(f32[258,1]{1,0:T(8,128)S(1)} %get-tuple-element.40), channel_id=1, source_target_pairs={{0,1},{1,2},{2,3},{4,5},{5,6},{6,7},{8,9},{9,10},{10,11},{12,13},{... | collective-permute-start | bytes 3104 | tf_op jit(solution)/shard_map/ppermute | solution.py:21
  341.8 2.7 collective-permute-start.29
  343.1 3.8 collective-permute-start.28
  347.0 7.2 %collective-permute-start.30 = (f32[258,1]{1,0:T(8,128)S(1)}, f32[258,1]{1,0:T(8,128)S(1)}, u32[]{:S(2)}, u32[]{:S(2)}) collective-permute-start(f32[258,1]{1,0:T(8,128)S(1)} %get-tuple-element.37), channel_id=1, source_target_pairs={{1,0},{2,1},{3,2},{5,4},{6,5},{7,6},{9,8},{10,9},{11,10},{13,12},{... | collective-permute-start | bytes 3104 | tf_op jit(solution)/shard_map/ppermute | solution.py:23
  348.3 7.4 %collective-permute-start.31 = (f32[258,1]{1,0:T(8,128)S(1)}, f32[258,1]{1,0:T(8,128)S(1)}, u32[]{:S(2)}, u32[]{:S(2)}) collective-permute-start(f32[258,1]{1,0:T(8,128)S(1)} %get-tuple-element.38), channel_id=1, source_target_pairs={{0,1},{1,2},{2,3},{4,5},{5,6},{6,7},{8,9},{9,10},{10,11},{12,13},{... | collective-permute-start | bytes 3104 | tf_op jit(solution)/shard_map/ppermute | solution.py:21
  (15 other events, 579.7 us)
where the time goes:
time: 413 us; the launch traced here: 411 us
  blocking collectives  264 us (64%)
  starting transfers between devices  78.2 us (19%)
  waiting for transfers between devices  23.6 us (6%)
  between operations  22.8 us (6%)
  other arithmetic  21 us (5%)
    psum x6, blocking collectives, products(): lax.psum((jnp.sum(residual * residual), jnp.sum(residual * applied)), ('r...  264 us
    ppermute x16, starting transfers between devices, padded_2(): lax.ppermute(tail, axis, [(i, (i + 1) % count) for i in range(ends)])  57.4 us
    ppermute x16, starting transfers between devices, padded_2(): lax.ppermute(head, axis, [((i + 1) % count, i) for i in range(ends)])  20.8 us
    ppermute x16, waiting for transfers between devices, padded_2(): lax.ppermute(head, axis, [((i + 1) % count, i) for i in range(ends)])  18.1 us
    reduce_sum x5, other arithmetic, products(): jnp.sum(residual * applied)  11.2 us
  transfers between devices with their start and end apart: 32, of which 14 were waited for; matrix products, arithmetic and copies ran while one was open for 0% of the time, Pallas kernels for 0%

commit v1 on v0

v1 whole, which is shorter than its diff:
```python
import functools

import jax
import jax.numpy as jnp
from jax import lax
from jax.experimental import pallas as pl
from jax.experimental.pallas import tpu as pltpu
from jax.sharding import PartitionSpec as P

discount_rate = 0.05
diffusion = 0.25
SCALE = 0.0625
FACE = diffusion * 0.5 * SCALE
LANES = 128
SUB = 8
WIDE = 7
PAD = 2 * SUB
VMEM_BYTES = 16 * 2**20
VM = pl.BlockSpec(memory_space=pltpu.VMEM)
BOTH = ("row", "col")


def two_sum(a, b):
    s = a + b
    t = s - a
    return s, (a - (s - t)) + (b - t)


def fast_sum(a, b):
    s = a + b
    return s, b - (s - a)


def halves(a):
    t = a * 4097.0
    hi = t - (t - a)
    return hi, a - hi


def two_prod(a, b):
    p = a * b
    ah, al = halves(a)
    bh, bl = halves(b)
    return p, ((ah * bh - p) + ah * bl + al * bh) + al * bl


def dmul(a, b):
    p, e = two_prod(a[0], b[0])
    return fast_sum(p, e + (a[0] * b[1] + a[1] * b[0]))


def dsub(a, b):
    s, e = two_sum(a[0], -b[0])
    return fast_sum(s, e + (a[1] - b[1]))


def ddiv(a, b):
    q = a[0] / b[0]
    r = dsub(a, dmul((q, jnp.zeros_like(q)), b))
    return fast_sum(q, r[0] / b[0])


def galerkin(dots):
    d00, d01, d02, d03, d11, d12, d13, d22, d23 = dots
    zero = jnp.zeros_like(d00[0])
    l1 = ddiv(d11, d01)
    l2 = ddiv(d12, d01)
    s11 = dsub(d12, dmul(l1, d02))
    s12 = dsub(d13, dmul(l1, d03))
    s21 = dsub(d22, dmul(l2, d02))
    s22 = dsub(d23, dmul(l2, d03))
    g0 = (d00[0] * SCALE, d00[1] * SCALE)
    g1 = dsub((d01[0] * SCALE, d01[1] * SCALE), dmul(l1, g0))
    g2 = dsub((d02[0] * SCALE, d02[1] * SCALE), dmul(l2, g0))
    l3 = ddiv(s21, s11)
    t22 = dsub(s22, dmul(l3, s12))
    g2 = dsub(g2, dmul(l3, g1))
    full1 = s11[0] > 1e-12 * d12[0]
    full2 = full1 & (t22[0] > 1e-12 * d23[0])
    c2 = jnp.where(full2, ddiv(g2, t22)[0], zero)
    c1 = ddiv(dsub(g1, dmul(s12, (c2, zero))), s11)[0]
    c1 = jnp.where(full1, c1, zero)
    r0 = dsub(dsub(g0, dmul(d02, (c1, zero))), dmul(d03, (c2, zero)))
    return ddiv(r0, d01)[0], c1, c2


PAIRS = ((0, 0), (0, 1), (0, 2), (0, 3), (1, 1), (1, 2), (1, 3), (2, 2), (2, 3))


def split_short(a):
    t = a * 65537.0
    hi = t - (t - a)
    return hi, a - hi


def dot_step(groups, sums):
    parts = [[split_short(v) for v in vs] for vs in groups]
    out = []
    for k, (i, j) in enumerate(PAIRS):
        main = None
        rest = None
        for vs, ps in zip(groups, parts):
            m = ps[i][0] * ps[j][0]
            if i == j:
                r = ps[i][1] * (vs[i] + ps[i][0])
            else:
                r = ps[i][0] * ps[j][1] + ps[i][1] * vs[j]
            main = m if main is None else main + m
            rest = r if rest is None else rest + r
        s, e = two_sum(sums[2 * k], main)
        out += [s, sums[2 * k + 1] + (e + rest)]
    return tuple(out)


def pack_sums(sums, extra=()):
    lane = lax.broadcasted_iota(jnp.int32, (1, LANES), 1)
    row = jnp.zeros((1, LANES), jnp.float32)
    total = lambda a: jnp.sum(jnp.sum(a, axis=0, keepdims=True), axis=1, keepdims=True)
    for k in range(len(PAIRS)):
        s, e = sums[2 * k], sums[2 * k + 1]
        peak = jnp.max(jnp.max(jnp.abs(s), axis=0, keepdims=True), axis=1, keepdims=True)
        lift = jnp.broadcast_to(peak * 2048.0, s.shape)
        main = (s + lift) - lift
        row = jnp.where(lane == k, total(main), row)
        row = jnp.where(lane == 64 + k, total((s - main) + e), row)
    for k, a in enumerate(extra):
        row = jnp.where(lane == len(PAIRS) + k, total(a), row)
    return row


def gathered_sums(ref, extra=0):
    rows = [(ref[d], None) for d in range(ref.shape[0])]
    while len(rows) > 1:
        merged = []
        for k in range(0, len(rows) - 1, 2):
            (a, ea), (b, eb) = rows[k], rows[k + 1]
            s, e = two_sum(a, b)
            e = e if ea is None else e + (ea + eb)
            merged.append((s, e))
        if len(rows) % 2:
            a, ea = rows[-1]
            merged.append((a, jnp.zeros_like(a) if ea is None else ea))
        rows = merged
    s, e = rows[0]
    lane = lax.broadcasted_iota(jnp.int32, s.shape, 1)
    pick = lambda a, k: jnp.sum(jnp.where(lane == k, a, 0.0), axis=1, keepdims=True)
    dots = []
    for k in range(len(PAIRS)):
        hi = pick(s, k)
        lo = pick(e, k) + pick(s, 64 + k)
        dots.append(fast_sum(hi, lo))
    return dots, [pick(s, len(PAIRS) + k) for k in range(extra)]


def fields_of(rc, cx, cy):
    control_cost = 0.5 * (cx * cx + cy * cy)
    return rc + control_cost, 1.0 + control_cost


def edge_rows_kernel(*refs):
    first, last, (up_ref, down_ref) = refs[:4], refs[4:8], refs[8:]
    for (rc, cx, cy, pd), out in ((first, up_ref), (last, down_ref)):
        forcing, conduct = fields_of(rc[...], cx[...], cy[...])
        out[0:SUB] = forcing
        out[SUB : 2 * SUB] = conduct
        out[2 * SUB :] = pd[...]


def fields_kernel(rc_ref, cx_ref, cy_ref, pd_ref, f_ref, c_ref, p_ref):
    i = pl.program_id(0)
    rows = rc_ref.shape[0]
    base = pl.multiple_of(i * rows, SUB)
    for j in range(f_ref.shape[0]):
        cols = slice(j * LANES, (j + 1) * LANES)
        forcing, conduct = fields_of(rc_ref[:, cols], cx_ref[:, cols], cy_ref[:, cols])
        f_ref[j, pl.ds(base, rows), :] = forcing
        c_ref[j, pl.ds(base, rows), :] = conduct
        p_ref[j, pl.ds(base, rows), :] = pd_ref[:, cols]


def row_tile(own_ref, north_ref, south_ref, field, j, t):
    tiles = own_ref.shape[1] // SUB + 2
    cols = slice(j * LANES, (j + 1) * LANES)
    if t == 0:
        return north_ref[field * SUB : (field + 1) * SUB, cols]
    if t == tiles - 1:
        return south_ref[field * SUB : (field + 1) * SUB, cols]
    return own_ref[j, (t - 1) * SUB : t * SUB, :]


def packing(tiles):
    per = LANES // WIDE
    return per, -(-tiles // per)


def pack_columns_kernel(f_ref, c_ref, p_ref, north_ref, south_ref, west_ref, east_ref):
    tiles = f_ref.shape[1] // SUB + 2
    per, groups = packing(tiles)
    lane = lax.broadcasted_iota(jnp.int32, (SUB, LANES), 1)
    last = f_ref.shape[0] - 1
    for field, own in enumerate((f_ref, c_ref, p_ref)):
        for v in range(groups):
            west = jnp.zeros((SUB, LANES), jnp.float32)
            east = west
            for g in range(min(per, tiles - v * per)):
                here = (lane >= WIDE * g) & (lane < WIDE * (g + 1))
                a = row_tile(own, north_ref, south_ref, field, 0, v * per + g)
                b = row_tile(own, north_ref, south_ref, field, last, v * per + g)
                west = jnp.where(here, pltpu.roll(a, (WIDE * g) % LANES, 1), west)
                east = jnp.where(here, pltpu.roll(b, (WIDE * (g + 1)) % LANES, 1), east)
            at = (field * groups + v) * SUB
            west_ref[at : at + SUB] = west
            east_ref[at : at + SUB] = east


def fill(refs, owns, north_ref, south_ref, west_ref, east_ref):
    last = refs[0].shape[0] - 1
    rows = refs[0].shape[1]
    tiles = (rows - 2 * PAD) // SUB + 2
    per, groups = packing(tiles)
    lane = lax.broadcasted_iota(jnp.int32, (SUB, LANES), 1)
    zero = jnp.zeros((SUB, LANES), jnp.float32)
    for field, ref in enumerate(refs):
        mine = slice(field * SUB, (field + 1) * SUB)
        for j in range(last + 1):
            ref[j, 0:SUB] = zero
            ref[j, rows - SUB : rows] = zero
        for j in range(last):
            cols = slice(j * LANES, (j + 1) * LANES)
            ref[j, SUB : 2 * SUB] = north_ref[mine, cols]
            ref[j, rows - 2 * SUB : rows - SUB] = south_ref[mine, cols]
            ref[j, PAD : rows - PAD] = owns[field][j]
        for t in range(tiles):
            v, g = divmod(t, per)
            at = (field * groups + v) * SUB
            west = pltpu.roll(west_ref[at : at + SUB], (-WIDE * (g + 1)) % LANES, 1)
            east = pltpu.roll(east_ref[at : at + SUB], (-WIDE * g) % LANES, 1)
            tile = jnp.where(lane < WIDE, east, jnp.where(lane >= LANES - WIDE, west, 0.0))
            ref[last, SUB + t * SUB : 2 * SUB + t * SUB] = tile


def beside(ref, r, count):
    lane = lax.broadcasted_iota(jnp.int32, (SUB, LANES), 1)
    here = [ref[j, pl.ds(r, SUB), :] for j in range(count)]
    south = [ref[j, pl.ds(r + 1, SUB), :] for j in range(count)]
    north = [ref[j, pl.ds(r - 1, SUB), :] for j in range(count)]
    left = [pltpu.roll(a, LANES - 1, 1) for a in here]
    right = [pltpu.roll(a, 1, 1) for a in here]
    east = [jnp.where(lane == LANES - 1, left[(j + 1) % count], left[j]) for j in range(count)]
    west = [jnp.where(lane == 0, right[(j - 1) % count], right[j]) for j in range(count)]
    return here, south, north, east, west


def weighted_apply(center, w, cells):
    here, south, north, east, west = cells
    return center * here - ((w[0] * south + w[1] * north) + (w[2] * east + w[3] * west))


def apply_tiles(ref, w_ref, center_ref, r, count):
    cells = beside(ref, r, count)
    at = pl.ds(r, SUB)
    out = []
    for j in range(count):
        w = [w_ref[k, j, at, :] for k in range(4)]
        out.append(weighted_apply(center_ref[j, at, :], w, [c[j] for c in cells]))
    return out, cells[0]


def clear_pads(refs):
    zero = jnp.zeros((SUB, LANES), jnp.float32)
    for ref in refs:
        rows = ref.shape[1]
        for j in range(ref.shape[0]):
            ref[j, 0:SUB] = zero
            ref[j, rows - SUB : rows] = zero


def row_tiles(ref):
    return (ref.shape[1] - 2 * SUB) // SUB


def krylov(v0_ref, v1_ref, v2_ref, w_ref, center_ref):
    count, tiles = v0_ref.shape[0], row_tiles(v0_ref)
    own = count - 1

    def second(t, _):
        r = pl.multiple_of(SUB + t * SUB, SUB)
        out, _h = apply_tiles(v1_ref, w_ref, center_ref, r, count)
        for j in range(count):
            v2_ref[j, pl.ds(r, SUB), :] = out[j]
        return 0

    lax.fori_loop(0, tiles, second, 0)

    def third(t, sums):
        groups = []
        for u in range(2):
            r = pl.multiple_of(PAD + (2 * t + u) * SUB, SUB)
            out, here = apply_tiles(v2_ref, w_ref, center_ref, r, count)
            at = pl.ds(r, SUB)
            for j in range(own):
                groups.append((v0_ref[j, at, :], v1_ref[j, at, :], here[j], out[j]))
        return dot_step(groups, sums)

    zero = jnp.zeros((SUB, LANES), jnp.float32)
    return lax.fori_loop(0, (tiles - 2) // 2, third, (zero,) * (2 * len(PAIRS)))


def value_kernel(f_in, c_in, p_in, north_ref, south_ref, west_ref, east_ref,
                 f_ref, c_ref, p_ref, v1_ref, v2_ref, w_ref, faces_ref, row_ref, center_ref):
    fill((f_ref, c_ref, p_ref), (f_in, c_in, p_in), north_ref, south_ref, west_ref, east_ref)
    clear_pads((v1_ref, v2_ref))
    count, tiles = f_ref.shape[0], row_tiles(f_ref)

    def first(t, _):
        r = pl.multiple_of(SUB + t * SUB, SUB)
        at = pl.ds(r, SUB)
        cond = beside(c_ref, r, count)
        cells = beside(f_ref, r, count)
        for j in range(count):
            c = cond[0][j]
            inside = jnp.minimum(c, 1.0)
            face = inside * FACE
            w = [face * (c + cond[k][j]) for k in (1, 2, 3, 4)]
            faces = (w[0] + w[1]) + (w[2] + w[3])
            center = inside * (discount_rate * SCALE) + faces
            for k in range(4):
                w_ref[k, j, at, :] = w[k]
            faces_ref[j, at, :] = faces
            center_ref[j, at, :] = center
            v1_ref[j, at, :] = weighted_apply(center, w, [x[j] for x in cells])
        return 0

    lax.fori_loop(0, tiles, first, 0)
    sums = krylov(f_ref, v1_ref, v2_ref, w_ref, center_ref)
    row_ref[...] = jnp.broadcast_to(pack_sums(sums)[None], row_ref.shape)


def density_kernel(rows_ref, f_ref, c_ref, p_ref, v1_ref, v2_ref, w_ref, faces_ref,
                   value_ref, u1_ref, u2_ref, row_ref, vx_ref, center_ref):
    dots, _unused = gathered_sums(rows_ref)
    c0, c1, c2 = [jnp.broadcast_to(c, (SUB, LANES)) for c in galerkin(dots)]
    count, tiles = f_ref.shape[0], row_tiles(f_ref)
    own = count - 1
    clear_pads((vx_ref, u1_ref, u2_ref))

    def value(t, _):
        at = pl.ds(pl.multiple_of(SUB + t * SUB, SUB), SUB)
        for j in range(count):
            vx_ref[j, at, :] = (c0 * f_ref[j, at, :] + c1 * v1_ref[j, at, :]) + c2 * v2_ref[j, at, :]
        return 0

    lax.fori_loop(0, tiles, value, 0)

    def first(t, _):
        r = pl.multiple_of(SUB + t * SUB, SUB)
        at = pl.ds(r, SUB)
        val = beside(vx_ref, r, count)
        cells = beside(p_ref, r, count)
        for j in range(count):
            inside = jnp.minimum(c_ref[j, at, :], 1.0)
            slope_row = 0.5 * (val[1][j] - val[2][j])
            slope_col = 0.5 * (val[3][j] - val[4][j])
            congestion = (slope_row * slope_row + slope_col * slope_col) * (0.5 / diffusion)
            zeroth = (discount_rate + congestion) * SCALE
            center = inside * zeroth + faces_ref[j, at, :]
            center_ref[j, at, :] = center
            w = [w_ref[k, j, at, :] for k in range(4)]
            u1_ref[j, at, :] = weighted_apply(center, w, [x[j] for x in cells])
        return 0

    lax.fori_loop(0, tiles, first, 0)

    def outer(t, sums):
        r = pl.multiple_of(PAD + t * SUB, SUB)
        at = pl.ds(r, SUB)
        to = pl.ds(pl.multiple_of(t * SUB, SUB), SUB)
        cost, weight = sums
        for j in range(own):
            v = vx_ref[j, at, :]
            p = p_ref[j, at, :]
            value_ref[to, j * LANES : (j + 1) * LANES] = v
            cost = cost + p * (f_ref[j, at, :] - discount_rate * v)
            weight = weight + p
        return cost, weight

    zero = jnp.zeros((SUB, LANES), jnp.float32)
    extra = lax.fori_loop(0, tiles - 2, outer, (zero, zero))
    sums = krylov(p_ref, u1_ref, u2_ref, w_ref, center_ref)
    row_ref[...] = jnp.broadcast_to(pack_sums(sums, extra)[None], row_ref.shape)


def finish_kernel(rows_ref, p_ref, u1_ref, u2_ref, density_ref, ergodic_ref):
    dots, (cost, weight) = gathered_sums(rows_ref, 2)
    ergodic_ref[...] = cost / weight
    c0, c1, c2 = [jnp.broadcast_to(c, (SUB, LANES)) for c in galerkin(dots)]
    own = p_ref.shape[0] - 1

    def tile(t, _):
        at = pl.ds(pl.multiple_of(PAD + t * SUB, SUB), SUB)
        to = pl.ds(pl.multiple_of(t * SUB, SUB), SUB)
        for j in range(own):
            density_ref[to, j * LANES : (j + 1) * LANES] = (
                c0 * p_ref[j, at, :] + c1 * u1_ref[j, at, :]
            ) + c2 * u2_ref[j, at, :]
        return 0

    lax.fori_loop(0, density_ref.shape[0] // SUB, tile, 0)


def f32(*shape):
    return jax.ShapeDtypeStruct(shape, jnp.float32)


def exchange(back, ahead, axis):
    count = lax.axis_size(axis)
    ends = count - 1
    after = lax.ppermute(back, axis, [(i + 1, i) for i in range(ends)])
    before = lax.ppermute(ahead, axis, [(i, i + 1) for i in range(ends)])
    return before, after


def everyone(row):
    return lax.all_to_all(row, BOTH, 0, 0, tiled=True)


def body(*args):
    rows, cols = args[0].shape
    devices = lax.axis_size("row") * lax.axis_size("col")
    count = cols // LANES + 1
    ext = (count, rows + 2 * PAD, LANES)
    tiles = rows // SUB + 2
    _per, groups = packing(tiles)
    top = pl.BlockSpec((SUB, cols), lambda i: (0, 0))
    end = pl.BlockSpec((SUB, cols), lambda i: (rows // SUB - 1, 0))
    small = pltpu.CompilerParams(vmem_limit_bytes=VMEM_BYTES)
    up, down = pl.pallas_call(
        edge_rows_kernel,
        grid=(1,),
        in_specs=[top] * 4 + [end] * 4,
        out_specs=[pl.BlockSpec((3 * SUB, cols), lambda i: (0, 0))] * 2,
        out_shape=[f32(3 * SUB, cols)] * 2,
        compiler_params=small,
    )(*args, *args)
    north, south = exchange(up, down, "row")
    step = min(rows, 64)
    fields = pl.pallas_call(
        fields_kernel,
        grid=(rows // step,),
        in_specs=[pl.BlockSpec((step, cols), lambda i: (i, 0))] * 4,
        out_specs=[VM] * 3,
        out_shape=[f32(count - 1, rows, LANES)] * 3,
        cost_estimate=pl.CostEstimate(flops=10**6, bytes_accessed=4 * 10**6, transcendentals=0),
        compiler_params=small,
    )(*args)
    west, east = pl.pallas_call(
        pack_columns_kernel,
        in_specs=[VM] * 5,
        out_specs=[VM] * 2,
        out_shape=[f32(3 * groups * SUB, LANES)] * 2,
        compiler_params=small,
    )(*fields, north, south)
    west, east = exchange(west, east, "col")
    f, c, p, v1, v2, w, faces, row = pl.pallas_call(
        value_kernel,
        in_specs=[VM] * 7,
        out_specs=[VM] * 8,
        out_shape=[f32(*ext)] * 5 + [f32(4, *ext), f32(*ext), f32(devices, 1, LANES)],
        scratch_shapes=[pltpu.VMEM(ext, jnp.float32)],
        compiler_params=small,
    )(*fields, north, south, west, east)
    value, u1, u2, row = pl.pallas_call(
        density_kernel,
        in_specs=[VM] * 8,
        out_specs=[VM] * 4,
        out_shape=[f32(rows, cols), f32(*ext), f32(*ext), f32(devices, 1, LANES)],
        scratch_shapes=[pltpu.VMEM(ext, jnp.float32)] * 2,
        compiler_params=small,
    )(everyone(row), f, c, p, v1, v2, w, faces)
    density, ergodic = pl.pallas_call(
        finish_kernel,
        in_specs=[VM] * 4,
        out_specs=[VM] * 2,
        out_shape=[f32(rows, cols), f32(1, 1)],
        compiler_params=small,
    )(everyone(row), p, u1, u2)
    return value, density, ergodic[0, 0]


def solution(mesh):
    spec = P("row", "col")
    return jax.shard_map(body, mesh=mesh, in_specs=(spec,) * 4, out_specs=(spec, spec, P()), check_vma=False)
```

time: 413 us -> 65.4 us (0.16)
  blocking collectives: 264 us -> 22.8 us
  starting transfers between devices: 78.2 us -> 8.38 us
  between operations: 22.8 us -> 0.71 us
  other arithmetic: 21 us -> 0 us
  Pallas kernels: 0 us -> 20.8 us
  waiting for transfers between devices: 23.6 us -> 8.18 us
    psum x6 -> x0, blocking collectives: 264 us -> none  [products(): lax.psum((jnp.sum(residual * residual), jnp.sum(residual * applied)), ('r...]
    ppermute x32 -> x4, starting transfers between devices: 78.2 us -> 8.38 us  [the longest x2 5.8 us: exchange(): before = lax.ppermute(ahead, axis, [(i, i + 1) for i in range(ends)])]
    all_to_all x0 -> x2, blocking collectives: none -> 22.8 us  [everyone(): return lax.all_to_all(row, BOTH, 0, 0, tiled=True)]
    pallas_call x0 -> x6, Pallas kernels: none -> 20.8 us  [the longest x1 10 us: body(): pl.pallas_call(density_kernel, in_specs=[VM] * 8, out_specs=[VM] * 4, out...]
    reduce_sum x8 -> x0, other arithmetic: 17.3 us -> none  [the longest x5 11.2 us: products(): jnp.sum(residual * applied)]
    ppermute x32 -> x4, waiting for transfers between devices: 23.6 us -> 8.18 us  [the longest x2 7.98 us: exchange(): after = lax.ppermute(back, axis, [(i + 1, i) for i in range(ends)])]
  transfers between devices with their start and end apart: 32 -> 4, of which waited for: 14 -> 3; matrix products, arithmetic and copies ran while one was open for 0% -> 0% of each run, Pallas kernels for 0% -> 0%
where the time goes in v1:
time: 65.4 us; the launch traced here: 65 us
  blocking collectives  22.8 us (35%)
  Pallas kernels  20.8 us (32%)
  starting transfers between devices  8.38 us (13%)
  waiting for transfers between devices  8.18 us (13%)
  local copies, waits for them, and re-layouts  4.16 us (6%)
  between operations  0.71 us (1%)
    all_to_all x2, blocking collectives, everyone(): return lax.all_to_all(row, BOTH, 0, 0, tiled=True)  22.8 us
    pallas_call x1, Pallas kernels, body(): pl.pallas_call(density_kernel, in_specs=[VM] * 8, out_specs=[VM] * 4, out...  10 us
    pallas_call x1, Pallas kernels, body(): pl.pallas_call(value_kernel, in_specs=[VM] * 7, out_specs=[VM] * 8, out_s...  8.87 us
    ppermute x2, waiting for transfers between devices, exchange(): after = lax.ppermute(back, axis, [(i + 1, i) for i in range(ends)])  7.98 us
    ppermute x2, starting transfers between devices, exchange(): before = lax.ppermute(ahead, axis, [(i, i + 1) for i in range(ends)])  5.8 us
    unnamed x8, local copies, waits for them, and re-layouts  4.16 us
    ppermute x2, starting transfers between devices, exchange(): after = lax.ppermute(back, axis, [(i + 1, i) for i in range(ends)])  2.58 us
    pallas_call x1, Pallas kernels, body(): pl.pallas_call(finish_kernel, in_specs=[VM] * 4, out_specs=[VM] * 2, out_...  1.47 us
  transfers between devices with their start and end apart: 4, of which 3 were waited for; matrix products, arithmetic and copies ran while one was open for 0% of the time, Pallas kernels for 0%

profile of v1, /device:TPU:0, one launch (start us, length us, event | category | flops | bytes accessed | tf_op | source)
XLA Modules:
  0.0 65.0 jit_solution(15474700460917387158)
XLA Ops:
  0.6 0.0 copy-start
  0.6 1.0 %copy-done = f32[256,512]{1,0:T(8,128)S(1)} copy-done((f32[256,512]{1,0:T(8,128)S(1)}, f32[256,512]{1,0:T(8,128)}, u32[]{:S(2)}) %copy-start) | copy-done | bytes 524312
  1.7 0.0 copy-start.1
  1.7 1.0 %copy-done.1 = f32[256,512]{1,0:T(8,128)S(1)} copy-done((f32[256,512]{1,0:T(8,128)S(1)}, f32[256,512]{1,0:T(8,128)}, u32[]{:S(2)}) %copy-start.1) | copy-done | bytes 524312
  2.7 0.0 copy-start.2
  2.7 1.0 %copy-done.2 = f32[256,512]{1,0:T(8,128)S(1)} copy-done((f32[256,512]{1,0:T(8,128)S(1)}, f32[256,512]{1,0:T(8,128)}, u32[]{:S(2)}) %copy-start.2) | copy-done | bytes 524312
  3.8 0.0 copy-start.3
  3.8 1.0 %copy-done.3 = f32[256,512]{1,0:T(8,128)S(1)} copy-done((f32[256,512]{1,0:T(8,128)S(1)}, f32[256,512]{1,0:T(8,128)}, u32[]{:S(2)}) %copy-start.3) | copy-done | bytes 524312
  4.8 2.4 %collective-permute-start = (f32[24,512]{1,0:T(8,128)S(1)}, f32[24,512]{1,0:T(8,128)S(1)}, u32[]{:S(2)}, u32[]{:S(2)}) collective-permute-start(f32[24,512]{1,0:T(8,128)S(1)} %get-tuple-element.27), channel_id=1, source_target_pairs={{0,4},{4,8},{8,12},{12,16},{16,20},{20,24},{24,28},{1,5},{5,9},{9,... | collective-permute-start | bytes 147464 | tf_op jit(solution)/shard_map/ppermute | solution.py:419
  7.2 1.3 %collective-permute-start.1 = (f32[24,512]{1,0:T(8,128)S(1)}, f32[24,512]{1,0:T(8,128)S(1)}, u32[]{:S(2)}, u32[]{:S(2)}) collective-permute-start(f32[24,512]{1,0:T(8,128)S(1)} %get-tuple-element.28), channel_id=1, source_target_pairs={{4,0},{8,4},{12,8},{16,12},{20,16},{24,20},{28,24},{5,1},{9,5},{13... | collective-permute-start | bytes 147464 | tf_op jit(solution)/shard_map/ppermute | solution.py:418
  8.5 0.2 shard_map.67
  8.8 0.0 collective-permute-done.north_ref
  8.8 3.8 %collective-permute-done.1.south_ref = f32[24,512]{1,0:T(8,128)S(1)} collective-permute-done((f32[24,512]{1,0:T(8,128)S(1)}, f32[24,512]{1,0:T(8,128)S(1)}, u32[]{:S(2)}, u32[]{:S(2)}) %collective-permute-start.1) | collective-permute-done | bytes 49184 | tf_op jit(solution)/shard_map/ppermute | solution.py:418
  12.5 0.3 shard_map.69
  12.8 3.4 %collective-permute-start.2 = (f32[48,128]{1,0:T(8,128)S(1)}, f32[48,128]{1,0:T(8,128)S(1)}, u32[]{:S(2)}, u32[]{:S(2)}) collective-permute-start(f32[48,128]{1,0:T(8,128)S(1)} %get-tuple-element.29), channel_id=1, source_target_pairs={{0,1},{1,2},{2,3},{4,5},{5,6},{6,7},{8,9},{9,10},{10,11},{12,13},{... | collective-permute-start | bytes 73736 | tf_op jit(solution)/shard_map/ppermute | solution.py:419
  16.2 1.3 %collective-permute-start.3 = (f32[48,128]{1,0:T(8,128)S(1)}, f32[48,128]{1,0:T(8,128)S(1)}, u32[]{:S(2)}, u32[]{:S(2)}) collective-permute-start(f32[48,128]{1,0:T(8,128)S(1)} %get-tuple-element.30), channel_id=1, source_target_pairs={{1,0},{2,1},{3,2},{5,4},{6,5},{7,6},{9,8},{10,9},{11,10},{13,12},{... | collective-permute-start | bytes 73736 | tf_op jit(solution)/shard_map/ppermute | solution.py:418
  17.5 0.2 collective-permute-done.2.west_ref
  17.7 4.2 %collective-permute-done.3.east_ref = f32[48,128]{1,0:T(8,128)S(1)} collective-permute-done((f32[48,128]{1,0:T(8,128)S(1)}, f32[48,128]{1,0:T(8,128)S(1)}, u32[]{:S(2)}, u32[]{:S(2)}) %collective-permute-start.3) | collective-permute-done | bytes 24608 | tf_op jit(solution)/shard_map/ppermute | solution.py:418
  21.9 8.9 %shard_map.70 = (f32[5,288,128]{2,1,0:T(8,128)S(1)}, f32[5,288,128]{2,1,0:T(8,128)S(1)}, f32[5,288,128]{2,1,0:T(8,128)S(1)}, f32[5,288,128]{2,1,0:T(8,128)S(1)},...) custom-call(f32[4,256,128]{2,1,0:T(8,128)S(1)} %get-tuple-element.24, ...), custom_call_target="tpu_custom_call" | custom-call | tf_op jit(solution)/shard_map/pallas_call | solution.py:464
  30.8 13.9 %all_to_all.10.rows_ref = f32[32,1,128]{2,1,0:T(1,128)S(1)} all-to-all(f32[32,1,128]{2,1,0:T(1,128)S(1)} %get-tuple-element.31), channel_id=1, replica_groups=mesh['row'=8,'col'=4] {'row','col'}, dimensions={0} | all-to-all | bytes 32768 | tf_op jit(solution)/shard_map/all_to_all | solution.py:424
  44.7 10.0 %shard_map.71 = (f32[256,512]{1,0:T(8,128)}, f32[5,288,128]{2,1,0:T(8,128)S(1)}, f32[5,288,128]{2,1,0:T(8,128)S(1)}, f32[32,1,128]{2,1,0:T(1,128)S(1)}) custom-call(f32[32,1,128]{2,1,0:T(1,128)S(1)} %all_to_all.10.rows_ref, f32[5,288,128]{2,1,0:T(8,128)S(1)} %get-tuple-element.32.f_ref, f32[5,288,128]{2,1,0:T(8,128)S(1)} %get-tuple-element.33.c_ref, ...), custom_call_target="tpu_custom_call" | custom-call | tf_op jit(solution)/shard_map/pallas_call | solution.py:472
  54.7 8.9 %all_to_all.11.rows_ref = f32[32,1,128]{2,1,0:T(1,128)S(1)} all-to-all(f32[32,1,128]{2,1,0:T(1,128)S(1)} %get-tuple-element.40), channel_id=1, replica_groups=mesh['row'=8,'col'=4] {'row','col'}, dimensions={0} | all-to-all | bytes 32768 | tf_op jit(solution)/shard_map/all_to_all | solution.py:424
  63.5 1.5 %shard_map.72 = (f32[256,512]{1,0:T(8,128)}, f32[1,1]{1,0:T(1,128)}) custom-call(f32[32,1,128]{2,1,0:T(1,128)S(1)} %all_to_all.11.rows_ref, f32[5,288,128]{2,1,0:T(8,128)S(1)} %get-tuple-element.34.p_ref, f32[5,288,128]{2,1,0:T(8,128)S(1)} %get-tuple-element.41.u1_ref, f32[5,288,128]{2,1,0:T(8,128)S(1)} %get-tuple-element.42.u2_ref), custom_call_target="tpu_custom_call" | custom-call | tf_op jit(solution)/shard_map/pallas_call | solution.py:480
  (1 shorter events, 0.0 us)
Async XLA Ops:
  0.6 1.0 %copy-start = (f32[256,512]{1,0:T(8,128)S(1)}, f32[256,512]{1,0:T(8,128)}, u32[]{:S(2)}) copy-start(f32[256,512]{1,0:T(8,128)} %refs_4_.1) | copy-start | bytes 1572868
  1.7 1.0 %copy-start.1 = (f32[256,512]{1,0:T(8,128)S(1)}, f32[256,512]{1,0:T(8,128)}, u32[]{:S(2)}) copy-start(f32[256,512]{1,0:T(8,128)} %refs_5_.1) | copy-start | bytes 1572868
  2.7 1.0 %copy-start.2 = (f32[256,512]{1,0:T(8,128)S(1)}, f32[256,512]{1,0:T(8,128)}, u32[]{:S(2)}) copy-start(f32[256,512]{1,0:T(8,128)} %refs_6_.1) | copy-start | bytes 1572868
  3.8 1.0 %copy-start.3 = (f32[256,512]{1,0:T(8,128)S(1)}, f32[256,512]{1,0:T(8,128)}, u32[]{:S(2)}) copy-start(f32[256,512]{1,0:T(8,128)} %refs_7_.1) | copy-start | bytes 1572868
  4.8 3.9 %collective-permute-start = (f32[24,512]{1,0:T(8,128)S(1)}, f32[24,512]{1,0:T(8,128)S(1)}, u32[]{:S(2)}, u32[]{:S(2)}) collective-permute-start(f32[24,512]{1,0:T(8,128)S(1)} %get-tuple-element.27), channel_id=1, source_target_pairs={{0,4},{4,8},{8,12},{12,16},{16,20},{20,24},{24,28},{1,5},{5,9},{9,... | collective-permute-start | bytes 147464 | tf_op jit(solution)/shard_map/ppermute | solution.py:419
  7.2 5.3 %collective-permute-start.1 = (f32[24,512]{1,0:T(8,128)S(1)}, f32[24,512]{1,0:T(8,128)S(1)}, u32[]{:S(2)}, u32[]{:S(2)}) collective-permute-start(f32[24,512]{1,0:T(8,128)S(1)} %get-tuple-element.28), channel_id=1, source_target_pairs={{4,0},{8,4},{12,8},{16,12},{20,16},{24,20},{28,24},{5,1},{9,5},{13... | collective-permute-start | bytes 147464 | tf_op jit(solution)/shard_map/ppermute | solution.py:418
  12.8 4.9 %collective-permute-start.2 = (f32[48,128]{1,0:T(8,128)S(1)}, f32[48,128]{1,0:T(8,128)S(1)}, u32[]{:S(2)}, u32[]{:S(2)}) collective-permute-start(f32[48,128]{1,0:T(8,128)S(1)} %get-tuple-element.29), channel_id=1, source_target_pairs={{0,1},{1,2},{2,3},{4,5},{5,6},{6,7},{8,9},{9,10},{10,11},{12,13},{... | collective-permute-start | bytes 73736 | tf_op jit(solution)/shard_map/ppermute | solution.py:419
  16.2 5.7 %collective-permute-start.3 = (f32[48,128]{1,0:T(8,128)S(1)}, f32[48,128]{1,0:T(8,128)S(1)}, u32[]{:S(2)}, u32[]{:S(2)}) collective-permute-start(f32[48,128]{1,0:T(8,128)S(1)} %get-tuple-element.30), channel_id=1, source_target_pairs={{1,0},{2,1},{3,2},{5,4},{6,5},{7,6},{9,8},{10,9},{11,10},{13,12},{... | collective-permute-start | bytes 73736 | tf_op jit(solution)/shard_map/ppermute | solution.py:418

commit v2 on v1

v2 whole, which is shorter than its diff:
```python
import functools

import jax
import jax.numpy as jnp
from jax import lax
from jax.experimental import pallas as pl
from jax.experimental.pallas import tpu as pltpu
from jax.sharding import PartitionSpec as P

discount_rate = 0.05
diffusion = 0.25
SCALE = 0.0625
FACE = diffusion * 0.5 * SCALE
LANES = 128
SUB = 8
WIDE = 7
DEEP = 3
PAD = 2 * SUB
VMEM_BYTES = 16 * 2**20
VM = pl.BlockSpec(memory_space=pltpu.VMEM)
BOTH = ("row", "col")


def two_sum(a, b):
    s = a + b
    t = s - a
    return s, (a - (s - t)) + (b - t)


def fast_sum(a, b):
    s = a + b
    return s, b - (s - a)


def halves(a):
    t = a * 4097.0
    hi = t - (t - a)
    return hi, a - hi


def two_prod(a, b):
    p = a * b
    ah, al = halves(a)
    bh, bl = halves(b)
    return p, ((ah * bh - p) + ah * bl + al * bh) + al * bl


def dmul(a, b):
    p, e = two_prod(a[0], b[0])
    return fast_sum(p, e + (a[0] * b[1] + a[1] * b[0]))


def dsub(a, b):
    s, e = two_sum(a[0], -b[0])
    return fast_sum(s, e + (a[1] - b[1]))


def ddiv(a, b):
    q = a[0] / b[0]
    r = dsub(a, dmul((q, jnp.zeros_like(q)), b))
    return fast_sum(q, r[0] / b[0])


def galerkin(dots):
    d00, d01, d02, d03, d11, d12, d13, d22, d23 = dots
    zero = jnp.zeros_like(d00[0])
    l1 = ddiv(d11, d01)
    l2 = ddiv(d12, d01)
    s11 = dsub(d12, dmul(l1, d02))
    s12 = dsub(d13, dmul(l1, d03))
    s21 = dsub(d22, dmul(l2, d02))
    s22 = dsub(d23, dmul(l2, d03))
    g0 = (d00[0] * SCALE, d00[1] * SCALE)
    g1 = dsub((d01[0] * SCALE, d01[1] * SCALE), dmul(l1, g0))
    g2 = dsub((d02[0] * SCALE, d02[1] * SCALE), dmul(l2, g0))
    l3 = ddiv(s21, s11)
    t22 = dsub(s22, dmul(l3, s12))
    g2 = dsub(g2, dmul(l3, g1))
    full1 = s11[0] > 1e-12 * d12[0]
    full2 = full1 & (t22[0] > 1e-12 * d23[0])
    c2 = jnp.where(full2, ddiv(g2, t22)[0], zero)
    c1 = ddiv(dsub(g1, dmul(s12, (c2, zero))), s11)[0]
    c1 = jnp.where(full1, c1, zero)
    r0 = dsub(dsub(g0, dmul(d02, (c1, zero))), dmul(d03, (c2, zero)))
    return ddiv(r0, d01)[0], c1, c2


PAIRS = ((0, 0), (0, 1), (0, 2), (0, 3), (1, 1), (1, 2), (1, 3), (2, 2), (2, 3))


def split_short(a):
    t = a * 65537.0
    hi = t - (t - a)
    return hi, a - hi


def dot_step(groups, sums):
    parts = [[split_short(v) for v in vs] for vs in groups]
    out = []
    for k, (i, j) in enumerate(PAIRS):
        main = None
        rest = None
        for vs, ps in zip(groups, parts):
            m = ps[i][0] * ps[j][0]
            if i == j:
                r = ps[i][1] * (vs[i] + ps[i][0])
            else:
                r = ps[i][0] * ps[j][1] + ps[i][1] * vs[j]
            main = m if main is None else main + m
            rest = r if rest is None else rest + r
        s, e = two_sum(sums[2 * k], main)
        out += [s, sums[2 * k + 1] + (e + rest)]
    return tuple(out)


def pack_sums(sums, extra=()):
    lane = lax.broadcasted_iota(jnp.int32, (1, LANES), 1)
    row = jnp.zeros((1, LANES), jnp.float32)
    total = lambda a: jnp.sum(jnp.sum(a, axis=0, keepdims=True), axis=1, keepdims=True)
    for k in range(len(PAIRS)):
        s, e = sums[2 * k], sums[2 * k + 1]
        peak = jnp.max(jnp.max(jnp.abs(s), axis=0, keepdims=True), axis=1, keepdims=True)
        lift = jnp.broadcast_to(peak * 2048.0, s.shape)
        main = (s + lift) - lift
        row = jnp.where(lane == k, total(main), row)
        row = jnp.where(lane == 64 + k, total((s - main) + e), row)
    for k, a in enumerate(extra):
        row = jnp.where(lane == len(PAIRS) + k, total(a), row)
    return row


def gathered_sums(ref, extra=0):
    rows = [(ref[d], None) for d in range(ref.shape[0])]
    while len(rows) > 1:
        merged = []
        for k in range(0, len(rows) - 1, 2):
            (a, ea), (b, eb) = rows[k], rows[k + 1]
            s, e = two_sum(a, b)
            e = e if ea is None else e + (ea + eb)
            merged.append((s, e))
        if len(rows) % 2:
            a, ea = rows[-1]
            merged.append((a, jnp.zeros_like(a) if ea is None else ea))
        rows = merged
    s, e = rows[0]
    lane = lax.broadcasted_iota(jnp.int32, s.shape, 1)
    pick = lambda a, k: jnp.sum(jnp.where(lane == k, a, 0.0), axis=1, keepdims=True)
    dots = []
    for k in range(len(PAIRS)):
        hi = pick(s, k)
        lo = pick(e, k) + pick(s, 64 + k)
        dots.append(fast_sum(hi, lo))
    return dots, [pick(s, len(PAIRS) + k) for k in range(extra)]


def fields_of(rc, cx, cy):
    control_cost = 0.5 * (cx * cx + cy * cy)
    return rc + control_cost, 1.0 + control_cost


def edge_rows(rc, cx, cy, pd):
    return jnp.concatenate([*fields_of(rc, cx, cy), pd])


def neighbours_along(axis):
    i = lax.axis_index(axis)
    return i > 0, i < lax.axis_size(axis) - 1


def lanes():
    return lax.broadcasted_iota(jnp.int32, (SUB, LANES), 1)


def tile_cols(j):
    return slice(j * LANES, (j + 1) * LANES)


def halo_tile(ref, field, j, present):
    return jnp.where(present, ref[field * SUB : (field + 1) * SUB, tile_cols(j)], 0.0)


def packing(tiles):
    per = LANES // WIDE
    return per, -(-tiles // per)


def pack_columns_kernel(f_ref, c_ref, p_ref, north_ref, south_ref, west_ref, east_ref):
    tiles = f_ref.shape[0] // SUB + 2
    per, groups = packing(tiles)
    lane = lanes()
    has_north, has_south = neighbours_along("row")
    for field, own in enumerate((f_ref, c_ref, p_ref)):

        def tile(j, t):
            if t == 0:
                return halo_tile(north_ref, field, j, has_north)
            if t == tiles - 1:
                return halo_tile(south_ref, field, j, has_south)
            return own[(t - 1) * SUB : t * SUB, tile_cols(j)]

        for v in range(groups):
            west = jnp.zeros((SUB, LANES), jnp.float32)
            east = west
            for g in range(min(per, tiles - v * per)):
                here = (lane >= WIDE * g) & (lane < WIDE * (g + 1))
                a = tile(0, v * per + g)
                b = tile(f_ref.shape[1] // LANES - 1, v * per + g)
                west = jnp.where(here, pltpu.roll(a, (WIDE * g) % LANES, 1), west)
                east = jnp.where(here, pltpu.roll(b, (WIDE * (g + 1)) % LANES, 1), east)
            at = (field * groups + v) * SUB
            west_ref[at : at + SUB] = west
            east_ref[at : at + SUB] = east


def beside(ref, r, which, margin=False):
    lane = lanes()
    here = [ref[j, pl.ds(r, SUB), :] for j in which]
    south = [ref[j, pl.ds(r + 1, SUB), :] for j in which]
    north = [ref[j, pl.ds(r - 1, SUB), :] for j in which]
    left = [pltpu.roll(a, LANES - 1, 1) for a in here]
    right = [pltpu.roll(a, 1, 1) for a in here]
    n = len(which) - 1 if margin else len(which)
    over, under = left[:n], right[:n]
    past, before = left[0], right[n - 1]
    if margin:
        past = pltpu.roll(here[n], LANES - 1 - SUB, 1)
        before = pltpu.roll(here[n], 1 + SUB, 1)
    if n > 1 or margin:
        over = [jnp.where(lane == LANES - 1, left[k + 1] if k < n - 1 else past, left[k]) for k in range(n)]
        under = [jnp.where(lane == 0, right[k - 1] if k > 0 else before, right[k]) for k in range(n)]
    return here, south, north, over + left[n:], under + right[n:]


def weighted_apply(center, w, cells):
    here, south, north, east, west = cells
    return center * here - ((w[0] * south + w[1] * north) + (w[2] * east + w[3] * west))


def apply_tiles(ref, w_ref, center_ref, r, which, margin=False, center_at=None):
    cells = beside(ref, r, which, margin)
    at = pl.ds(r, SUB)
    out = []
    for i, j in enumerate(which):
        w = [w_ref[k, j, at, :] for k in range(4)]
        center = center_ref[j if center_at is None else center_at, at, :]
        out.append(weighted_apply(center, w, [c[i] for c in cells]))
    return out, cells[0]


def first_vector(f_ref, c_ref, v1_ref, w_ref, faces_ref, center_ref, r, which, center_at=None):
    at = pl.ds(r, SUB)
    cond = beside(c_ref, r, which)
    cells = beside(f_ref, r, which)
    for i, j in enumerate(which):
        c = cond[0][i]
        inside = jnp.minimum(c, 1.0)
        face = inside * FACE
        w = [face * (c + cond[k][i]) for k in (1, 2, 3, 4)]
        faces = (w[0] + w[1]) + (w[2] + w[3])
        center = inside * (discount_rate * SCALE) + faces
        for k in range(4):
            w_ref[k, j, at, :] = w[k]
        faces_ref[j, at, :] = faces
        center_ref[j if center_at is None else center_at, at, :] = center
        v1_ref[j, at, :] = weighted_apply(center, w, [x[i] for x in cells])


def clear_pads(refs, which):
    zero = jnp.zeros((SUB, LANES), jnp.float32)
    for ref in refs:
        rows = ref.shape[1]
        for j in which:
            ref[j, 0:SUB] = zero
            ref[j, rows - SUB : rows] = zero


def row_tiles(ref):
    return (ref.shape[1] - 2 * SUB) // SUB


def sweep(start, stop, step, unroll=2):
    def some(t, _):
        for u in range(unroll):
            step(pl.multiple_of(SUB + (start + t * unroll + u) * SUB, SUB))
        return 0

    whole = (stop - start) // unroll
    lax.fori_loop(0, whole, some, 0)
    for t in range(start + whole * unroll, stop):
        step(SUB + t * SUB)


def second_vector(v1_ref, v2_ref, w_ref, center_ref, which, margin=False, center_at=None, unroll=2):
    def step(r):
        out, _here = apply_tiles(v1_ref, w_ref, center_ref, r, which, margin, center_at)
        for i, j in enumerate(which):
            v2_ref[j, pl.ds(r, SUB), :] = out[i]

    sweep(0, row_tiles(v1_ref), step, unroll)


def products(v_refs, w_ref, center_ref, which, take, margin=False, center_at=None, unroll=2):
    v0_ref, v1_ref, v2_ref = v_refs
    own = which[:-1] if margin else which

    def step(t, sums):
        groups = []
        for u in range(unroll):
            r = pl.multiple_of(PAD + (t * unroll + u) * SUB, SUB)
            out, here = apply_tiles(v2_ref, w_ref, center_ref, r, which if margin else own, margin, center_at)
            at = pl.ds(r, SUB)
            for i, j in enumerate(own):
                vs = [v0_ref[j, at, :], v1_ref[j, at, :], here[i]]
                mask = take(j)
                if mask is not None:
                    vs = [jnp.where(mask, v, 0.0) for v in vs]
                groups.append((*vs, out[i]))
        return dot_step(groups, sums)

    zero = jnp.zeros((SUB, LANES), jnp.float32)
    return lax.fori_loop(0, (row_tiles(v0_ref) - 2) // unroll, step, (zero,) * (2 * len(PAIRS)))


def inner_first_kernel(f_in, c_in, f_ref, c_ref, v1_ref, w_ref, faces_ref, center_ref):
    own = list(range(f_ref.shape[0] - 1))
    rows = f_in.shape[0]
    clear_pads((f_ref, c_ref, v1_ref), own)
    for j in own:
        f_ref[j, PAD : PAD + rows] = f_in[:, tile_cols(j)]
        c_ref[j, PAD : PAD + rows] = c_in[:, tile_cols(j)]
    sweep(2, row_tiles(f_ref) - 2,
          lambda r: first_vector(f_ref, c_ref, v1_ref, w_ref, faces_ref, center_ref, r, own))


def inner_rest_kernel(after, p_in, north_ref, south_ref, f_in, c_in, v1_in, w_in, faces_in, center_in,
                      f_ref, c_ref, v1_ref, w_ref, faces_ref, center_ref, p_ref, v2_ref, sums_ref):
    count = f_ref.shape[0] - 1
    own = list(range(count))
    rows = f_ref.shape[1]
    tiles = row_tiles(f_ref)
    has_north, has_south = neighbours_along("row")
    clear_pads((p_ref, v2_ref), own)
    lane = lanes()
    for j in own:
        p_ref[j, PAD : rows - PAD] = p_in[:, tile_cols(j)]
    for field, ref in enumerate((f_ref, c_ref, p_ref)):
        for j in own:
            ref[j, SUB : 2 * SUB] = halo_tile(north_ref, field, j, has_north)
            ref[j, rows - 2 * SUB : rows - SUB] = halo_tile(south_ref, field, j, has_south)
        for t in range(1, tiles + 1):
            at = slice(t * SUB, (t + 1) * SUB)
            last = pltpu.roll(ref[count - 1, at], SUB, 1)
            first = pltpu.roll(ref[0, at], LANES - SUB, 1)
            ref[count, at] = jnp.where(lane < SUB, last, jnp.where(lane >= LANES - SUB, first, 0.0))
    for t in (0, 1, tiles - 2, tiles - 1):
        first_vector(f_ref, c_ref, v1_ref, w_ref, faces_ref, center_ref, SUB + t * SUB, own)
    second_vector(v1_ref, v2_ref, w_ref, center_ref, own)

    def take(j):
        mask = lane >= DEEP if j == 0 else None
        if j == count - 1:
            far = lane < LANES - DEEP
            mask = far if mask is None else mask & far
        return mask

    sums = products((f_ref, v1_ref, v2_ref), w_ref, center_ref, own, take)
    for k, a in enumerate(sums):
        sums_ref[k] = a


def margin_kernel(west_ref, east_ref, sums_in, f_in, c_in, p_in, v1_in, v2_in, w_in, faces_in,
                  f_ref, c_ref, p_ref, v1_ref, v2_ref, w_ref, faces_ref, row_ref, center_ref):
    count = f_ref.shape[0] - 1
    margin = [count]
    tiles = row_tiles(f_ref)
    per, groups = packing(tiles)
    lane = lanes()
    has_west, has_east = neighbours_along("col")
    take_east = (lane >= SUB) & (lane < SUB + WIDE) & has_east
    take_west = (lane >= LANES - SUB - WIDE) & (lane < LANES - SUB) & has_west
    clear_pads((f_ref, c_ref, p_ref, v1_ref, v2_ref), margin)
    for field, ref in enumerate((f_ref, c_ref, p_ref)):
        for t in range(tiles):
            v, g = divmod(t, per)
            src = slice((field * groups + v) * SUB, (field * groups + v + 1) * SUB)
            at = slice(SUB + t * SUB, 2 * SUB + t * SUB)
            west = pltpu.roll(west_ref[src], (LANES - SUB - WIDE * (g + 1)) % LANES, 1)
            east = pltpu.roll(east_ref[src], (SUB - WIDE * g) % LANES, 1)
            ref[count, at] = jnp.where(take_east, east, jnp.where(take_west, west, ref[count, at]))
    sweep(0, tiles, lambda r: first_vector(
        f_ref, c_ref, v1_ref, w_ref, faces_ref, center_ref, r, margin, 0), 4)
    second_vector(v1_ref, v2_ref, w_ref, center_ref, margin, center_at=0, unroll=4)
    mask = ((lane >= SUB - DEEP) & (lane < SUB)) | ((lane >= LANES - SUB) & (lane < LANES - SUB + DEEP))
    sums = products((f_ref, v1_ref, v2_ref), w_ref, center_ref, margin, lambda j: mask,
                    center_at=0, unroll=4)

    def patch(r):
        at = pl.ds(r, SUB)
        first, last = lane < DEEP, lane >= LANES - DEEP
        for ref in (v1_ref, v2_ref, faces_ref, w_ref.at[3]):
            ref[0, at, :] = jnp.where(first, pltpu.roll(ref[count, at, :], SUB, 1), ref[0, at, :])
        for ref in (v1_ref, v2_ref, faces_ref, w_ref.at[2]):
            tile = jnp.where(last, pltpu.roll(ref[count, at, :], LANES - SUB, 1), ref[count - 1, at, :])
            ref[count - 1, at, :] = tile

    sweep(0, tiles, patch)
    total = []
    for k in range(len(PAIRS)):
        s, e = two_sum(sums[2 * k], sums_in[2 * k])
        total += [s, e + (sums[2 * k + 1] + sums_in[2 * k + 1])]
    row_ref[...] = jnp.broadcast_to(pack_sums(total)[None], row_ref.shape)


def density_kernel(rows_ref, f_ref, c_ref, p_ref, v1_ref, v2_ref, w_ref, faces_ref,
                   value_ref, u1_ref, u2_ref, row_ref, vx_ref, center_ref):
    dots, _unused = gathered_sums(rows_ref)
    c0, c1, c2 = [jnp.broadcast_to(c, (SUB, LANES)) for c in galerkin(dots)]
    which = list(range(f_ref.shape[0]))
    own = which[:-1]
    tiles = row_tiles(f_ref)
    clear_pads((vx_ref, u1_ref, u2_ref), which)

    def value(r):
        at = pl.ds(r, SUB)
        for j in which:
            vx_ref[j, at, :] = (c0 * f_ref[j, at, :] + c1 * v1_ref[j, at, :]) + c2 * v2_ref[j, at, :]

    sweep(0, tiles, value)

    def first(r):
        at = pl.ds(r, SUB)
        val = beside(vx_ref, r, which, True)
        cells = beside(p_ref, r, which, True)
        for j in which:
            inside = jnp.minimum(c_ref[j, at, :], 1.0)
            slope_row = 0.5 * (val[1][j] - val[2][j])
            slope_col = 0.5 * (val[3][j] - val[4][j])
            congestion = (slope_row * slope_row + slope_col * slope_col) * (0.5 / diffusion)
            zeroth = (discount_rate + congestion) * SCALE
            center = inside * zeroth + faces_ref[j, at, :]
            center_ref[j, at, :] = center
            w = [w_ref[k, j, at, :] for k in range(4)]
            u1_ref[j, at, :] = weighted_apply(center, w, [x[j] for x in cells])

    sweep(0, tiles, first)

    def outer(t, sums):
        r = pl.multiple_of(PAD + t * SUB, SUB)
        at = pl.ds(r, SUB)
        to = pl.ds(pl.multiple_of(t * SUB, SUB), SUB)
        cost, weight = sums
        for j in own:
            v = vx_ref[j, at, :]
            p = p_ref[j, at, :]
            value_ref[to, tile_cols(j)] = v
            cost = cost + p * (f_ref[j, at, :] - discount_rate * v)
            weight = weight + p
        return cost, weight

    zero = jnp.zeros((SUB, LANES), jnp.float32)
    extra = lax.fori_loop(0, tiles - 2, outer, (zero, zero))
    second_vector(u1_ref, u2_ref, w_ref, center_ref, which, True)
    sums = products((p_ref, u1_ref, u2_ref), w_ref, center_ref, which, lambda j: None, True)
    row_ref[...] = jnp.broadcast_to(pack_sums(sums, extra)[None], row_ref.shape)


def finish_kernel(rows_ref, p_ref, u1_ref, u2_ref, density_ref, ergodic_ref):
    dots, (cost, weight) = gathered_sums(rows_ref, 2)
    ergodic_ref[...] = cost / weight
    c0, c1, c2 = [jnp.broadcast_to(c, (SUB, LANES)) for c in galerkin(dots)]
    own = p_ref.shape[0] - 1

    def tile(t, _):
        at = pl.ds(pl.multiple_of(PAD + t * SUB, SUB), SUB)
        to = pl.ds(pl.multiple_of(t * SUB, SUB), SUB)
        for j in range(own):
            density_ref[to, j * LANES : (j + 1) * LANES] = (
                c0 * p_ref[j, at, :] + c1 * u1_ref[j, at, :]
            ) + c2 * u2_ref[j, at, :]
        return 0

    lax.fori_loop(0, density_ref.shape[0] // SUB, tile, 0)


def f32(*shape):
    return jax.ShapeDtypeStruct(shape, jnp.float32)


def exchange(back, ahead, axis):
    count = lax.axis_size(axis)
    after = lax.ppermute(back, axis, [((i + 1) % count, i) for i in range(count)])
    before = lax.ppermute(ahead, axis, [(i, (i + 1) % count) for i in range(count)])
    return before, after


def everyone(row):
    return lax.all_to_all(row, BOTH, 0, 0, tiled=True)


def body(*args):
    rows, cols = args[0].shape
    devices = lax.axis_size("row") * lax.axis_size("col")
    count = cols // LANES
    ext = f32(count + 1, rows + 2 * PAD, LANES)
    ext4 = f32(4, *ext.shape)
    everyones = f32(devices, 1, LANES)
    _per, groups = packing(rows // SUB + 2)
    small = pltpu.CompilerParams(vmem_limit_bytes=VMEM_BYTES)

    def call(kernel, ins, outs, scratch=0, **more):
        return pl.pallas_call(
            kernel,
            in_specs=[VM] * len(ins),
            out_specs=[VM] * len(outs),
            out_shape=outs,
            scratch_shapes=[pltpu.VMEM(ext.shape if scratch > 1 else (1, *ext.shape[1:]), jnp.float32)] * scratch,
            compiler_params=small,
            **more,
        )(*ins)

    cost = lambda us: pl.CostEstimate(flops=0, bytes_accessed=int(us * 2e6), transcendentals=0)
    up, down = [edge_rows(*[x[at] for x in args]) for at in (slice(0, SUB), slice(rows - SUB, rows))]
    north, south = exchange(up, down, "row")
    forcing, conduct = fields_of(*args[:3])
    prior = args[3]
    f, c, v1, w, faces, center = call(
        inner_first_kernel, (forcing, conduct), [ext] * 3 + [ext4, ext, ext], cost_estimate=cost(1.5))
    packs = call(
        pack_columns_kernel, (forcing, conduct, prior, north, south), [f32(3 * groups * SUB, LANES)] * 2)
    west, east = exchange(*packs, "col")
    f, c, v1, w, faces, _center, p, v2, sums = call(
        inner_rest_kernel, (packs[0], prior, north, south, f, c, v1, w, faces, center),
        [ext] * 3 + [ext4] + [ext] * 4 + [f32(2 * len(PAIRS), SUB, LANES)],
        input_output_aliases={4 + k: k for k in range(6)}, cost_estimate=cost(4))
    f, c, p, v1, v2, w, faces, row = call(
        margin_kernel, (west, east, sums, f, c, p, v1, v2, w, faces),
        [ext] * 5 + [ext4, ext, everyones], 1, input_output_aliases={3 + k: k for k in range(7)})
    value, u1, u2, row = call(
        density_kernel, (everyone(row), f, c, p, v1, v2, w, faces),
        [f32(rows, cols), ext, ext, everyones], 2)
    density, ergodic = call(finish_kernel, (everyone(row), p, u1, u2), [f32(rows, cols), f32(1, 1)])
    return value, density, ergodic[0, 0]


def solution(mesh):
    spec = P("row", "col")
    return jax.shard_map(body, mesh=mesh, in_specs=(spec,) * 4, out_specs=(spec, spec, P()), check_vma=False)
```

time: 65.4 us -> 51.9 us (0.79)
  waiting for transfers between devices: 8.18 us -> 0.21 us
  local copies, waits for them, and re-layouts: 4.16 us -> 0.01 us
  other arithmetic: 0 us -> 2.46 us
  Pallas kernels: 20.8 us -> 19 us
  blocking collectives: 22.8 us -> 21.5 us
  starting transfers between devices: 8.38 us -> 7.63 us
    ppermute x4, waiting for transfers between devices: 8.18 us -> 0.21 us  [the longest x2 0.15 us: exchange(): lax.ppermute(ahead, axis, [(i, (i + 1) % count) for i in range(count)])]
    unnamed x8 -> x2, local copies, waits for them, and re-layouts: 4.16 us -> 0.01 us
    add x0 -> x2, other arithmetic: none -> 2.45 us  [fields_of(): return (rc + control_cost, 1.0 + control_cost)]
    pallas_call x6, Pallas kernels: 20.8 us -> 19 us  [call(): pl.pallas_call(kernel, in_specs=[VM] * len(ins), out_specs=[VM] * len(out...]
    all_to_all x2, blocking collectives: 22.8 us -> 21.5 us  [everyone(): return lax.all_to_all(row, BOTH, 0, 0, tiled=True)]
    ppermute x4, starting transfers between devices: 8.38 us -> 7.63 us  [the longest x2 7.09 us: exchange(): lax.ppermute(back, axis, [((i + 1) % count, i) for i in range(count)])]
  transfers between devices with their start and end apart: 4 -> 4, of which waited for: 3 -> 2; matrix products, arithmetic and copies ran while one was open for 0% -> 3% of each run, Pallas kernels for 0% -> 11%
where the time goes in v2:
time: 51.9 us; the launch traced here: 51.6 us
  blocking collectives  21.5 us (41%)
  Pallas kernels  19 us (37%)
  starting transfers between devices  7.63 us (15%)
  other arithmetic  2.46 us (5%)
  between operations  0.71 us (1%)
    all_to_all x2, blocking collectives, everyone(): return lax.all_to_all(row, BOTH, 0, 0, tiled=True)  21.5 us
    pallas_call x6, Pallas kernels, call(): pl.pallas_call(kernel, in_specs=[VM] * len(ins), out_specs=[VM] * len(out...  19 us
    ppermute x2, starting transfers between devices, exchange(): lax.ppermute(back, axis, [((i + 1) % count, i) for i in range(count)])  7.09 us
    add x2, other arithmetic, fields_of(): return (rc + control_cost, 1.0 + control_cost)  2.45 us
  transfers between devices with their start and end apart: 4, of which 2 were waited for; matrix products, arithmetic and copies ran while one was open for 3% of the time, Pallas kernels for 11%

profile of v2, /device:TPU:0, one launch (start us, length us, event | category | flops | bytes accessed | tf_op | source)
XLA Modules:
  0.0 51.6 jit_solution(10091404307321370202)
XLA Ops:
  0.6 0.0 copy-start
  0.6 0.9 %slice_add_fusion = (f32[8,512]{1,0:T(8,128)S(1)}, f32[8,512]{1,0:T(8,128)S(1)}, f32[8,512]{1,0:T(8,128)S(1)}, f32[8,512]{1,0:T(8,128)S(1)}, f32[8,512]{1,0:T(8,128)S(1)}, /*index=5*/f32[8,512]{1,0:T(8,128)S(1)}) fusion(f32[256,512]{1,0:T(8,128)} %param.4, f32[256,512]{1,0:T(8,128)} %param.6, f32[256,512]{1,0:T(8,128)} %param.5, f32[256,512]{1,0:T(8,128)} %p_in.1), kind=kLoop, calls=%fused_computation.6 | loop fusion | flops 49152 | bytes 229376 | tf_op jit(solution)/shard_map/add | solution.py:158
  1.6 0.5 %collective-permute-start = (f32[24,512]{1,0:T(8,128)S(1)}, f32[24,512]{1,0:T(8,128)S(1)}, u32[]{:S(2)}, u32[]{:S(2)}) collective-permute-start(f32[24,512]{1,0:T(8,128)S(1)} %pad_maximum_fusion), channel_id=1, source_target_pairs={{0,4},{4,8},{8,12},{12,16},{16,20},{20,24},{24,28},{28,0},{1,5},{5... | collective-permute-start | bytes 147464 | tf_op jit(solution)/shard_map/ppermute | solution.py:492
  2.1 4.1 %collective-permute-start.1 = (f32[24,512]{1,0:T(8,128)S(1)}, f32[24,512]{1,0:T(8,128)S(1)}, u32[]{:S(2)}, u32[]{:S(2)}) collective-permute-start(f32[24,512]{1,0:T(8,128)S(1)} %pad_maximum_fusion.1), channel_id=1, source_target_pairs={{4,0},{8,4},{12,8},{16,12},{20,16},{24,20},{28,24},{0,28},{5,1},{9... | collective-permute-start | bytes 147464 | tf_op jit(solution)/shard_map/ppermute | solution.py:491
  6.2 1.5 %broadcast_add_fusion = (f32[256,512]{1,0:T(8,128)S(1)}, f32[256,512]{1,0:T(8,128)S(1)}) fusion(f32[256,512]{1,0:T(8,128)} %param.6, f32[256,512]{1,0:T(8,128)} %param.5, f32[256,512]{1,0:T(8,128)} %param.4), kind=kLoop, calls=%fused_computation.1 | loop fusion | flops 786432 | bytes 2621440 | tf_op jit(solution)/shard_map/add | solution.py:158
  7.8 0.1 collective-permute-done.north_ref
  7.9 0.1 collective-permute-done.1.south_ref
  8.0 0.0 copy-done
  8.0 0.3 shard_map.67
  8.2 3.0 %collective-permute-start.3 = (f32[48,128]{1,0:T(8,128)S(1)}, f32[48,128]{1,0:T(8,128)S(1)}, u32[]{:S(2)}, u32[]{:S(2)}) collective-permute-start(f32[48,128]{1,0:T(8,128)S(1)} %get-tuple-element.34.after), channel_id=1, source_target_pairs={{1,0},{2,1},{3,2},{0,3},{5,4},{6,5},{7,6},{4,7},{9,8},{10,9},{11,1... | collective-permute-start | bytes 73736 | tf_op jit(solution)/shard_map/ppermute | solution.py:491
  11.2 0.0 collective-permute-start.2
  11.2 1.7 %shard_map.68 = (f32[5,288,128]{2,1,0:T(8,128)S(1)}, f32[5,288,128]{2,1,0:T(8,128)S(1)}, f32[5,288,128]{2,1,0:T(8,128)S(1)}, f32[4,5,288,128]{3,2,1,0:T(8,128)S(...) custom-call(f32[256,512]{1,0:T(8,128)S(1)} %get-tuple-element.68.f_ref.f_in, ...), custom_call_target="tpu_custom_call" | custom-call | bytes 3000000 | tf_op jit(solution)/shard_map/pallas_call | solution.py:511
  13.0 3.9 %shard_map.69 = (f32[5,288,128]{2,1,0:T(8,128)S(1)}, f32[5,288,128]{2,1,0:T(8,128)S(1)}, f32[5,288,128]{2,1,0:T(8,128)S(1)}, f32[4,5,288,128]{3,2,1,0:T(8,128)S(...) custom-call(f32[48,128]{1,0:T(8,128)S(1)} %get-tuple-element.34.afte, ...), custom_call_target="tpu_custom_call", output_to_operand_aliasing={{0}: (4, {}), {1}: (5, {}), {2}: (6, {}), {3}: (7, {}), {4}... | custom-call | bytes 8000000 | tf_op jit(solution)/shard_map/pallas_call | solution.py:511
  16.8 0.0 collective-permute-done.3.east_ref
  16.8 0.0 collective-permute-done.2.west_ref
  16.8 4.2 %shard_map.70 = (f32[5,288,128]{2,1,0:T(8,128)S(1)}, f32[5,288,128]{2,1,0:T(8,128)S(1)}, f32[5,288,128]{2,1,0:T(8,128)S(1)}, f32[5,288,128]{2,1,0:T(8,128)S(1)},...) custom-call(f32[48,128]{1,0:T(8,128)S(1)} %collective-permute-done.2, ...), custom_call_target="tpu_custom_call", output_to_operand_aliasing={{0}: (3, {}), {1}: (4, {}), {2}: (5, {}), {3}: (6, {}), {4}... | custom-call | tf_op jit(solution)/shard_map/pallas_call | solution.py:511
  21.1 12.7 %all_to_all.10.rows_ref = f32[32,1,128]{2,1,0:T(1,128)S(1)} all-to-all(f32[32,1,128]{2,1,0:T(1,128)S(1)} %get-tuple-element.49), channel_id=1, replica_groups=mesh['row'=8,'col'=4] {'row','col'}, dimensions={0} | all-to-all | bytes 32768 | tf_op jit(solution)/shard_map/all_to_all | solution.py:497
  33.8 7.5 %shard_map.71 = (f32[256,512]{1,0:T(8,128)}, f32[5,288,128]{2,1,0:T(8,128)S(1)}, f32[5,288,128]{2,1,0:T(8,128)S(1)}, f32[32,1,128]{2,1,0:T(1,128)S(1)}) custom-call(f32[32,1,128]{2,1,0:T(1,128)S(1)} %all_to_all.10.rows_ref, f32[5,288,128]{2,1,0:T(8,128)S(1)} %get-tuple-element.50.f_ref, f32[5,288,128]{2,1,0:T(8,128)S(1)} %get-tuple-element.51.c_ref, ...), custom_call_target="tpu_custom_call" | custom-call | tf_op jit(solution)/shard_map/pallas_call | solution.py:511
  41.2 8.9 %all_to_all.11.rows_ref = f32[32,1,128]{2,1,0:T(1,128)S(1)} all-to-all(f32[32,1,128]{2,1,0:T(1,128)S(1)} %get-tuple-element.58), channel_id=1, replica_groups=mesh['row'=8,'col'=4] {'row','col'}, dimensions={0} | all-to-all | bytes 32768 | tf_op jit(solution)/shard_map/all_to_all | solution.py:497
  50.1 1.5 %shard_map.72 = (f32[256,512]{1,0:T(8,128)}, f32[1,1]{1,0:T(1,128)}) custom-call(f32[32,1,128]{2,1,0:T(1,128)S(1)} %all_to_all.11.rows_ref, f32[5,288,128]{2,1,0:T(8,128)S(1)} %get-tuple-element.52.p_ref, f32[5,288,128]{2,1,0:T(8,128)S(1)} %get-tuple-element.59.u1_ref, f32[5,288,128]{2,1,0:T(8,128)S(1)} %get-tuple-element.60.u2_ref), custom_call_target="tpu_custom_call" | custom-call | tf_op jit(solution)/shard_map/pallas_call | solution.py:511
  (2 shorter events, 0.0 us)
Async XLA Ops:
  0.6 7.3 %copy-start = (f32[256,512]{1,0:T(8,128)S(1)}, f32[256,512]{1,0:T(8,128)}, u32[]{:S(2)}) copy-start(f32[256,512]{1,0:T(8,128)} %p_in.1) | copy-start | bytes 1572868
  1.6 6.3 %collective-permute-start = (f32[24,512]{1,0:T(8,128)S(1)}, f32[24,512]{1,0:T(8,128)S(1)}, u32[]{:S(2)}, u32[]{:S(2)}) collective-permute-start(f32[24,512]{1,0:T(8,128)S(1)} %pad_maximum_fusion), channel_id=1, source_target_pairs={{0,4},{4,8},{8,12},{12,16},{16,20},{20,24},{24,28},{28,0},{1,5},{5... | collective-permute-start | bytes 147464 | tf_op jit(solution)/shard_map/ppermute | solution.py:492
  2.1 5.9 %collective-permute-start.1 = (f32[24,512]{1,0:T(8,128)S(1)}, f32[24,512]{1,0:T(8,128)S(1)}, u32[]{:S(2)}, u32[]{:S(2)}) collective-permute-start(f32[24,512]{1,0:T(8,128)S(1)} %pad_maximum_fusion.1), channel_id=1, source_target_pairs={{4,0},{8,4},{12,8},{16,12},{20,16},{24,20},{28,24},{0,28},{5,1},{9... | collective-permute-start | bytes 147464 | tf_op jit(solution)/shard_map/ppermute | solution.py:491
  8.2 8.6 %collective-permute-start.3 = (f32[48,128]{1,0:T(8,128)S(1)}, f32[48,128]{1,0:T(8,128)S(1)}, u32[]{:S(2)}, u32[]{:S(2)}) collective-permute-start(f32[48,128]{1,0:T(8,128)S(1)} %get-tuple-element.34.after), channel_id=1, source_target_pairs={{1,0},{2,1},{3,2},{0,3},{5,4},{6,5},{7,6},{4,7},{9,8},{10,9},{11,1... | collective-permute-start | bytes 73736 | tf_op jit(solution)/shard_map/ppermute | solution.py:491
  11.2 5.6 %collective-permute-start.2 = (f32[48,128]{1,0:T(8,128)S(1)}, f32[48,128]{1,0:T(8,128)S(1)}, u32[]{:S(2)}, u32[]{:S(2)}) collective-permute-start(f32[48,128]{1,0:T(8,128)S(1)} %get-tuple-element.33), channel_id=1, source_target_pairs={{0,1},{1,2},{2,3},{3,0},{4,5},{5,6},{6,7},{7,4},{8,9},{9,10},{10,1... | collective-permute-start | bytes 73736 | tf_op jit(solution)/shard_map/ppermute | solution.py:492

commit v3 on v2

v3 whole, which is shorter than its diff:
```python
import functools

import jax
import jax.numpy as jnp
from jax import lax
from jax.experimental import pallas as pl
from jax.experimental.pallas import tpu as pltpu
from jax.sharding import PartitionSpec as P

discount_rate = 0.05
diffusion = 0.25
SCALE = 0.0625
FACE = diffusion * 0.5 * SCALE
LANES = 128
SUB = 8
WIDE = 7
EDGE = 10
DEEP = 5
PAD = 2 * SUB
VMEM_BYTES = 16 * 2**20
VM = pl.BlockSpec(memory_space=pltpu.VMEM)
BOTH = ("row", "col")


def two_sum(a, b):
    s = a + b
    t = s - a
    return s, (a - (s - t)) + (b - t)


def fast_sum(a, b):
    s = a + b
    return s, b - (s - a)


def halves(a):
    t = a * 4097.0
    hi = t - (t - a)
    return hi, a - hi


def two_prod(a, b):
    p = a * b
    ah, al = halves(a)
    bh, bl = halves(b)
    return p, ((ah * bh - p) + ah * bl + al * bh) + al * bl


def dmul(a, b):
    p, e = two_prod(a[0], b[0])
    return fast_sum(p, e + (a[0] * b[1] + a[1] * b[0]))


def dsub(a, b):
    s, e = two_sum(a[0], -b[0])
    return fast_sum(s, e + (a[1] - b[1]))


def ddiv(a, b):
    q = a[0] / b[0]
    r = dsub(a, dmul((q, jnp.zeros_like(q)), b))
    return fast_sum(q, r[0] / b[0])


def galerkin(dots):
    d00, d01, d02, d03, d11, d12, d13, d22, d23 = dots
    zero = jnp.zeros_like(d00[0])
    l1 = ddiv(d11, d01)
    l2 = ddiv(d12, d01)
    s11 = dsub(d12, dmul(l1, d02))
    s12 = dsub(d13, dmul(l1, d03))
    s21 = dsub(d22, dmul(l2, d02))
    s22 = dsub(d23, dmul(l2, d03))
    g0 = (d00[0] * SCALE, d00[1] * SCALE)
    g1 = dsub((d01[0] * SCALE, d01[1] * SCALE), dmul(l1, g0))
    g2 = dsub((d02[0] * SCALE, d02[1] * SCALE), dmul(l2, g0))
    l3 = ddiv(s21, s11)
    t22 = dsub(s22, dmul(l3, s12))
    g2 = dsub(g2, dmul(l3, g1))
    full1 = s11[0] > 1e-12 * d12[0]
    full2 = full1 & (t22[0] > 1e-12 * d23[0])
    c2 = jnp.where(full2, ddiv(g2, t22)[0], zero)
    c1 = ddiv(dsub(g1, dmul(s12, (c2, zero))), s11)[0]
    c1 = jnp.where(full1, c1, zero)
    r0 = dsub(dsub(g0, dmul(d02, (c1, zero))), dmul(d03, (c2, zero)))
    return ddiv(r0, d01)[0], c1, c2


PAIRS = ((0, 0), (0, 1), (0, 2), (0, 3), (1, 1), (1, 2), (1, 3), (2, 2), (2, 3))


def split_short(a):
    t = a * 65537.0
    hi = t - (t - a)
    return hi, a - hi


def dot_step(groups, sums):
    parts = [[split_short(v) for v in vs] for vs in groups]
    out = []
    for k, (i, j) in enumerate(PAIRS):
        main = None
        rest = None
        for vs, ps in zip(groups, parts):
            m = ps[i][0] * ps[j][0]
            if i == j:
                r = ps[i][1] * (vs[i] + ps[i][0])
            else:
                r = ps[i][0] * ps[j][1] + ps[i][1] * vs[j]
            main = m if main is None else main + m
            rest = r if rest is None else rest + r
        s, e = two_sum(sums[2 * k], main)
        out += [s, sums[2 * k + 1] + (e + rest)]
    return tuple(out)


def pack_sums(sums, extra=()):
    lane = lax.broadcasted_iota(jnp.int32, (1, LANES), 1)
    row = jnp.zeros((1, LANES), jnp.float32)
    total = lambda a: jnp.sum(jnp.sum(a, axis=0, keepdims=True), axis=1, keepdims=True)
    for k in range(len(PAIRS)):
        s, e = sums[2 * k], sums[2 * k + 1]
        peak = jnp.max(jnp.max(jnp.abs(s), axis=0, keepdims=True), axis=1, keepdims=True)
        lift = jnp.broadcast_to(peak * 2048.0, s.shape)
        main = (s + lift) - lift
        row = jnp.where(lane == k, total(main), row)
        row = jnp.where(lane == 64 + k, total((s - main) + e), row)
    for k, a in enumerate(extra):
        row = jnp.where(lane == len(PAIRS) + k, total(a), row)
    return row


def gathered_sums(ref, extra=0):
    rows = [(ref[d], None) for d in range(ref.shape[0])]
    while len(rows) > 1:
        merged = []
        for k in range(0, len(rows) - 1, 2):
            (a, ea), (b, eb) = rows[k], rows[k + 1]
            s, e = two_sum(a, b)
            e = e if ea is None else e + (ea + eb)
            merged.append((s, e))
        if len(rows) % 2:
            a, ea = rows[-1]
            merged.append((a, jnp.zeros_like(a) if ea is None else ea))
        rows = merged
    s, e = rows[0]
    lane = lax.broadcasted_iota(jnp.int32, s.shape, 1)
    pick = lambda a, k: jnp.sum(jnp.where(lane == k, a, 0.0), axis=1, keepdims=True)
    dots = []
    for k in range(len(PAIRS)):
        hi = pick(s, k)
        lo = pick(e, k) + pick(s, 64 + k)
        dots.append(fast_sum(hi, lo))
    return dots, [pick(s, len(PAIRS) + k) for k in range(extra)]


FIRST = EDGE + 2 * WIDE


def fields_of(rc, cx, cy):
    control_cost = 0.5 * (cx * cx + cy * cy)
    return rc + control_cost, 1.0 + control_cost


def edge_rows(rc, cx, cy, pd):
    return jnp.concatenate([*fields_of(rc, cx, cy), pd])


def neighbours_along(axis):
    i = lax.axis_index(axis)
    return i > 0, i < lax.axis_size(axis) - 1


def lanes():
    return lax.broadcasted_iota(jnp.int32, (SUB, LANES), 1)


def tile_cols(j):
    return slice(j * LANES, (j + 1) * LANES)


def halo_tile(ref, field, j, present):
    return jnp.where(present, ref[field * SUB : (field + 1) * SUB, tile_cols(j)], 0.0)


def packing(tiles):
    per = LANES // (2 * WIDE)
    return per, -(-tiles // per)


def pack_columns_kernel(f_ref, c_ref, p_ref, north_ref, south_ref, west_ref, east_ref):
    tiles = row_tiles(f_ref)
    per, groups = packing(tiles)
    end = p_ref.shape[1] // LANES - 1
    lane = lanes()
    has_north, has_south = neighbours_along("row")
    for field in range(3):

        def tile(j, t):
            if t == 0:
                return halo_tile(north_ref, field, j, has_north)
            if t == tiles - 1:
                return halo_tile(south_ref, field, j, has_south)
            if field == 2:
                return p_ref[(t - 1) * SUB : t * SUB, tile_cols(j)]
            return (f_ref, c_ref)[field][j, (t + 1) * SUB : (t + 2) * SUB]

        for v in range(groups):
            west = jnp.zeros((SUB, LANES), jnp.float32)
            east = west
            for g in range(min(per, tiles - v * per)):
                at = 2 * WIDE * g
                a, b = tile(0, v * per + g), tile(end, v * per + g)
                west = jnp.where((lane >= at) & (lane < at + WIDE), pltpu.roll(a, at, 1), west)
                there = (lane >= at + WIDE) & (lane < at + 2 * WIDE)
                east = jnp.where(there, pltpu.roll(b, (at + 2 * WIDE) % LANES, 1), east)
            at = (field * groups + v) * SUB
            west_ref[at : at + SUB] = west
            east_ref[at : at + SUB] = east


def beside(ref, r, which):
    lane = lanes()
    n = len(which)
    here = [ref[j, pl.ds(r, SUB), :] for j in which]
    south = [ref[j, pl.ds(r + 1, SUB), :] for j in which]
    north = [ref[j, pl.ds(r - 1, SUB), :] for j in which]
    east = [pltpu.roll(a, LANES - 1, 1) for a in here]
    west = [pltpu.roll(a, 1, 1) for a in here]
    if n > 1:
        east, west = (
            [jnp.where(lane == LANES - 1, east[(k + 1) % n], east[k]) for k in range(n)],
            [jnp.where(lane == 0, west[k - 1], west[k]) for k in range(n)],
        )
    return [dict(zip(which, x)) for x in (here, south, north, east, west)]


def beside_all(ref, r, parts):
    found = [beside(ref, r, which) for which in parts]
    return [{j: x for part in found for j, x in part[k].items()} for k in range(5)]


def weighted_apply(center, w, cells):
    here, south, north, east, west = cells
    return center * here - ((w[0] * south + w[1] * north) + (w[2] * east + w[3] * west))


def apply_tiles(ref, w_ref, center_ref, r, parts):
    cells = beside_all(ref, r, parts)
    at = pl.ds(r, SUB)
    out = {}
    for j in cells[0]:
        w = [w_ref[k, j, at, :] for k in range(4)]
        out[j] = weighted_apply(center_ref[j, at, :], w, [c[j] for c in cells])
    return out, cells[0]


def first_vector(f_ref, c_ref, v1_ref, w_ref, faces_ref, center_ref, r, which):
    at = pl.ds(r, SUB)
    cond = beside(c_ref, r, which)
    cells = beside(f_ref, r, which)
    out = []
    for j in which:
        c = cond[0][j]
        inside = jnp.minimum(c, 1.0)
        face = inside * FACE
        w = [face * (c + cond[k][j]) for k in (1, 2, 3, 4)]
        faces = (w[0] + w[1]) + (w[2] + w[3])
        center = inside * (discount_rate * SCALE) + faces
        out += [(w_ref.at[k], j, at, w[k]) for k in range(4)]
        out.append((faces_ref, j, at, faces))
        out.append((center_ref, j, at, center))
        out.append((v1_ref, j, at, weighted_apply(center, w, [x[j] for x in cells])))
    return out


def clear_pads(refs, which):
    zero = jnp.zeros((SUB, LANES), jnp.float32)
    for ref in refs:
        rows = ref.shape[1]
        for j in which:
            ref[j, 0:SUB] = zero
            ref[j, rows - SUB : rows] = zero


def row_tiles(ref):
    return (ref.shape[1] - 2 * SUB) // SUB


def sweep(start, stop, step, unroll=2):
    def group(rows):
        stores = [store for r in rows for store in step(r)]
        for ref, j, at, value in stores:
            ref[j, at, :] = value

    def some(t, _):
        base = start + t * unroll
        group([pl.multiple_of(SUB + (base + u) * SUB, SUB) for u in range(unroll)])
        return 0

    whole = (stop - start) // unroll
    lax.fori_loop(0, whole, some, 0)
    rest = range(start + whole * unroll, stop)
    if len(rest):
        group([SUB + t * SUB for t in rest])


def second_vector(v1_ref, v2_ref, w_ref, center_ref, parts, unroll=8):
    def step(r):
        out, _here = apply_tiles(v1_ref, w_ref, center_ref, r, parts)
        return [(v2_ref, j, pl.ds(r, SUB), x) for j, x in out.items()]

    sweep(0, row_tiles(v1_ref), step, unroll)


def no_sums():
    return (jnp.zeros((SUB, LANES), jnp.float32),) * (2 * len(PAIRS))


def own_products(v0_ref, v1_ref, v2_ref, w_ref, center_ref, sums, unroll=2):
    own = list(range(v0_ref.shape[0] - 1))
    lane = lanes()

    def step(t, sums):
        groups = []
        for u in range(unroll):
            r = pl.multiple_of(PAD + (t * unroll + u) * SUB, SUB)
            out, here = apply_tiles(v2_ref, w_ref, center_ref, r, [own])
            at = pl.ds(r, SUB)
            for j in own:
                vs = [v0_ref[j, at, :], v1_ref[j, at, :], here[j]]
                if j == 0:
                    vs = [jnp.where(lane >= DEEP, v, 0.0) for v in vs]
                if j == own[-1]:
                    vs = [jnp.where(lane < LANES - DEEP, v, 0.0) for v in vs]
                groups.append((*vs, out[j]))
        return dot_step(groups, sums)

    return lax.fori_loop(0, (row_tiles(v0_ref) - 2) // unroll, step, sums)


def margin_products(v0_ref, v1_ref, v2_ref, w_ref, center_ref, sums):
    margin = v0_ref.shape[0] - 1
    lane = lanes()
    span = FIRST + DEEP - (EDGE - DEEP)
    runs = (FIRST - EDGE + DEEP) // DEEP
    block = span + (runs - 1) * DEEP
    slots = [block * b + DEEP * k for b in range(LANES // block) for k in range(runs)]
    tiles = row_tiles(v0_ref) - 2
    groups = []
    for start in range(0, tiles, len(slots)):
        packed = None
        for t, slot in zip(range(start, tiles), slots):
            at = slice(PAD + t * SUB, PAD + (t + 1) * SUB)
            out, here = apply_tiles(v2_ref, w_ref, center_ref, PAD + t * SUB, [[margin]])
            vs = [v0_ref[margin, at], v1_ref[margin, at], here[margin], out[margin]]
            put = (slot - (EDGE - DEEP)) % LANES
            vs = [pltpu.roll(v, put, 1) if put else v for v in vs]
            low, high = slot, slot + span - DEEP
            mask = ((lane >= low) & (lane < low + DEEP)) | ((lane >= high) & (lane < high + DEEP))
            if packed is None:
                packed = [jnp.where(mask, v, 0.0) for v in vs]
            else:
                packed = [jnp.where(mask, v, x) for v, x in zip(vs, packed)]
        groups.append(tuple(packed))
    return dot_step(groups, sums)


def with_sides(tile, side, j, count):
    lane = lanes()
    if j == 0:
        tile = jnp.where(lane < DEEP, pltpu.roll(side, LANES - FIRST, 1), tile)
    if j == count - 1:
        tile = jnp.where(lane >= LANES - DEEP, pltpu.roll(side, LANES - EDGE, 1), tile)
    return tile


def inner_first_kernel(f_in, c_in, f_ref, c_ref, v1_ref, w_ref, faces_ref, center_ref):
    own = list(range(f_ref.shape[0] - 1))
    rows = f_in.shape[0]
    clear_pads((f_ref, c_ref, v1_ref), own)
    for j in own:
        f_ref[j, PAD : PAD + rows] = f_in[:, tile_cols(j)]
        c_ref[j, PAD : PAD + rows] = c_in[:, tile_cols(j)]
    sweep(2, row_tiles(f_ref) - 2,
          lambda r: first_vector(f_ref, c_ref, v1_ref, w_ref, faces_ref, center_ref, r, own), 6)


def inner_rest_kernel(after, p_in, north_ref, south_ref, f_in, c_in, v1_in, w_in, faces_in, center_in,
                      f_ref, c_ref, v1_ref, w_ref, faces_ref, center_ref, p_ref, v2_ref, sums_ref):
    count = f_ref.shape[0] - 1
    own = list(range(count))
    rows = f_ref.shape[1]
    tiles = row_tiles(f_ref)
    has_north, has_south = neighbours_along("row")
    clear_pads((p_ref, v2_ref), own)
    lane = lanes()
    for j in own:
        p_ref[j, PAD : rows - PAD] = p_in[:, tile_cols(j)]
    for field, ref in enumerate((f_ref, c_ref, p_ref)):
        for j in own:
            ref[j, SUB : 2 * SUB] = halo_tile(north_ref, field, j, has_north)
            ref[j, rows - 2 * SUB : rows - SUB] = halo_tile(south_ref, field, j, has_south)
        for t in range(1, tiles + 1):
            at = slice(t * SUB, (t + 1) * SUB)
            last = pltpu.roll(ref[count - 1, at], EDGE, 1)
            first = pltpu.roll(ref[0, at], FIRST, 1)
            keep = (lane >= FIRST) & (lane < FIRST + EDGE)
            ref[count, at] = jnp.where(lane < EDGE, last, jnp.where(keep, first, 0.0))
    for start in (0, tiles - 2):
        sweep(start, start + 2,
              lambda r: first_vector(f_ref, c_ref, v1_ref, w_ref, faces_ref, center_ref, r, own))
    second_vector(v1_ref, v2_ref, w_ref, center_ref, [own])
    sums = own_products(f_ref, v1_ref, v2_ref, w_ref, center_ref, no_sums())
    for k, a in enumerate(sums):
        sums_ref[k] = a


def margin_kernel(west_ref, east_ref, sums_in, f_in, c_in, p_in, v1_in, v2_in, w_in, faces_in, center_in,
                  f_ref, c_ref, p_ref, v1_ref, v2_ref, w_ref, faces_ref, center_ref, row_ref):
    count = f_ref.shape[0] - 1
    tiles = row_tiles(f_ref)
    per, groups = packing(tiles)
    lane = lanes()
    has_west, has_east = neighbours_along("col")
    from_east = lax.rem(lane, 2 * WIDE) < WIDE
    halo = (lane >= EDGE) & (lane < FIRST)
    clear_pads((f_ref, c_ref, p_ref, v1_ref, v2_ref), [count])
    for field, ref in enumerate((f_ref, c_ref, p_ref)):
        for v in range(groups):
            src = slice((field * groups + v) * SUB, (field * groups + v + 1) * SUB)
            east = jnp.where(has_east, east_ref[src], 0.0)
            west = jnp.where(has_west, west_ref[src], 0.0)
            both = jnp.where(from_east, east, west)
            for g in range(min(per, tiles - v * per)):
                t = v * per + g
                at = slice(SUB + t * SUB, 2 * SUB + t * SUB)
                ref[count, at] = jnp.where(halo, pltpu.roll(both, (EDGE - 2 * WIDE * g) % LANES, 1), ref[count, at])
    sweep(0, tiles, lambda r: first_vector(
        f_ref, c_ref, v1_ref, w_ref, faces_ref, center_ref, r, [count]), 8)
    second_vector(v1_ref, v2_ref, w_ref, center_ref, [[count]], 8)
    sums = tuple(sums_in[k] for k in range(2 * len(PAIRS)))
    sums = margin_products(f_ref, v1_ref, v2_ref, w_ref, center_ref, sums)
    row_ref[...] = jnp.broadcast_to(pack_sums(sums)[None], row_ref.shape)


def density_kernel(rows_ref, f_ref, c_ref, p_ref, v1_ref, v2_ref, w_ref, faces_ref,
                   value_ref, u1_ref, u2_ref, row_ref, vx_ref, center_ref):
    dots, _unused = gathered_sums(rows_ref)
    c0, c1, c2 = [jnp.broadcast_to(c, (SUB, LANES)) for c in galerkin(dots)]
    which = list(range(f_ref.shape[0]))
    own = which[:-1]
    parts = [own, which[-1:]]
    tiles = row_tiles(f_ref)
    clear_pads((vx_ref, u1_ref, u2_ref), which)

    def value(r):
        at = pl.ds(r, SUB)
        return [
            (vx_ref, j, at, (c0 * f_ref[j, at, :] + c1 * v1_ref[j, at, :]) + c2 * v2_ref[j, at, :])
            for j in which
        ]

    sweep(0, tiles, value, 4)

    def first(r):
        at = pl.ds(r, SUB)
        val = beside_all(vx_ref, r, parts)
        cells = beside_all(p_ref, r, parts)
        out = []
        for j in which:
            inside = jnp.minimum(c_ref[j, at, :], 1.0)
            slope_row = 0.5 * (val[1][j] - val[2][j])
            slope_col = 0.5 * (val[3][j] - val[4][j])
            congestion = (slope_row * slope_row + slope_col * slope_col) * (0.5 / diffusion)
            zeroth = (discount_rate + congestion) * SCALE
            center = inside * zeroth + faces_ref[j, at, :]
            w = [w_ref[k, j, at, :] for k in range(4)]
            out.append((center_ref, j, at, center))
            out.append((u1_ref, j, at, weighted_apply(center, w, [x[j] for x in cells])))
        return out

    sweep(0, tiles, first, 8)

    def outer(t, sums):
        cost, weight = sums
        for u in range(8):
            at = pl.ds(pl.multiple_of(PAD + (8 * t + u) * SUB, SUB), SUB)
            to = pl.ds(pl.multiple_of((8 * t + u) * SUB, SUB), SUB)
            for j in own:
                v = with_sides(vx_ref[j, at, :], vx_ref[len(own), at, :], j, len(own))
                p = p_ref[j, at, :]
                value_ref[to, tile_cols(j)] = v
                cost = cost + p * (f_ref[j, at, :] - discount_rate * v)
                weight = weight + p
        return cost, weight

    zero = jnp.zeros((SUB, LANES), jnp.float32)
    extra = lax.fori_loop(0, (tiles - 2) // 8, outer, (zero, zero))
    second_vector(u1_ref, u2_ref, w_ref, center_ref, parts)
    sums = own_products(p_ref, u1_ref, u2_ref, w_ref, center_ref, no_sums())
    sums = margin_products(p_ref, u1_ref, u2_ref, w_ref, center_ref, sums)
    row_ref[...] = jnp.broadcast_to(pack_sums(sums, extra)[None], row_ref.shape)


def finish_kernel(rows_ref, p_ref, u1_ref, u2_ref, density_ref, ergodic_ref):
    dots, (cost, weight) = gathered_sums(rows_ref, 2)
    ergodic_ref[...] = cost / weight
    c0, c1, c2 = [jnp.broadcast_to(c, (SUB, LANES)) for c in galerkin(dots)]
    count = p_ref.shape[0] - 1

    def tile(t, _):
        for u in range(8):
            at = pl.ds(pl.multiple_of(PAD + (8 * t + u) * SUB, SUB), SUB)
            to = pl.ds(pl.multiple_of((8 * t + u) * SUB, SUB), SUB)
            made = [(c0 * p_ref[j, at, :] + c1 * u1_ref[j, at, :]) + c2 * u2_ref[j, at, :] for j in range(count + 1)]
            for j in range(count):
                density_ref[to, tile_cols(j)] = with_sides(made[j], made[count], j, count)
        return 0

    lax.fori_loop(0, density_ref.shape[0] // (8 * SUB), tile, 0)


def f32(*shape):
    return jax.ShapeDtypeStruct(shape, jnp.float32)


def exchange(back, ahead, axis):
    count = lax.axis_size(axis)
    after = lax.ppermute(back, axis, [((i + 1) % count, i) for i in range(count)])
    before = lax.ppermute(ahead, axis, [(i, (i + 1) % count) for i in range(count)])
    return before, after


def everyone(row):
    return lax.all_to_all(row, BOTH, 0, 0, tiled=True)


def body(*args):
    rows, cols = args[0].shape
    devices = lax.axis_size("row") * lax.axis_size("col")
    count = cols // LANES
    ext = f32(count + 1, rows + 2 * PAD, LANES)
    ext4 = f32(4, *ext.shape)
    everyones = f32(devices, 1, LANES)
    _per, groups = packing(rows // SUB + 2)
    small = pltpu.CompilerParams(vmem_limit_bytes=VMEM_BYTES)

    def call(kernel, ins, outs, scratch=0, **more):
        return pl.pallas_call(
            kernel,
            in_specs=[VM] * len(ins),
            out_specs=[VM] * len(outs),
            out_shape=outs,
            scratch_shapes=[pltpu.VMEM(ext.shape, jnp.float32)] * scratch,
            compiler_params=small,
            **more,
        )(*ins)

    cost = lambda us: pl.CostEstimate(flops=0, bytes_accessed=int(us * 2e6), transcendentals=0)
    up, down = [edge_rows(*[x[at] for x in args]) for at in (slice(0, SUB), slice(rows - SUB, rows))]
    north, south = exchange(up, down, "row")
    forcing, conduct = fields_of(*args[:3])
    prior = args[3]
    f, c, v1, w, faces, center = call(
        inner_first_kernel, (forcing, conduct), [ext] * 3 + [ext4, ext, ext], cost_estimate=cost(1.5))
    packs = call(
        pack_columns_kernel, (f, c, prior, north, south), [f32(3 * groups * SUB, LANES)] * 2)
    west, east = exchange(*packs, "col")
    f, c, v1, w, faces, center, p, v2, sums = call(
        inner_rest_kernel, (packs[0], prior, north, south, f, c, v1, w, faces, center),
        [ext] * 3 + [ext4] + [ext] * 4 + [f32(2 * len(PAIRS), SUB, LANES)],
        input_output_aliases={4 + k: k for k in range(6)}, cost_estimate=cost(4))
    f, c, p, v1, v2, w, faces, _center, row = call(
        margin_kernel, (west, east, sums, f, c, p, v1, v2, w, faces, center),
        [ext] * 5 + [ext4, ext, ext, everyones], input_output_aliases={3 + k: k for k in range(8)})
    value, u1, u2, row = call(
        density_kernel, (everyone(row), f, c, p, v1, v2, w, faces),
        [f32(rows, cols), ext, ext, everyones], 2)
    density, ergodic = call(finish_kernel, (everyone(row), p, u1, u2), [f32(rows, cols), f32(1, 1)])
    return value, density, ergodic[0, 0]


def solution(mesh):
    spec = P("row", "col")
    return jax.shard_map(body, mesh=mesh, in_specs=(spec,) * 4, out_specs=(spec, spec, P()), check_vma=False)
```

time: 51.9 us -> 44.6 us (0.86)
  Pallas kernels: 19 us -> 13.1 us
  blocking collectives: 21.5 us -> 20.4 us
    pallas_call x6, Pallas kernels: 19 us -> 13.1 us  [call(): pl.pallas_call(kernel, in_specs=[VM] * len(ins), out_specs=[VM] * len(out...]
    ppermute x2, starting transfers between devices: 0.55 us -> 2.52 us  [exchange(): lax.ppermute(ahead, axis, [(i, (i + 1) % count) for i in range(count)])]
    ppermute x2, starting transfers between devices: 7.09 us -> 5.12 us  [exchange(): lax.ppermute(back, axis, [((i + 1) % count, i) for i in range(count)])]
    all_to_all x2, blocking collectives: 21.5 us -> 20.4 us  [everyone(): return lax.all_to_all(row, BOTH, 0, 0, tiled=True)]
  transfers between devices with their start and end apart: 4 -> 4, of which waited for: 2 -> 1; matrix products, arithmetic and copies ran while one was open for 3% -> 3% of each run, Pallas kernels for 11% -> 9%
where the time goes in v3:
time: 44.6 us; the launch traced here: 44.4 us
  blocking collectives  20.4 us (46%)
  Pallas kernels  13.1 us (29%)
  starting transfers between devices  7.64 us (17%)
  other arithmetic  2.46 us (6%)
  between operations  0.72 us (2%)
    all_to_all x2, blocking collectives, everyone(): return lax.all_to_all(row, BOTH, 0, 0, tiled=True)  20.4 us
    pallas_call x6, Pallas kernels, call(): pl.pallas_call(kernel, in_specs=[VM] * len(ins), out_specs=[VM] * len(out...  13.1 us
    ppermute x2, starting transfers between devices, exchange(): lax.ppermute(back, axis, [((i + 1) % count, i) for i in range(count)])  5.12 us
    ppermute x2, starting transfers between devices, exchange(): lax.ppermute(ahead, axis, [(i, (i + 1) % count) for i in range(count)])  2.52 us
    add x2, other arithmetic, fields_of(): return (rc + control_cost, 1.0 + control_cost)  2.45 us
  transfers between devices with their start and end apart: 4, of which 1 were waited for; matrix products, arithmetic and copies ran while one was open for 3% of the time, Pallas kernels for 9%

profile of v3, /device:TPU:0, one launch (start us, length us, event | category | flops | bytes accessed | tf_op | source)
XLA Modules:
  0.0 44.4 jit_solution(4936461170045340090)
XLA Ops:
  0.6 0.0 copy-start
  0.6 0.9 %slice_add_fusion = (f32[8,512]{1,0:T(8,128)S(1)}, f32[8,512]{1,0:T(8,128)S(1)}, f32[8,512]{1,0:T(8,128)S(1)}, f32[8,512]{1,0:T(8,128)S(1)}, f32[8,512]{1,0:T(8,128)S(1)}, /*index=5*/f32[8,512]{1,0:T(8,128)S(1)}) fusion(f32[256,512]{1,0:T(8,128)} %param.4, f32[256,512]{1,0:T(8,128)} %param.6, f32[256,512]{1,0:T(8,128)} %param.5, f32[256,512]{1,0:T(8,128)} %p_in.1), kind=kLoop, calls=%fused_computation.6 | loop fusion | flops 49152 | bytes 229376 | tf_op jit(solution)/shard_map/add | solution.py:162
  1.6 0.5 %collective-permute-start = (f32[24,512]{1,0:T(8,128)S(1)}, f32[24,512]{1,0:T(8,128)S(1)}, u32[]{:S(2)}, u32[]{:S(2)}) collective-permute-start(f32[24,512]{1,0:T(8,128)S(1)} %pad_maximum_fusion), channel_id=1, source_target_pairs={{0,4},{4,8},{8,12},{12,16},{16,20},{20,24},{24,28},{28,0},{1,5},{5... | collective-permute-start | bytes 147464 | tf_op jit(solution)/shard_map/ppermute | solution.py:531
  2.1 4.1 %collective-permute-start.1 = (f32[24,512]{1,0:T(8,128)S(1)}, f32[24,512]{1,0:T(8,128)S(1)}, u32[]{:S(2)}, u32[]{:S(2)}) collective-permute-start(f32[24,512]{1,0:T(8,128)S(1)} %pad_maximum_fusion.1), channel_id=1, source_target_pairs={{4,0},{8,4},{12,8},{16,12},{20,16},{24,20},{28,24},{0,28},{5,1},{9... | collective-permute-start | bytes 147464 | tf_op jit(solution)/shard_map/ppermute | solution.py:530
  6.2 1.5 %broadcast_add_fusion = (f32[256,512]{1,0:T(8,128)S(1)}, f32[256,512]{1,0:T(8,128)S(1)}) fusion(f32[256,512]{1,0:T(8,128)} %param.6, f32[256,512]{1,0:T(8,128)} %param.5, f32[256,512]{1,0:T(8,128)} %param.4), kind=kLoop, calls=%fused_computation.1 | loop fusion | flops 786432 | bytes 2621440 | tf_op jit(solution)/shard_map/add | solution.py:162
  7.8 1.0 %shard_map.67 = (f32[5,288,128]{2,1,0:T(8,128)S(1)}, f32[5,288,128]{2,1,0:T(8,128)S(1)}, f32[5,288,128]{2,1,0:T(8,128)S(1)}, f32[4,5,288,128]{3,2,1,0:T(8,128)S(...) custom-call(f32[256,512]{1,0:T(8,128)S(1)} %get-tuple-element.70.f_in, f32[256,512]{1,0:T(8,128)S(1)} %get-tuple-element.69.c_in), custom_call_target="tpu_custom_call" | custom-call | bytes 3000000 | tf_op jit(solution)/shard_map/pallas_call | solution.py:550
  8.8 0.0 collective-permute-done.north_ref
  8.8 0.0 collective-permute-done.1.south_ref
  8.8 0.0 copy-done
  8.8 0.3 shard_map.68
  9.1 2.0 %collective-permute-start.2 = (f32[96,128]{1,0:T(8,128)S(1)}, f32[96,128]{1,0:T(8,128)S(1)}, u32[]{:S(2)}, u32[]{:S(2)}) collective-permute-start(f32[96,128]{1,0:T(8,128)S(1)} %get-tuple-element.36), channel_id=1, source_target_pairs={{0,1},{1,2},{2,3},{3,0},{4,5},{5,6},{6,7},{7,4},{8,9},{9,10},{10,1... | collective-permute-start | bytes 147464 | tf_op jit(solution)/shard_map/ppermute | solution.py:531
  11.1 1.0 %collective-permute-start.3 = (f32[96,128]{1,0:T(8,128)S(1)}, f32[96,128]{1,0:T(8,128)S(1)}, u32[]{:S(2)}, u32[]{:S(2)}) collective-permute-start(f32[96,128]{1,0:T(8,128)S(1)} %get-tuple-element.37.after), channel_id=1, source_target_pairs={{1,0},{2,1},{3,2},{0,3},{5,4},{6,5},{7,6},{4,7},{9,8},{10,9},{11,1... | collective-permute-start | bytes 147464 | tf_op jit(solution)/shard_map/ppermute | solution.py:530
  12.1 2.9 %shard_map.69 = (f32[5,288,128]{2,1,0:T(8,128)S(1)}, f32[5,288,128]{2,1,0:T(8,128)S(1)}, f32[5,288,128]{2,1,0:T(8,128)S(1)}, f32[4,5,288,128]{3,2,1,0:T(8,128)S(...) custom-call(f32[96,128]{1,0:T(8,128)S(1)} %get-tuple-element.37.afte, ...), custom_call_target="tpu_custom_call", output_to_operand_aliasing={{0}: (4, {}), {1}: (5, {}), {2}: (6, {}), {3}: (7, {}), {4}... | custom-call | bytes 8000000 | tf_op jit(solution)/shard_map/pallas_call | solution.py:550
  15.1 0.0 collective-permute-done.2.west_ref
  15.1 0.1 collective-permute-done.3.east_ref
  15.2 1.5 %shard_map.70 = (f32[5,288,128]{2,1,0:T(8,128)S(1)}, f32[5,288,128]{2,1,0:T(8,128)S(1)}, f32[5,288,128]{2,1,0:T(8,128)S(1)}, f32[5,288,128]{2,1,0:T(8,128)S(1)},...) custom-call(f32[96,128]{1,0:T(8,128)S(1)} %collective-permute-done.2, ...), custom_call_target="tpu_custom_call", output_to_operand_aliasing={{0}: (3, {}), {1}: (4, {}), {2}: (5, {}), {3}: (6, {}), {4}... | custom-call | tf_op jit(solution)/shard_map/pallas_call | solution.py:550
  16.7 11.5 %all_to_all.10.rows_ref = f32[32,1,128]{2,1,0:T(1,128)S(1)} all-to-all(f32[32,1,128]{2,1,0:T(1,128)S(1)} %get-tuple-element.51), channel_id=1, replica_groups=mesh['row'=8,'col'=4] {'row','col'}, dimensions={0} | all-to-all | bytes 32768 | tf_op jit(solution)/shard_map/all_to_all | solution.py:536
  28.2 5.8 %shard_map.71 = (f32[256,512]{1,0:T(8,128)}, f32[5,288,128]{2,1,0:T(8,128)S(1)}, f32[5,288,128]{2,1,0:T(8,128)S(1)}, f32[32,1,128]{2,1,0:T(1,128)S(1)}) custom-call(f32[32,1,128]{2,1,0:T(1,128)S(1)} %all_to_all.10.rows_ref, f32[5,288,128]{2,1,0:T(8,128)S(1)} %get-tuple-element.52.f_ref, f32[5,288,128]{2,1,0:T(8,128)S(1)} %get-tuple-element.53.c_ref, ...), custom_call_target="tpu_custom_call" | custom-call | tf_op jit(solution)/shard_map/pallas_call | solution.py:550
  34.0 8.9 %all_to_all.11.rows_ref = f32[32,1,128]{2,1,0:T(1,128)S(1)} all-to-all(f32[32,1,128]{2,1,0:T(1,128)S(1)} %get-tuple-element.60), channel_id=1, replica_groups=mesh['row'=8,'col'=4] {'row','col'}, dimensions={0} | all-to-all | bytes 32768 | tf_op jit(solution)/shard_map/all_to_all | solution.py:536
  42.9 1.5 %shard_map.72 = (f32[256,512]{1,0:T(8,128)}, f32[1,1]{1,0:T(1,128)}) custom-call(f32[32,1,128]{2,1,0:T(1,128)S(1)} %all_to_all.11.rows_ref, f32[5,288,128]{2,1,0:T(8,128)S(1)} %get-tuple-element.54.p_ref, f32[5,288,128]{2,1,0:T(8,128)S(1)} %get-tuple-element.61.u1_ref, f32[5,288,128]{2,1,0:T(8,128)S(1)} %get-tuple-element.62.u2_ref), custom_call_target="tpu_custom_call" | custom-call | tf_op jit(solution)/shard_map/pallas_call | solution.py:550
  (2 shorter events, 0.0 us)
Async XLA Ops:
  0.6 8.2 %copy-start = (f32[256,512]{1,0:T(8,128)S(1)}, f32[256,512]{1,0:T(8,128)}, u32[]{:S(2)}) copy-start(f32[256,512]{1,0:T(8,128)} %p_in.1) | copy-start | bytes 1572868
  1.6 7.2 %collective-permute-start = (f32[24,512]{1,0:T(8,128)S(1)}, f32[24,512]{1,0:T(8,128)S(1)}, u32[]{:S(2)}, u32[]{:S(2)}) collective-permute-start(f32[24,512]{1,0:T(8,128)S(1)} %pad_maximum_fusion), channel_id=1, source_target_pairs={{0,4},{4,8},{8,12},{12,16},{16,20},{20,24},{24,28},{28,0},{1,5},{5... | collective-permute-start | bytes 147464 | tf_op jit(solution)/shard_map/ppermute | solution.py:531
  2.1 6.7 %collective-permute-start.1 = (f32[24,512]{1,0:T(8,128)S(1)}, f32[24,512]{1,0:T(8,128)S(1)}, u32[]{:S(2)}, u32[]{:S(2)}) collective-permute-start(f32[24,512]{1,0:T(8,128)S(1)} %pad_maximum_fusion.1), channel_id=1, source_target_pairs={{4,0},{8,4},{12,8},{16,12},{20,16},{24,20},{28,24},{0,28},{5,1},{9... | collective-permute-start | bytes 147464 | tf_op jit(solution)/shard_map/ppermute | solution.py:530
  9.1 5.9 %collective-permute-start.2 = (f32[96,128]{1,0:T(8,128)S(1)}, f32[96,128]{1,0:T(8,128)S(1)}, u32[]{:S(2)}, u32[]{:S(2)}) collective-permute-start(f32[96,128]{1,0:T(8,128)S(1)} %get-tuple-element.36), channel_id=1, source_target_pairs={{0,1},{1,2},{2,3},{3,0},{4,5},{5,6},{6,7},{7,4},{8,9},{9,10},{10,1... | collective-permute-start | bytes 147464 | tf_op jit(solution)/shard_map/ppermute | solution.py:531
  11.1 4.1 %collective-permute-start.3 = (f32[96,128]{1,0:T(8,128)S(1)}, f32[96,128]{1,0:T(8,128)S(1)}, u32[]{:S(2)}, u32[]{:S(2)}) collective-permute-start(f32[96,128]{1,0:T(8,128)S(1)} %get-tuple-element.37.after), channel_id=1, source_target_pairs={{1,0},{2,1},{3,2},{0,3},{5,4},{6,5},{7,6},{4,7},{9,8},{10,9},{11,1... | collective-permute-start | bytes 147464 | tf_op jit(solution)/shard_map/ppermute | solution.py:530

commit v4 on v3

--- a/solution.py
+++ b/solution.py
@@ -13,7 +13,7 @@
 FACE = diffusion * 0.5 * SCALE
 LANES = 128
 SUB = 8
-WIDE = 7
+WIDE = 5
 EDGE = 10
 DEEP = 5
 PAD = 2 * SUB
@@ -163,7 +163,13 @@
 
 
 def edge_rows(rc, cx, cy, pd):
-    return jnp.concatenate([*fields_of(rc, cx, cy), pd])
+    rows, cols = rc.shape
+    few = WIDE - 2
+    gap = jnp.zeros((2 * SUB - 2 * WIDE - few, cols), jnp.float32)
+    ends = [[x[:SUB] for x in (rc, cx, cy, pd)], [x[rows - SUB :] for x in (rc, cx, cy, pd)]]
+    (f, c, p), (g, d, q) = lax.optimization_barrier([(*fields_of(*x[:3]), x[3]) for x in ends])
+    up = jnp.concatenate([p[:few], f[:WIDE], c[:WIDE], gap])
+    return up, jnp.concatenate([gap, d[SUB - WIDE :], g[SUB - WIDE :], q[SUB - few :]])
 
 
 def neighbours_along(axis):
@@ -171,6 +177,10 @@
     return i > 0, i < lax.axis_size(axis) - 1
 
 
+def is_even(axis):
+    return lax.rem(lax.axis_index(axis), 2) == 0
+
+
 def lanes():
     return lax.broadcasted_iota(jnp.int32, (SUB, LANES), 1)
 
@@ -179,8 +189,11 @@
     return slice(j * LANES, (j + 1) * LANES)
 
 
-def halo_tile(ref, field, j, present):
-    return jnp.where(present, ref[field * SUB : (field + 1) * SUB, tile_cols(j)], 0.0)
+def halo_tile(refs, field, j, south):
+    at = ((3, 8, 0) if south else (5, 0, 8))[field]
+    first, second = [ref[at : at + SUB, tile_cols(j)] for ref in refs]
+    tile = jnp.where(is_even("row"), first, second) if south else jnp.where(is_even("row"), second, first)
+    return jnp.where(neighbours_along("row")[int(south)], tile, 0.0)
 
 
 def packing(tiles):
@@ -188,22 +201,20 @@
     return per, -(-tiles // per)
 
 
-def pack_columns_kernel(f_ref, c_ref, p_ref, north_ref, south_ref, west_ref, east_ref):
+def pack_columns_kernel(f_ref, c_ref, p_ref, near_ref, far_ref, first_ref, second_ref):
     tiles = row_tiles(f_ref)
     per, groups = packing(tiles)
-    end = p_ref.shape[1] // LANES - 1
+    end = p_ref.shape[0] - 2
     lane = lanes()
-    has_north, has_south = neighbours_along("row")
+    even = is_even("col")
     for field in range(3):
 
         def tile(j, t):
             if t == 0:
-                return halo_tile(north_ref, field, j, has_north)
+                return halo_tile((near_ref, far_ref), field, j, False)
             if t == tiles - 1:
-                return halo_tile(south_ref, field, j, has_south)
-            if field == 2:
-                return p_ref[(t - 1) * SUB : t * SUB, tile_cols(j)]
-            return (f_ref, c_ref)[field][j, (t + 1) * SUB : (t + 2) * SUB]
+                return halo_tile((near_ref, far_ref), field, j, True)
+            return (f_ref, c_ref, p_ref)[field][j, (t + 1) * SUB : (t + 2) * SUB]
 
         for v in range(groups):
             west = jnp.zeros((SUB, LANES), jnp.float32)
@@ -215,8 +226,8 @@
                 there = (lane >= at + WIDE) & (lane < at + 2 * WIDE)
                 east = jnp.where(there, pltpu.roll(b, (at + 2 * WIDE) % LANES, 1), east)
             at = (field * groups + v) * SUB
-            west_ref[at : at + SUB] = west
-            east_ref[at : at + SUB] = east
+            first_ref[at : at + SUB] = jnp.where(even, east, west)
+            second_ref[at : at + SUB] = jnp.where(even, west, east)
 
 
 def beside(ref, r, which):
@@ -305,12 +316,12 @@
         group([SUB + t * SUB for t in rest])
 
 
-def second_vector(v1_ref, v2_ref, w_ref, center_ref, parts, unroll=8):
+def second_vector(v1_ref, v2_ref, w_ref, center_ref, parts, unroll=17, start=0, stop=None):
     def step(r):
         out, _here = apply_tiles(v1_ref, w_ref, center_ref, r, parts)
         return [(v2_ref, j, pl.ds(r, SUB), x) for j, x in out.items()]
 
-    sweep(0, row_tiles(v1_ref), step, unroll)
+    sweep(start, row_tiles(v1_ref) if stop is None else stop, step, unroll)
 
 
 def no_sums():
@@ -375,62 +386,70 @@
     return tile
 
 
-def inner_first_kernel(f_in, c_in, f_ref, c_ref, v1_ref, w_ref, faces_ref, center_ref):
+def repeat_sides(ref, t):
+    count = ref.shape[0] - 1
+    lane = lanes()
+    at = slice((t + 1) * SUB, (t + 2) * SUB)
+    last = pltpu.roll(ref[count - 1, at], EDGE, 1)
+    first = pltpu.roll(ref[0, at], FIRST, 1)
+    keep = (lane >= FIRST) & (lane < FIRST + EDGE)
+    ref[count, at] = jnp.where(lane < EDGE, last, jnp.where(keep, first, 0.0))
+
+
+def inner_first_kernel(f_in, c_in, p_in,
+                       f_ref, c_ref, p_ref, v1_ref, v2_ref, w_ref, faces_ref, center_ref):
     own = list(range(f_ref.shape[0] - 1))
     rows = f_in.shape[0]
-    clear_pads((f_ref, c_ref, v1_ref), own)
-    for j in own:
-        f_ref[j, PAD : PAD + rows] = f_in[:, tile_cols(j)]
-        c_ref[j, PAD : PAD + rows] = c_in[:, tile_cols(j)]
-    sweep(2, row_tiles(f_ref) - 2,
+    tiles = row_tiles(f_ref)
+    clear_pads((f_ref, c_ref, p_ref, v1_ref, v2_ref), own)
+    for ref, source in ((f_ref, f_in), (c_ref, c_in), (p_ref, p_in)):
+        for j in own:
+            ref[j, PAD : PAD + rows] = source[:, tile_cols(j)]
+        for t in range(1, tiles - 1):
+            repeat_sides(ref, t)
+    sweep(2, tiles - 2,
           lambda r: first_vector(f_ref, c_ref, v1_ref, w_ref, faces_ref, center_ref, r, own), 6)
-
-
-def inner_rest_kernel(after, p_in, north_ref, south_ref, f_in, c_in, v1_in, w_in, faces_in, center_in,
-                      f_ref, c_ref, v1_ref, w_ref, faces_ref, center_ref, p_ref, v2_ref, sums_ref):
-    count = f_ref.shape[0] - 1
-    own = list(range(count))
+    second_vector(v1_ref, v2_ref, w_ref, center_ref, [own], 7, 3, tiles - 3)
+
+
+def inner_rest_kernel(after, near_ref, far_ref, f_in, c_in, p_in, v1_in, v2_in, w_in, faces_in, center_in,
+                      f_ref, c_ref, p_ref, v1_ref, v2_ref, w_ref, faces_ref, center_ref, sums_ref):
+    own = list(range(f_ref.shape[0] - 1))
     rows = f_ref.shape[1]
     tiles = row_tiles(f_ref)
-    has_north, has_south = neighbours_along("row")
-    clear_pads((p_ref, v2_ref), own)
-    lane = lanes()
-    for j in own:
-        p_ref[j, PAD : rows - PAD] = p_in[:, tile_cols(j)]
     for field, ref in enumerate((f_ref, c_ref, p_ref)):
         for j in own:
-            ref[j, SUB : 2 * SUB] = halo_tile(north_ref, field, j, has_north)
-            ref[j, rows - 2 * SUB : rows - SUB] = halo_tile(south_ref, field, j, has_south)
-        for t in range(1, tiles + 1):
-            at = slice(t * SUB, (t + 1) * SUB)
-            last = pltpu.roll(ref[count - 1, at], EDGE, 1)
-            first = pltpu.roll(ref[0, at], FIRST, 1)
-            keep = (lane >= FIRST) & (lane < FIRST + EDGE)
-            ref[count, at] = jnp.where(lane < EDGE, last, jnp.where(keep, first, 0.0))
+            ref[j, SUB : 2 * SUB] = halo_tile((near_ref, far_ref), field, j, False)
+            ref[j, rows - 2 * SUB : rows - SUB] = halo_tile((near_ref, far_ref), field, j, True)
+        repeat_sides(ref, 0)
+        repeat_sides(ref, tiles - 1)
     for start in (0, tiles - 2):
         sweep(start, start + 2,
               lambda r: first_vector(f_ref, c_ref, v1_ref, w_ref, faces_ref, center_ref, r, own))
-    second_vector(v1_ref, v2_ref, w_ref, center_ref, [own])
+    for start in (0, tiles - 3):
+        second_vector(v1_ref, v2_ref, w_ref, center_ref, [own], 3, start, start + 3)
     sums = own_products(f_ref, v1_ref, v2_ref, w_ref, center_ref, no_sums())
     for k, a in enumerate(sums):
         sums_ref[k] = a
 
 
-def margin_kernel(west_ref, east_ref, sums_in, f_in, c_in, p_in, v1_in, v2_in, w_in, faces_in, center_in,
+def margin_kernel(near_ref, far_ref, sums_in, f_in, c_in, p_in, v1_in, v2_in, w_in, faces_in, center_in,
                   f_ref, c_ref, p_ref, v1_ref, v2_ref, w_ref, faces_ref, center_ref, row_ref):
     count = f_ref.shape[0] - 1
     tiles = row_tiles(f_ref)
     per, groups = packing(tiles)
     lane = lanes()
     has_west, has_east = neighbours_along("col")
+    even = is_even("col")
     from_east = lax.rem(lane, 2 * WIDE) < WIDE
     halo = (lane >= EDGE) & (lane < FIRST)
     clear_pads((f_ref, c_ref, p_ref, v1_ref, v2_ref), [count])
     for field, ref in enumerate((f_ref, c_ref, p_ref)):
         for v in range(groups):
             src = slice((field * groups + v) * SUB, (field * groups + v + 1) * SUB)
-            east = jnp.where(has_east, east_ref[src], 0.0)
-            west = jnp.where(has_west, west_ref[src], 0.0)
+            near, far = near_ref[src], far_ref[src]
+            east = jnp.where(has_east, jnp.where(even, near, far), 0.0)
+            west = jnp.where(has_west, jnp.where(even, far, near), 0.0)
             both = jnp.where(from_east, east, west)
             for g in range(min(per, tiles - v * per)):
                 t = v * per + g
@@ -445,7 +464,7 @@
 
 
 def density_kernel(rows_ref, f_ref, c_ref, p_ref, v1_ref, v2_ref, w_ref, faces_ref,
-                   value_ref, u1_ref, u2_ref, row_ref, vx_ref, center_ref):
+                   value_out, u1_ref, u2_ref, row_ref, vx_ref, center_ref, value_ref, sem):
     dots, _unused = gathered_sums(rows_ref)
     c0, c1, c2 = [jnp.broadcast_to(c, (SUB, LANES)) for c in galerkin(dots)]
     which = list(range(f_ref.shape[0]))
@@ -480,10 +499,10 @@
             out.append((u1_ref, j, at, weighted_apply(center, w, [x[j] for x in cells])))
         return out
 
-    sweep(0, tiles, first, 8)
+    sweep(0, tiles, first, 17)
 
     def outer(t, sums):
-        cost, weight = sums
+        cost, weight = [list(x) for x in sums]
         for u in range(8):
             at = pl.ds(pl.multiple_of(PAD + (8 * t + u) * SUB, SUB), SUB)
             to = pl.ds(pl.multiple_of((8 * t + u) * SUB, SUB), SUB)
@@ -491,16 +510,19 @@
                 v = with_sides(vx_ref[j, at, :], vx_ref[len(own), at, :], j, len(own))
                 p = p_ref[j, at, :]
                 value_ref[to, tile_cols(j)] = v
-                cost = cost + p * (f_ref[j, at, :] - discount_rate * v)
-                weight = weight + p
-        return cost, weight
-
-    zero = jnp.zeros((SUB, LANES), jnp.float32)
-    extra = lax.fori_loop(0, (tiles - 2) // 8, outer, (zero, zero))
+                cost[j] = cost[j] + p * (f_ref[j, at, :] - discount_rate * v)
+                weight[j] = weight[j] + p
+        return tuple(cost), tuple(weight)
+
+    zeros = (jnp.zeros((SUB, LANES), jnp.float32),) * len(own)
+    extra = [sum(x) for x in lax.fori_loop(0, (tiles - 2) // 8, outer, (zeros, zeros))]
+    copy = pltpu.make_async_copy(value_ref, value_out, sem)
+    copy.start()
     second_vector(u1_ref, u2_ref, w_ref, center_ref, parts)
     sums = own_products(p_ref, u1_ref, u2_ref, w_ref, center_ref, no_sums())
     sums = margin_products(p_ref, u1_ref, u2_ref, w_ref, center_ref, sums)
     row_ref[...] = jnp.broadcast_to(pack_sums(sums, extra)[None], row_ref.shape)
+    copy.wait()
 
 
 def finish_kernel(rows_ref, p_ref, u1_ref, u2_ref, density_ref, ergodic_ref):
@@ -509,27 +531,30 @@
     c0, c1, c2 = [jnp.broadcast_to(c, (SUB, LANES)) for c in galerkin(dots)]
     count = p_ref.shape[0] - 1
 
-    def tile(t, _):
-        for u in range(8):
-            at = pl.ds(pl.multiple_of(PAD + (8 * t + u) * SUB, SUB), SUB)
-            to = pl.ds(pl.multiple_of((8 * t + u) * SUB, SUB), SUB)
+    unroll = 8
+
+    def some(t, _):
+        for u in range(unroll):
+            at = pl.ds(pl.multiple_of(PAD + (unroll * t + u) * SUB, SUB), SUB)
+            to = pl.ds(pl.multiple_of((unroll * t + u) * SUB, SUB), SUB)
             made = [(c0 * p_ref[j, at, :] + c1 * u1_ref[j, at, :]) + c2 * u2_ref[j, at, :] for j in range(count + 1)]
             for j in range(count):
                 density_ref[to, tile_cols(j)] = with_sides(made[j], made[count], j, count)
         return 0
 
-    lax.fori_loop(0, density_ref.shape[0] // (8 * SUB), tile, 0)
+    lax.fori_loop(0, density_ref.shape[0] // (unroll * SUB), some, 0)
 
 
 def f32(*shape):
     return jax.ShapeDtypeStruct(shape, jnp.float32)
 
 
-def exchange(back, ahead, axis):
-    count = lax.axis_size(axis)
-    after = lax.ppermute(back, axis, [((i + 1) % count, i) for i in range(count)])
-    before = lax.ppermute(ahead, axis, [(i, (i + 1) % count) for i in range(count)])
-    return before, after
+def exchange(near, far, axis):
+    n = lax.axis_size(axis)
+    assert n % 2 == 0
+    near = lax.ppermute(near, axis, [(i, i ^ 1) for i in range(n)])
+    far = lax.ppermute(far, axis, [(i, (((i + 1) % n ^ 1) - 1) % n) for i in range(n)])
+    return near, far
 
 
 def everyone(row):
@@ -546,38 +571,42 @@
     _per, groups = packing(rows // SUB + 2)
     small = pltpu.CompilerParams(vmem_limit_bytes=VMEM_BYTES)
 
-    def call(kernel, ins, outs, scratch=0, **more):
+    def call(kernel, ins, outs, scratch=(), to_hbm=0, **more):
         return pl.pallas_call(
             kernel,
             in_specs=[VM] * len(ins),
-            out_specs=[VM] * len(outs),
+            out_specs=[pl.BlockSpec(memory_space=pltpu.HBM)] * to_hbm + [VM] * (len(outs) - to_hbm),
             out_shape=outs,
-            scratch_shapes=[pltpu.VMEM(ext.shape, jnp.float32)] * scratch,
+            scratch_shapes=scratch,
             compiler_params=small,
             **more,
         )(*ins)
 
     cost = lambda us: pl.CostEstimate(flops=0, bytes_accessed=int(us * 2e6), transcendentals=0)
-    up, down = [edge_rows(*[x[at] for x in args]) for at in (slice(0, SUB), slice(rows - SUB, rows))]
-    north, south = exchange(up, down, "row")
+    up, down = edge_rows(*args)
+    even = is_even("row")
+    near, far = exchange(jnp.where(even, down, up), jnp.where(even, up, down), "row")
     forcing, conduct = fields_of(*args[:3])
     prior = args[3]
-    f, c, v1, w, faces, center = call(
-        inner_first_kernel, (forcing, conduct), [ext] * 3 + [ext4, ext, ext], cost_estimate=cost(1.5))
-    packs = call(
-        pack_columns_kernel, (f, c, prior, north, south), [f32(3 * groups * SUB, LANES)] * 2)
-    west, east = exchange(*packs, "col")
-    f, c, v1, w, faces, center, p, v2, sums = call(
-        inner_rest_kernel, (packs[0], prior, north, south, f, c, v1, w, faces, center),
-        [ext] * 3 + [ext4] + [ext] * 4 + [f32(2 * len(PAIRS), SUB, LANES)],
-        input_output_aliases={4 + k: k for k in range(6)}, cost_estimate=cost(4))
+    state = call(
+        inner_first_kernel, (forcing, conduct, prior),
+        [ext] * 5 + [ext4, ext, ext], cost_estimate=cost(1.5))
+    packs = call(pack_columns_kernel, (*state[:3], near, far), [f32(3 * groups * SUB, LANES)] * 2)
+    sides = exchange(*packs, "col")
+    *state, sums = call(
+        inner_rest_kernel, (packs[0], near, far, *state),
+        [ext] * 5 + [ext4, ext, ext, f32(2 * len(PAIRS), SUB, LANES)],
+        input_output_aliases={3 + k: k for k in range(8)}, cost_estimate=cost(4))
     f, c, p, v1, v2, w, faces, _center, row = call(
-        margin_kernel, (west, east, sums, f, c, p, v1, v2, w, faces, center),
+        margin_kernel, (*sides, sums, *state),
         [ext] * 5 + [ext4, ext, ext, everyones], input_output_aliases={3 + k: k for k in range(8)})
+    vmem = lambda like: pltpu.VMEM(like.shape, jnp.float32)
+    block = f32(rows, cols)
     value, u1, u2, row = call(
-        density_kernel, (everyone(row), f, c, p, v1, v2, w, faces),
-        [f32(rows, cols), ext, ext, everyones], 2)
-    density, ergodic = call(finish_kernel, (everyone(row), p, u1, u2), [f32(rows, cols), f32(1, 1)])
+        density_kernel, (everyone(row), f, c, p, v1, v2, w, faces), [block, ext, ext, everyones],
+        [vmem(ext), vmem(ext), vmem(block), pltpu.SemaphoreType.DMA], 1)
+    density, ergodic = call(
+        finish_kernel, (everyone(row), p, u1, u2), [block, f32(1, 1)])
     return value, density, ergodic[0, 0]
 
 

time: 44.6 us -> 42.3 us (0.948)
  blocking collectives: 20.4 us -> 17.8 us
  waiting for transfers between devices: 0.12 us -> 1.25 us
  Pallas kernels: 13.1 us -> 12.1 us
    all_to_all x2, blocking collectives: 20.4 us -> 17.8 us  [everyone(): return lax.all_to_all(row, BOTH, 0, 0, tiled=True)]
    ppermute x4, waiting for transfers between devices: 0.12 us -> 1.25 us  [the longest x2 1.25 us: exchange(): near = lax.ppermute(near, axis, [(i, i ^ 1) for i in range(n)])]
    pallas_call x6, Pallas kernels: 13.1 us -> 12.1 us  [call(): pl.pallas_call(kernel, in_specs=[VM] * len(ins), out_specs=[pl.BlockSpec(...]
  transfers between devices with their start and end apart: 4 -> 4, of which waited for: 1 -> 1; matrix products, arithmetic and copies ran while one was open for 3% -> 4% of each run, Pallas kernels for 9% -> 9%
where the time goes in v4:
time: 42.3 us; the launch traced here: 42.1 us
  blocking collectives  17.8 us (42%)
  Pallas kernels  12.1 us (29%)
  starting transfers between devices  7.63 us (18%)
  other arithmetic  2.47 us (6%)
  waiting for transfers between devices  1.25 us (3%)
  between operations  0.78 us (2%)
    all_to_all x2, blocking collectives, everyone(): return lax.all_to_all(row, BOTH, 0, 0, tiled=True)  17.8 us
    pallas_call x6, Pallas kernels, call(): pl.pallas_call(kernel, in_specs=[VM] * len(ins), out_specs=[pl.BlockSpec(...  12.1 us
    ppermute x2, starting transfers between devices, exchange(): lax.ppermute(far, axis, [(i, (((i + 1) % n ^ 1) - 1) % n) for i in range(...  7.09 us
    add x2, other arithmetic, fields_of(): return (rc + control_cost, 1.0 + control_cost)  2.44 us
    ppermute x2, waiting for transfers between devices, exchange(): near = lax.ppermute(near, axis, [(i, i ^ 1) for i in range(n)])  1.25 us
  transfers between devices with their start and end apart: 4, of which 1 were waited for; matrix products, arithmetic and copies ran while one was open for 4% of the time, Pallas kernels for 9%

profile of v4, /device:TPU:0, one launch (start us, length us, event | category | flops | bytes accessed | tf_op | source)
XLA Modules:
  0.0 42.1 jit_solution(8511874565071486372)
XLA Ops:
  0.6 0.0 copy-start
  0.6 0.9 %broadcast_add_fusion.1 = (f32[8,512]{1,0:T(8,128)S(1)}, f32[8,512]{1,0:T(8,128)S(1)}, f32[8,512]{1,0:T(8,128)S(1)}, f32[8,512]{1,0:T(8,128)S(1)}, f32[8,512]{1,0:T(8,128)S(1)}, /*index=5*/f32[8,512]{1,0:T(8,128)S(1)}) fusion(f32[256,512]{1,0:T(8,128)} %param.6, f32[256,512]{1,0:T(8,128)} %param.5, f32[256,512]{1,0:T(8,128)} %param.4, f32[256,512]{1,0:T(8,128)} %p_in.1), kind=kLoop, calls=%fused_computation.11 | loop fusion | flops 49152 | bytes 229376 | tf_op jit(solution)/shard_map/add | solution.py:162
  1.6 4.6 %collective-permute-start.1 = (f32[16,512]{1,0:T(8,128)S(1)}, f32[16,512]{1,0:T(8,128)S(1)}, u32[]{:S(2)}, u32[]{:S(2)}) collective-permute-start(f32[16,512]{1,0:T(8,128)S(1)} %get-tuple-element.91), channel_id=1, source_target_pairs={{0,28},{4,8},{8,4},{12,16},{16,12},{20,24},{24,20},{28,0},{1,29},{... | collective-permute-start | bytes 98312 | tf_op jit(solution)/shard_map/ppermute | solution.py:556
  6.2 0.0 collective-permute-start
  6.2 1.5 %broadcast_add_fusion = (f32[256,512]{1,0:T(8,128)S(1)}, f32[256,512]{1,0:T(8,128)S(1)}) fusion(f32[256,512]{1,0:T(8,128)} %param.6, f32[256,512]{1,0:T(8,128)} %param.5, f32[256,512]{1,0:T(8,128)} %param.4), kind=kLoop, calls=%fused_computation.1 | loop fusion | flops 786432 | bytes 2621440 | tf_op jit(solution)/shard_map/add | solution.py:162
  7.8 0.0 copy-done
  7.8 1.8 %shard_map.67 = (f32[5,288,128]{2,1,0:T(8,128)S(1)}, f32[5,288,128]{2,1,0:T(8,128)S(1)}, f32[5,288,128]{2,1,0:T(8,128)S(1)}, f32[5,288,128]{2,1,0:T(8,128)S(1)},...) custom-call(f32[256,512]{1,0:T(8,128)S(1)} %get-tuple-element.88.f_i, ...), custom_call_target="tpu_custom_call" | custom-call | bytes 3000000 | tf_op jit(solution)/shard_map/pallas_call | solution.py:575
  9.6 0.0 collective-permute-done.1.far_ref
  9.6 0.0 collective-permute-done.near_ref
  9.6 0.3 shard_map.68
  9.9 2.5 %collective-permute-start.3 = (f32[72,128]{1,0:T(8,128)S(1)}, f32[72,128]{1,0:T(8,128)S(1)}, u32[]{:S(2)}, u32[]{:S(2)}) collective-permute-start(f32[72,128]{1,0:T(8,128)S(1)} %get-tuple-element.52), channel_id=1, source_target_pairs={{0,3},{1,2},{2,1},{3,0},{4,7},{5,6},{6,5},{7,4},{8,11},{9,10},{10,... | collective-permute-start | bytes 110600 | tf_op jit(solution)/shard_map/ppermute | solution.py:556
  12.4 0.5 %collective-permute-start.2 = (f32[72,128]{1,0:T(8,128)S(1)}, f32[72,128]{1,0:T(8,128)S(1)}, u32[]{:S(2)}, u32[]{:S(2)}) collective-permute-start(f32[72,128]{1,0:T(8,128)S(1)} %get-tuple-element.51.after), channel_id=1, source_target_pairs={{0,1},{1,0},{2,3},{3,2},{4,5},{5,4},{6,7},{7,6},{8,9},{9,8},{10,11... | collective-permute-start | bytes 110600 | tf_op jit(solution)/shard_map/ppermute | solution.py:555
  12.9 2.2 %shard_map.69 = (f32[5,288,128]{2,1,0:T(8,128)S(1)}, f32[5,288,128]{2,1,0:T(8,128)S(1)}, f32[5,288,128]{2,1,0:T(8,128)S(1)}, f32[5,288,128]{2,1,0:T(8,128)S(1)},...) custom-call(f32[72,128]{1,0:T(8,128)S(1)} %get-tuple-element.51.afte, ...), custom_call_target="tpu_custom_call", output_to_operand_aliasing={{0}: (3, {}), {1}: (4, {}), {2}: (5, {}), {3}: (6, {}), {4}... | custom-call | bytes 8000000 | tf_op jit(solution)/shard_map/pallas_call | solution.py:575
  15.1 0.0 collective-permute-done.3.far_ref
  15.1 1.2 %collective-permute-done.2.near_ref = f32[72,128]{1,0:T(8,128)S(1)} collective-permute-done((f32[72,128]{1,0:T(8,128)S(1)}, f32[72,128]{1,0:T(8,128)S(1)}, u32[]{:S(2)}, u32[]{:S(2)}) %collective-permute-start.2) | collective-permute-done | bytes 36896 | tf_op jit(solution)/shard_map/ppermute | solution.py:555
  16.3 1.5 %shard_map.70 = (f32[5,288,128]{2,1,0:T(8,128)S(1)}, f32[5,288,128]{2,1,0:T(8,128)S(1)}, f32[5,288,128]{2,1,0:T(8,128)S(1)}, f32[5,288,128]{2,1,0:T(8,128)S(1)},...) custom-call(f32[72,128]{1,0:T(8,128)S(1)} %collective-permute-done.2, ...), custom_call_target="tpu_custom_call", output_to_operand_aliasing={{0}: (3, {}), {1}: (4, {}), {2}: (5, {}), {3}: (6, {}), {4}... | custom-call | tf_op jit(solution)/shard_map/pallas_call | solution.py:575
  17.9 8.9 %all_to_all.10.rows_ref = f32[32,1,128]{2,1,0:T(1,128)S(1)} all-to-all(f32[32,1,128]{2,1,0:T(1,128)S(1)} %get-tuple-element.67), channel_id=1, replica_groups=mesh['row'=8,'col'=4] {'row','col'}, dimensions={0} | all-to-all | bytes 32768 | tf_op jit(solution)/shard_map/all_to_all | solution.py:561
  26.8 4.9 %shard_map.71 = (f32[256,512]{1,0:T(8,128)}, f32[5,288,128]{2,1,0:T(8,128)S(1)}, f32[5,288,128]{2,1,0:T(8,128)S(1)}, f32[32,1,128]{2,1,0:T(1,128)S(1)}) custom-call(f32[32,1,128]{2,1,0:T(1,128)S(1)} %all_to_all.10.rows_ref, f32[5,288,128]{2,1,0:T(8,128)S(1)} %get-tuple-element.68.f_ref, f32[5,288,128]{2,1,0:T(8,128)S(1)} %get-tuple-element.69.c_ref, ...), custom_call_target="tpu_custom_call" | custom-call | tf_op jit(solution)/shard_map/pallas_call | solution.py:575
  31.7 8.9 %all_to_all.11.rows_ref = f32[32,1,128]{2,1,0:T(1,128)S(1)} all-to-all(f32[32,1,128]{2,1,0:T(1,128)S(1)} %get-tuple-element.76), channel_id=1, replica_groups=mesh['row'=8,'col'=4] {'row','col'}, dimensions={0} | all-to-all | bytes 32768 | tf_op jit(solution)/shard_map/all_to_all | solution.py:561
  40.6 1.5 %shard_map.72 = (f32[256,512]{1,0:T(8,128)}, f32[1,1]{1,0:T(1,128)}) custom-call(f32[32,1,128]{2,1,0:T(1,128)S(1)} %all_to_all.11.rows_ref, f32[5,288,128]{2,1,0:T(8,128)S(1)} %get-tuple-element.70.p_ref, f32[5,288,128]{2,1,0:T(8,128)S(1)} %get-tuple-element.77.u1_ref, f32[5,288,128]{2,1,0:T(8,128)S(1)} %get-tuple-element.78.u2_ref), custom_call_target="tpu_custom_call" | custom-call | tf_op jit(solution)/shard_map/pallas_call | solution.py:575
  (6 shorter events, 0.0 us)
Async XLA Ops:
  0.6 7.2 %copy-start = (f32[256,512]{1,0:T(8,128)S(1)}, f32[256,512]{1,0:T(8,128)}, u32[]{:S(2)}) copy-start(f32[256,512]{1,0:T(8,128)} %p_in.1) | copy-start | bytes 1572868
  1.6 7.9 %collective-permute-start.1 = (f32[16,512]{1,0:T(8,128)S(1)}, f32[16,512]{1,0:T(8,128)S(1)}, u32[]{:S(2)}, u32[]{:S(2)}) collective-permute-start(f32[16,512]{1,0:T(8,128)S(1)} %get-tuple-element.91), channel_id=1, source_target_pairs={{0,28},{4,8},{8,4},{12,16},{16,12},{20,24},{24,20},{28,0},{1,29},{... | collective-permute-start | bytes 98312 | tf_op jit(solution)/shard_map/ppermute | solution.py:556
  6.2 3.4 %collective-permute-start = (f32[16,512]{1,0:T(8,128)S(1)}, f32[16,512]{1,0:T(8,128)S(1)}, u32[]{:S(2)}, u32[]{:S(2)}) collective-permute-start(f32[16,512]{1,0:T(8,128)S(1)} %get-tuple-element.92), channel_id=1, source_target_pairs={{0,4},{4,0},{8,12},{12,8},{16,20},{20,16},{24,28},{28,24},{1,5},{5... | collective-permute-start | bytes 98312 | tf_op jit(solution)/shard_map/ppermute | solution.py:555
  9.9 5.2 %collective-permute-start.3 = (f32[72,128]{1,0:T(8,128)S(1)}, f32[72,128]{1,0:T(8,128)S(1)}, u32[]{:S(2)}, u32[]{:S(2)}) collective-permute-start(f32[72,128]{1,0:T(8,128)S(1)} %get-tuple-element.52), channel_id=1, source_target_pairs={{0,3},{1,2},{2,1},{3,0},{4,7},{5,6},{6,5},{7,4},{8,11},{9,10},{10,... | collective-permute-start | bytes 110600 | tf_op jit(solution)/shard_map/ppermute | solution.py:556
  12.4 4.0 %collective-permute-start.2 = (f32[72,128]{1,0:T(8,128)S(1)}, f32[72,128]{1,0:T(8,128)S(1)}, u32[]{:S(2)}, u32[]{:S(2)}) collective-permute-start(f32[72,128]{1,0:T(8,128)S(1)} %get-tuple-element.51.after), channel_id=1, source_target_pairs={{0,1},{1,0},{2,3},{3,2},{4,5},{5,4},{6,7},{7,6},{8,9},{9,8},{10,11... | collective-permute-start | bytes 110600 | tf_op jit(solution)/shard_map/ppermute | solution.py:555

commit v5 on v4

--- a/solution.py
+++ b/solution.py
@@ -20,6 +20,7 @@
 VMEM_BYTES = 16 * 2**20
 VM = pl.BlockSpec(memory_space=pltpu.VMEM)
 BOTH = ("row", "col")
+CHAIN = 8
 
 
 def two_sum(a, b):
@@ -79,11 +80,11 @@
     g2 = dsub(g2, dmul(l3, g1))
     full1 = s11[0] > 1e-12 * d12[0]
     full2 = full1 & (t22[0] > 1e-12 * d23[0])
-    c2 = jnp.where(full2, ddiv(g2, t22)[0], zero)
-    c1 = ddiv(dsub(g1, dmul(s12, (c2, zero))), s11)[0]
+    c2 = jnp.where(full2, g2[0] / t22[0], zero)
+    c1 = dsub(g1, dmul(s12, (c2, zero)))[0] / s11[0]
     c1 = jnp.where(full1, c1, zero)
     r0 = dsub(dsub(g0, dmul(d02, (c1, zero))), dmul(d03, (c2, zero)))
-    return ddiv(r0, d01)[0], c1, c2
+    return r0[0] / d01[0], c1, c2
 
 
 PAIRS = ((0, 0), (0, 1), (0, 2), (0, 3), (1, 1), (1, 2), (1, 3), (2, 2), (2, 3))
@@ -96,19 +97,19 @@
 
 
 def dot_step(groups, sums):
-    parts = [[split_short(v) for v in vs] for vs in groups]
+    mains, rests = [None] * len(PAIRS), [None] * len(PAIRS)
+    for vs in groups:
+        parts = [split_short(v) for v in vs]
+        for k, (i, j) in enumerate(PAIRS):
+            m = parts[i][0] * parts[j][0]
+            if i == j:
+                r = parts[i][1] * (vs[i] + parts[i][0])
+            else:
+                r = parts[i][0] * parts[j][1] + parts[i][1] * vs[j]
+            mains[k] = m if mains[k] is None else mains[k] + m
+            rests[k] = r if rests[k] is None else rests[k] + r
     out = []
-    for k, (i, j) in enumerate(PAIRS):
-        main = None
-        rest = None
-        for vs, ps in zip(groups, parts):
-            m = ps[i][0] * ps[j][0]
-            if i == j:
-                r = ps[i][1] * (vs[i] + ps[i][0])
-            else:
-                r = ps[i][0] * ps[j][1] + ps[i][1] * vs[j]
-            main = m if main is None else main + m
-            rest = r if rest is None else rest + r
+    for k, (main, rest) in enumerate(zip(mains, rests)):
         s, e = two_sum(sums[2 * k], main)
         out += [s, sums[2 * k + 1] + (e + rest)]
     return tuple(out)
@@ -328,7 +329,7 @@
     return (jnp.zeros((SUB, LANES), jnp.float32),) * (2 * len(PAIRS))
 
 
-def own_products(v0_ref, v1_ref, v2_ref, w_ref, center_ref, sums, unroll=2):
+def own_products(v0_ref, v1_ref, v2_ref, w_ref, center_ref, sums, unroll=4):
     own = list(range(v0_ref.shape[0] - 1))
     lane = lanes()
 
@@ -345,7 +346,9 @@
                 if j == own[-1]:
                     vs = [jnp.where(lane < LANES - DEEP, v, 0.0) for v in vs]
                 groups.append((*vs, out[j]))
-        return dot_step(groups, sums)
+        for k in range(0, len(groups), CHAIN):
+            sums = dot_step(groups[k : k + CHAIN], sums)
+        return sums
 
     return lax.fori_loop(0, (row_tiles(v0_ref) - 2) // unroll, step, sums)
 
@@ -456,8 +459,8 @@
                 at = slice(SUB + t * SUB, 2 * SUB + t * SUB)
                 ref[count, at] = jnp.where(halo, pltpu.roll(both, (EDGE - 2 * WIDE * g) % LANES, 1), ref[count, at])
     sweep(0, tiles, lambda r: first_vector(
-        f_ref, c_ref, v1_ref, w_ref, faces_ref, center_ref, r, [count]), 8)
-    second_vector(v1_ref, v2_ref, w_ref, center_ref, [[count]], 8)
+        f_ref, c_ref, v1_ref, w_ref, faces_ref, center_ref, r, [count]), 17)
+    second_vector(v1_ref, v2_ref, w_ref, center_ref, [[count]], 17)
     sums = tuple(sums_in[k] for k in range(2 * len(PAIRS)))
     sums = margin_products(f_ref, v1_ref, v2_ref, w_ref, center_ref, sums)
     row_ref[...] = jnp.broadcast_to(pack_sums(sums)[None], row_ref.shape)

time: 42.3 us -> 41.6 us (0.983)
  Pallas kernels: 12.1 us -> 11.1 us
    pallas_call x6, Pallas kernels: 12.1 us -> 11.1 us  [call(): pl.pallas_call(kernel, in_specs=[VM] * len(ins), out_specs=[pl.BlockSpec(...]
where the time goes in v5:
time: 41.6 us; the launch traced here: 41.4 us
  blocking collectives  17.8 us (43%)
  Pallas kernels  11.1 us (27%)
  starting transfers between devices  7.63 us (18%)
  other arithmetic  2.47 us (6%)
  waiting for transfers between devices  1.51 us (4%)
  between operations  0.78 us (2%)
    all_to_all x2, blocking collectives, everyone(): return lax.all_to_all(row, BOTH, 0, 0, tiled=True)  17.8 us
    pallas_call x6, Pallas kernels, call(): pl.pallas_call(kernel, in_specs=[VM] * len(ins), out_specs=[pl.BlockSpec(...  11.1 us
    ppermute x2, starting transfers between devices, exchange(): lax.ppermute(far, axis, [(i, (((i + 1) % n ^ 1) - 1) % n) for i in range(...  7.09 us
    add x2, other arithmetic, fields_of(): return (rc + control_cost, 1.0 + control_cost)  2.44 us
    ppermute x2, waiting for transfers between devices, exchange(): near = lax.ppermute(near, axis, [(i, i ^ 1) for i in range(n)])  1.51 us
  transfers between devices with their start and end apart: 4, of which 1 were waited for; matrix products, arithmetic and copies ran while one was open for 4% of the time, Pallas kernels for 9%

profile of v5, /device:TPU:0, one launch (start us, length us, event | category | flops | bytes accessed | tf_op | source)
XLA Modules:
  0.0 41.4 jit_solution(870818458760198713)
XLA Ops:
  0.6 0.0 copy-start
  0.6 0.9 %broadcast_add_fusion.1 = (f32[8,512]{1,0:T(8,128)S(1)}, f32[8,512]{1,0:T(8,128)S(1)}, f32[8,512]{1,0:T(8,128)S(1)}, f32[8,512]{1,0:T(8,128)S(1)}, f32[8,512]{1,0:T(8,128)S(1)}, /*index=5*/f32[8,512]{1,0:T(8,128)S(1)}) fusion(f32[256,512]{1,0:T(8,128)} %param.6, f32[256,512]{1,0:T(8,128)} %param.5, f32[256,512]{1,0:T(8,128)} %param.4, f32[256,512]{1,0:T(8,128)} %p_in.1), kind=kLoop, calls=%fused_computation.11 | loop fusion | flops 49152 | bytes 229376 | tf_op jit(solution)/shard_map/add | solution.py:163
  1.6 4.6 %collective-permute-start.1 = (f32[16,512]{1,0:T(8,128)S(1)}, f32[16,512]{1,0:T(8,128)S(1)}, u32[]{:S(2)}, u32[]{:S(2)}) collective-permute-start(f32[16,512]{1,0:T(8,128)S(1)} %get-tuple-element.91), channel_id=1, source_target_pairs={{0,28},{4,8},{8,4},{12,16},{16,12},{20,24},{24,20},{28,0},{1,29},{... | collective-permute-start | bytes 98312 | tf_op jit(solution)/shard_map/ppermute | solution.py:559
  6.2 0.0 collective-permute-start
  6.2 1.5 %broadcast_add_fusion = (f32[256,512]{1,0:T(8,128)S(1)}, f32[256,512]{1,0:T(8,128)S(1)}) fusion(f32[256,512]{1,0:T(8,128)} %param.6, f32[256,512]{1,0:T(8,128)} %param.5, f32[256,512]{1,0:T(8,128)} %param.4), kind=kLoop, calls=%fused_computation.1 | loop fusion | flops 786432 | bytes 2621440 | tf_op jit(solution)/shard_map/add | solution.py:163
  7.8 0.0 copy-done
  7.8 1.8 %shard_map.67 = (f32[5,288,128]{2,1,0:T(8,128)S(1)}, f32[5,288,128]{2,1,0:T(8,128)S(1)}, f32[5,288,128]{2,1,0:T(8,128)S(1)}, f32[5,288,128]{2,1,0:T(8,128)S(1)},...) custom-call(f32[256,512]{1,0:T(8,128)S(1)} %get-tuple-element.88.f_i, ...), custom_call_target="tpu_custom_call" | custom-call | bytes 3000000 | tf_op jit(solution)/shard_map/pallas_call | solution.py:578
  9.6 0.0 collective-permute-done.1.far_ref
  9.6 0.0 collective-permute-done.near_ref
  9.6 0.3 shard_map.68
  9.9 2.5 %collective-permute-start.3 = (f32[72,128]{1,0:T(8,128)S(1)}, f32[72,128]{1,0:T(8,128)S(1)}, u32[]{:S(2)}, u32[]{:S(2)}) collective-permute-start(f32[72,128]{1,0:T(8,128)S(1)} %get-tuple-element.52), channel_id=1, source_target_pairs={{0,3},{1,2},{2,1},{3,0},{4,7},{5,6},{6,5},{7,4},{8,11},{9,10},{10,... | collective-permute-start | bytes 110600 | tf_op jit(solution)/shard_map/ppermute | solution.py:559
  12.4 0.5 %collective-permute-start.2 = (f32[72,128]{1,0:T(8,128)S(1)}, f32[72,128]{1,0:T(8,128)S(1)}, u32[]{:S(2)}, u32[]{:S(2)}) collective-permute-start(f32[72,128]{1,0:T(8,128)S(1)} %get-tuple-element.51.after), channel_id=1, source_target_pairs={{0,1},{1,0},{2,3},{3,2},{4,5},{5,4},{6,7},{7,6},{8,9},{9,8},{10,11... | collective-permute-start | bytes 110600 | tf_op jit(solution)/shard_map/ppermute | solution.py:558
  12.9 1.9 %shard_map.69 = (f32[5,288,128]{2,1,0:T(8,128)S(1)}, f32[5,288,128]{2,1,0:T(8,128)S(1)}, f32[5,288,128]{2,1,0:T(8,128)S(1)}, f32[5,288,128]{2,1,0:T(8,128)S(1)},...) custom-call(f32[72,128]{1,0:T(8,128)S(1)} %get-tuple-element.51.afte, ...), custom_call_target="tpu_custom_call", output_to_operand_aliasing={{0}: (3, {}), {1}: (4, {}), {2}: (5, {}), {3}: (6, {}), {4}... | custom-call | bytes 8000000 | tf_op jit(solution)/shard_map/pallas_call | solution.py:578
  14.8 0.0 collective-permute-done.3.far_ref
  14.8 1.5 %collective-permute-done.2.near_ref = f32[72,128]{1,0:T(8,128)S(1)} collective-permute-done((f32[72,128]{1,0:T(8,128)S(1)}, f32[72,128]{1,0:T(8,128)S(1)}, u32[]{:S(2)}, u32[]{:S(2)}) %collective-permute-start.2) | collective-permute-done | bytes 36896 | tf_op jit(solution)/shard_map/ppermute | solution.py:558
  16.3 1.2 %shard_map.70 = (f32[5,288,128]{2,1,0:T(8,128)S(1)}, f32[5,288,128]{2,1,0:T(8,128)S(1)}, f32[5,288,128]{2,1,0:T(8,128)S(1)}, f32[5,288,128]{2,1,0:T(8,128)S(1)},...) custom-call(f32[72,128]{1,0:T(8,128)S(1)} %collective-permute-done.2, ...), custom_call_target="tpu_custom_call", output_to_operand_aliasing={{0}: (3, {}), {1}: (4, {}), {2}: (5, {}), {3}: (6, {}), {4}... | custom-call | tf_op jit(solution)/shard_map/pallas_call | solution.py:578
  17.5 8.9 %all_to_all.10.rows_ref = f32[32,1,128]{2,1,0:T(1,128)S(1)} all-to-all(f32[32,1,128]{2,1,0:T(1,128)S(1)} %get-tuple-element.67), channel_id=1, replica_groups=mesh['row'=8,'col'=4] {'row','col'}, dimensions={0} | all-to-all | bytes 32768 | tf_op jit(solution)/shard_map/all_to_all | solution.py:564
  26.5 4.6 %shard_map.71 = (f32[256,512]{1,0:T(8,128)}, f32[5,288,128]{2,1,0:T(8,128)S(1)}, f32[5,288,128]{2,1,0:T(8,128)S(1)}, f32[32,1,128]{2,1,0:T(1,128)S(1)}) custom-call(f32[32,1,128]{2,1,0:T(1,128)S(1)} %all_to_all.10.rows_ref, f32[5,288,128]{2,1,0:T(8,128)S(1)} %get-tuple-element.68.f_ref, f32[5,288,128]{2,1,0:T(8,128)S(1)} %get-tuple-element.69.c_ref, ...), custom_call_target="tpu_custom_call" | custom-call | tf_op jit(solution)/shard_map/pallas_call | solution.py:578
  31.0 8.9 %all_to_all.11.rows_ref = f32[32,1,128]{2,1,0:T(1,128)S(1)} all-to-all(f32[32,1,128]{2,1,0:T(1,128)S(1)} %get-tuple-element.76), channel_id=1, replica_groups=mesh['row'=8,'col'=4] {'row','col'}, dimensions={0} | all-to-all | bytes 32768 | tf_op jit(solution)/shard_map/all_to_all | solution.py:564
  39.9 1.4 %shard_map.72 = (f32[256,512]{1,0:T(8,128)}, f32[1,1]{1,0:T(1,128)}) custom-call(f32[32,1,128]{2,1,0:T(1,128)S(1)} %all_to_all.11.rows_ref, f32[5,288,128]{2,1,0:T(8,128)S(1)} %get-tuple-element.70.p_ref, f32[5,288,128]{2,1,0:T(8,128)S(1)} %get-tuple-element.77.u1_ref, f32[5,288,128]{2,1,0:T(8,128)S(1)} %get-tuple-element.78.u2_ref), custom_call_target="tpu_custom_call" | custom-call | tf_op jit(solution)/shard_map/pallas_call | solution.py:578
  (6 shorter events, 0.0 us)
Async XLA Ops:
  0.6 7.2 %copy-start = (f32[256,512]{1,0:T(8,128)S(1)}, f32[256,512]{1,0:T(8,128)}, u32[]{:S(2)}) copy-start(f32[256,512]{1,0:T(8,128)} %p_in.1) | copy-start | bytes 1572868
  1.6 7.9 %collective-permute-start.1 = (f32[16,512]{1,0:T(8,128)S(1)}, f32[16,512]{1,0:T(8,128)S(1)}, u32[]{:S(2)}, u32[]{:S(2)}) collective-permute-start(f32[16,512]{1,0:T(8,128)S(1)} %get-tuple-element.91), channel_id=1, source_target_pairs={{0,28},{4,8},{8,4},{12,16},{16,12},{20,24},{24,20},{28,0},{1,29},{... | collective-permute-start | bytes 98312 | tf_op jit(solution)/shard_map/ppermute | solution.py:559
  6.2 3.4 %collective-permute-start = (f32[16,512]{1,0:T(8,128)S(1)}, f32[16,512]{1,0:T(8,128)S(1)}, u32[]{:S(2)}, u32[]{:S(2)}) collective-permute-start(f32[16,512]{1,0:T(8,128)S(1)} %get-tuple-element.92), channel_id=1, source_target_pairs={{0,4},{4,0},{8,12},{12,8},{16,20},{20,16},{24,28},{28,24},{1,5},{5... | collective-permute-start | bytes 98312 | tf_op jit(solution)/shard_map/ppermute | solution.py:558
  9.9 5.0 %collective-permute-start.3 = (f32[72,128]{1,0:T(8,128)S(1)}, f32[72,128]{1,0:T(8,128)S(1)}, u32[]{:S(2)}, u32[]{:S(2)}) collective-permute-start(f32[72,128]{1,0:T(8,128)S(1)} %get-tuple-element.52), channel_id=1, source_target_pairs={{0,3},{1,2},{2,1},{3,0},{4,7},{5,6},{6,5},{7,4},{8,11},{9,10},{10,... | collective-permute-start | bytes 110600 | tf_op jit(solution)/shard_map/ppermute | solution.py:559
  12.4 4.0 %collective-permute-start.2 = (f32[72,128]{1,0:T(8,128)S(1)}, f32[72,128]{1,0:T(8,128)S(1)}, u32[]{:S(2)}, u32[]{:S(2)}) collective-permute-start(f32[72,128]{1,0:T(8,128)S(1)} %get-tuple-element.51.after), channel_id=1, source_target_pairs={{0,1},{1,0},{2,3},{3,2},{4,5},{5,4},{6,7},{7,6},{8,9},{9,8},{10,11... | collective-permute-start | bytes 110600 | tf_op jit(solution)/shard_map/ppermute | solution.py:558

commit v6 on v5

--- a/solution.py
+++ b/solution.py
@@ -182,6 +182,10 @@
     return lax.rem(lax.axis_index(axis), 2) == 0
 
 
+def even_share(n, most):
+    return max(d for d in range(1, most + 1) if n % d == 0)
+
+
 def lanes():
     return lax.broadcasted_iota(jnp.int32, (SUB, LANES), 1)
 
@@ -317,7 +321,7 @@
         group([SUB + t * SUB for t in rest])
 
 
-def second_vector(v1_ref, v2_ref, w_ref, center_ref, parts, unroll=17, start=0, stop=None):
+def second_vector(v1_ref, v2_ref, w_ref, center_ref, parts, unroll=34, start=0, stop=None):
     def step(r):
         out, _here = apply_tiles(v1_ref, w_ref, center_ref, r, parts)
         return [(v2_ref, j, pl.ds(r, SUB), x) for j, x in out.items()]
@@ -329,9 +333,10 @@
     return (jnp.zeros((SUB, LANES), jnp.float32),) * (2 * len(PAIRS))
 
 
-def own_products(v0_ref, v1_ref, v2_ref, w_ref, center_ref, sums, unroll=4):
+def own_products(v0_ref, v1_ref, v2_ref, w_ref, center_ref, sums, most=8):
     own = list(range(v0_ref.shape[0] - 1))
     lane = lanes()
+    unroll = even_share(row_tiles(v0_ref) - 2, most)
 
     def step(t, sums):
         groups = []
@@ -411,8 +416,8 @@
         for t in range(1, tiles - 1):
             repeat_sides(ref, t)
     sweep(2, tiles - 2,
-          lambda r: first_vector(f_ref, c_ref, v1_ref, w_ref, faces_ref, center_ref, r, own), 6)
-    second_vector(v1_ref, v2_ref, w_ref, center_ref, [own], 7, 3, tiles - 3)
+          lambda r: first_vector(f_ref, c_ref, v1_ref, w_ref, faces_ref, center_ref, r, own), 15)
+    second_vector(v1_ref, v2_ref, w_ref, center_ref, [own], 14, 3, tiles - 3)
 
 
 def inner_rest_kernel(after, near_ref, far_ref, f_in, c_in, p_in, v1_in, v2_in, w_in, faces_in, center_in,
@@ -459,8 +464,8 @@
                 at = slice(SUB + t * SUB, 2 * SUB + t * SUB)
                 ref[count, at] = jnp.where(halo, pltpu.roll(both, (EDGE - 2 * WIDE * g) % LANES, 1), ref[count, at])
     sweep(0, tiles, lambda r: first_vector(
-        f_ref, c_ref, v1_ref, w_ref, faces_ref, center_ref, r, [count]), 17)
-    second_vector(v1_ref, v2_ref, w_ref, center_ref, [[count]], 17)
+        f_ref, c_ref, v1_ref, w_ref, faces_ref, center_ref, r, [count]), 34)
+    second_vector(v1_ref, v2_ref, w_ref, center_ref, [[count]], 34)
     sums = tuple(sums_in[k] for k in range(2 * len(PAIRS)))
     sums = margin_products(f_ref, v1_ref, v2_ref, w_ref, center_ref, sums)
     row_ref[...] = jnp.broadcast_to(pack_sums(sums)[None], row_ref.shape)
@@ -483,7 +488,7 @@
             for j in which
         ]
 
-    sweep(0, tiles, value, 4)
+    sweep(0, tiles, value, 34)
 
     def first(r):
         at = pl.ds(r, SUB)
@@ -502,13 +507,15 @@
             out.append((u1_ref, j, at, weighted_apply(center, w, [x[j] for x in cells])))
         return out
 
-    sweep(0, tiles, first, 17)
+    sweep(0, tiles, first, 34)
+
+    unroll = even_share(tiles - 2, 32)
 
     def outer(t, sums):
         cost, weight = [list(x) for x in sums]
-        for u in range(8):
-            at = pl.ds(pl.multiple_of(PAD + (8 * t + u) * SUB, SUB), SUB)
-            to = pl.ds(pl.multiple_of((8 * t + u) * SUB, SUB), SUB)
+        for u in range(unroll):
+            at = pl.ds(pl.multiple_of(PAD + (unroll * t + u) * SUB, SUB), SUB)
+            to = pl.ds(pl.multiple_of((unroll * t + u) * SUB, SUB), SUB)
             for j in own:
                 v = with_sides(vx_ref[j, at, :], vx_ref[len(own), at, :], j, len(own))
                 p = p_ref[j, at, :]
@@ -518,7 +525,7 @@
         return tuple(cost), tuple(weight)
 
     zeros = (jnp.zeros((SUB, LANES), jnp.float32),) * len(own)
-    extra = [sum(x) for x in lax.fori_loop(0, (tiles - 2) // 8, outer, (zeros, zeros))]
+    extra = [sum(x) for x in lax.fori_loop(0, (tiles - 2) // unroll, outer, (zeros, zeros))]
     copy = pltpu.make_async_copy(value_ref, value_out, sem)
     copy.start()
     second_vector(u1_ref, u2_ref, w_ref, center_ref, parts)
@@ -534,7 +541,8 @@
     c0, c1, c2 = [jnp.broadcast_to(c, (SUB, LANES)) for c in galerkin(dots)]
     count = p_ref.shape[0] - 1
 
-    unroll = 8
+    tiles = density_ref.shape[0] // SUB
+    unroll = even_share(tiles, 32)
 
     def some(t, _):
         for u in range(unroll):
@@ -545,7 +553,7 @@
                 density_ref[to, tile_cols(j)] = with_sides(made[j], made[count], j, count)
         return 0
 
-    lax.fori_loop(0, density_ref.shape[0] // (unroll * SUB), some, 0)
+    lax.fori_loop(0, tiles // unroll, some, 0)
 
 
 def f32(*shape):

time: 41.6 us -> 40.3 us (0.969)
  Pallas kernels: 11.1 us -> 9.69 us
    pallas_call x6, Pallas kernels: 11.1 us -> 9.69 us  [call(): pl.pallas_call(kernel, in_specs=[VM] * len(ins), out_specs=[pl.BlockSpec(...]
  transfers between devices with their start and end apart: 4 -> 4, of which waited for: 1 -> 1; matrix products, arithmetic and copies ran while one was open for 4% -> 4% of each run, Pallas kernels for 9% -> 8%
where the time goes in v6:
time: 40.3 us; the launch traced here: 40 us
  blocking collectives  17.9 us (44%)
  Pallas kernels  9.69 us (24%)
  starting transfers between devices  7.63 us (19%)
  other arithmetic  2.47 us (6%)
  waiting for transfers between devices  1.57 us (4%)
  between operations  0.77 us (2%)
    all_to_all x2, blocking collectives, everyone(): return lax.all_to_all(row, BOTH, 0, 0, tiled=True)  17.9 us
    pallas_call x6, Pallas kernels, call(): pl.pallas_call(kernel, in_specs=[VM] * len(ins), out_specs=[pl.BlockSpec(...  9.69 us
    ppermute x2, starting transfers between devices, exchange(): lax.ppermute(far, axis, [(i, (((i + 1) % n ^ 1) - 1) % n) for i in range(...  7.09 us
    add x2, other arithmetic, fields_of(): return (rc + control_cost, 1.0 + control_cost)  2.44 us
    ppermute x2, waiting for transfers between devices, exchange(): near = lax.ppermute(near, axis, [(i, i ^ 1) for i in range(n)])  1.55 us
  transfers between devices with their start and end apart: 4, of which 1 were waited for; matrix products, arithmetic and copies ran while one was open for 4% of the time, Pallas kernels for 8%

profile of v6, /device:TPU:0, one launch (start us, length us, event | category | flops | bytes accessed | tf_op | source)
XLA Modules:
  0.0 40.0 jit_solution(7084800847068649817)
XLA Ops:
  0.6 0.0 copy-start
  0.6 0.9 %broadcast_add_fusion.1 = (f32[8,512]{1,0:T(8,128)S(1)}, f32[8,512]{1,0:T(8,128)S(1)}, f32[8,512]{1,0:T(8,128)S(1)}, f32[8,512]{1,0:T(8,128)S(1)}, f32[8,512]{1,0:T(8,128)S(1)}, /*index=5*/f32[8,512]{1,0:T(8,128)S(1)}) fusion(f32[256,512]{1,0:T(8,128)} %param.6, f32[256,512]{1,0:T(8,128)} %param.5, f32[256,512]{1,0:T(8,128)} %param.4, f32[256,512]{1,0:T(8,128)} %p_in.1), kind=kLoop, calls=%fused_computation.11 | loop fusion | flops 49152 | bytes 229376 | tf_op jit(solution)/shard_map/add | solution.py:163
  1.6 4.6 %collective-permute-start.1 = (f32[16,512]{1,0:T(8,128)S(1)}, f32[16,512]{1,0:T(8,128)S(1)}, u32[]{:S(2)}, u32[]{:S(2)}) collective-permute-start(f32[16,512]{1,0:T(8,128)S(1)} %get-tuple-element.91), channel_id=1, source_target_pairs={{0,28},{4,8},{8,4},{12,16},{16,12},{20,24},{24,20},{28,0},{1,29},{... | collective-permute-start | bytes 98312 | tf_op jit(solution)/shard_map/ppermute | solution.py:567
  6.2 0.0 collective-permute-start
  6.2 1.5 %broadcast_add_fusion = (f32[256,512]{1,0:T(8,128)S(1)}, f32[256,512]{1,0:T(8,128)S(1)}) fusion(f32[256,512]{1,0:T(8,128)} %param.6, f32[256,512]{1,0:T(8,128)} %param.5, f32[256,512]{1,0:T(8,128)} %param.4), kind=kLoop, calls=%fused_computation.1 | loop fusion | flops 786432 | bytes 2621440 | tf_op jit(solution)/shard_map/add | solution.py:163
  7.8 0.0 copy-done
  7.8 1.5 %shard_map.67 = (f32[5,288,128]{2,1,0:T(8,128)S(1)}, f32[5,288,128]{2,1,0:T(8,128)S(1)}, f32[5,288,128]{2,1,0:T(8,128)S(1)}, f32[5,288,128]{2,1,0:T(8,128)S(1)},...) custom-call(f32[256,512]{1,0:T(8,128)S(1)} %get-tuple-element.88.f_i, ...), custom_call_target="tpu_custom_call" | custom-call | bytes 3000000 | tf_op jit(solution)/shard_map/pallas_call | solution.py:586
  9.3 0.0 collective-permute-done.1.far_ref
  9.3 0.0 collective-permute-done.near_ref
  9.3 0.3 shard_map.68
  9.6 2.5 %collective-permute-start.3 = (f32[72,128]{1,0:T(8,128)S(1)}, f32[72,128]{1,0:T(8,128)S(1)}, u32[]{:S(2)}, u32[]{:S(2)}) collective-permute-start(f32[72,128]{1,0:T(8,128)S(1)} %get-tuple-element.52), channel_id=1, source_target_pairs={{0,3},{1,2},{2,1},{3,0},{4,7},{5,6},{6,5},{7,4},{8,11},{9,10},{10,... | collective-permute-start | bytes 110600 | tf_op jit(solution)/shard_map/ppermute | solution.py:567
  12.1 0.5 %collective-permute-start.2 = (f32[72,128]{1,0:T(8,128)S(1)}, f32[72,128]{1,0:T(8,128)S(1)}, u32[]{:S(2)}, u32[]{:S(2)}) collective-permute-start(f32[72,128]{1,0:T(8,128)S(1)} %get-tuple-element.51.after), channel_id=1, source_target_pairs={{0,1},{1,0},{2,3},{3,2},{4,5},{5,4},{6,7},{7,6},{8,9},{9,8},{10,11... | collective-permute-start | bytes 110600 | tf_op jit(solution)/shard_map/ppermute | solution.py:566
  12.6 1.9 %shard_map.69 = (f32[5,288,128]{2,1,0:T(8,128)S(1)}, f32[5,288,128]{2,1,0:T(8,128)S(1)}, f32[5,288,128]{2,1,0:T(8,128)S(1)}, f32[5,288,128]{2,1,0:T(8,128)S(1)},...) custom-call(f32[72,128]{1,0:T(8,128)S(1)} %get-tuple-element.51.afte, ...), custom_call_target="tpu_custom_call", output_to_operand_aliasing={{0}: (3, {}), {1}: (4, {}), {2}: (5, {}), {3}: (6, {}), {4}... | custom-call | bytes 8000000 | tf_op jit(solution)/shard_map/pallas_call | solution.py:586
  14.5 0.0 collective-permute-done.3.far_ref
  14.5 1.5 %collective-permute-done.2.near_ref = f32[72,128]{1,0:T(8,128)S(1)} collective-permute-done((f32[72,128]{1,0:T(8,128)S(1)}, f32[72,128]{1,0:T(8,128)S(1)}, u32[]{:S(2)}, u32[]{:S(2)}) %collective-permute-start.2) | collective-permute-done | bytes 36896 | tf_op jit(solution)/shard_map/ppermute | solution.py:566
  16.0 1.1 %shard_map.70 = (f32[5,288,128]{2,1,0:T(8,128)S(1)}, f32[5,288,128]{2,1,0:T(8,128)S(1)}, f32[5,288,128]{2,1,0:T(8,128)S(1)}, f32[5,288,128]{2,1,0:T(8,128)S(1)},...) custom-call(f32[72,128]{1,0:T(8,128)S(1)} %collective-permute-done.2, ...), custom_call_target="tpu_custom_call", output_to_operand_aliasing={{0}: (3, {}), {1}: (4, {}), {2}: (5, {}), {3}: (6, {}), {4}... | custom-call | tf_op jit(solution)/shard_map/pallas_call | solution.py:586
  17.2 9.0 %all_to_all.10.rows_ref = f32[32,1,128]{2,1,0:T(1,128)S(1)} all-to-all(f32[32,1,128]{2,1,0:T(1,128)S(1)} %get-tuple-element.67), channel_id=1, replica_groups=mesh['row'=8,'col'=4] {'row','col'}, dimensions={0} | all-to-all | bytes 32768 | tf_op jit(solution)/shard_map/all_to_all | solution.py:572
  26.1 3.8 %shard_map.71 = (f32[256,512]{1,0:T(8,128)}, f32[5,288,128]{2,1,0:T(8,128)S(1)}, f32[5,288,128]{2,1,0:T(8,128)S(1)}, f32[32,1,128]{2,1,0:T(1,128)S(1)}) custom-call(f32[32,1,128]{2,1,0:T(1,128)S(1)} %all_to_all.10.rows_ref, f32[5,288,128]{2,1,0:T(8,128)S(1)} %get-tuple-element.68.f_ref, f32[5,288,128]{2,1,0:T(8,128)S(1)} %get-tuple-element.69.c_ref, ...), custom_call_target="tpu_custom_call" | custom-call | tf_op jit(solution)/shard_map/pallas_call | solution.py:586
  29.9 8.9 %all_to_all.11.rows_ref = f32[32,1,128]{2,1,0:T(1,128)S(1)} all-to-all(f32[32,1,128]{2,1,0:T(1,128)S(1)} %get-tuple-element.76), channel_id=1, replica_groups=mesh['row'=8,'col'=4] {'row','col'}, dimensions={0} | all-to-all | bytes 32768 | tf_op jit(solution)/shard_map/all_to_all | solution.py:572
  38.8 1.2 %shard_map.72 = (f32[256,512]{1,0:T(8,128)}, f32[1,1]{1,0:T(1,128)}) custom-call(f32[32,1,128]{2,1,0:T(1,128)S(1)} %all_to_all.11.rows_ref, f32[5,288,128]{2,1,0:T(8,128)S(1)} %get-tuple-element.70.p_ref, f32[5,288,128]{2,1,0:T(8,128)S(1)} %get-tuple-element.77.u1_ref, f32[5,288,128]{2,1,0:T(8,128)S(1)} %get-tuple-element.78.u2_ref), custom_call_target="tpu_custom_call" | custom-call | tf_op jit(solution)/shard_map/pallas_call | solution.py:586
  (6 shorter events, 0.0 us)
Async XLA Ops:
  0.6 7.2 %copy-start = (f32[256,512]{1,0:T(8,128)S(1)}, f32[256,512]{1,0:T(8,128)}, u32[]{:S(2)}) copy-start(f32[256,512]{1,0:T(8,128)} %p_in.1) | copy-start | bytes 1572868
  1.6 7.6 %collective-permute-start.1 = (f32[16,512]{1,0:T(8,128)S(1)}, f32[16,512]{1,0:T(8,128)S(1)}, u32[]{:S(2)}, u32[]{:S(2)}) collective-permute-start(f32[16,512]{1,0:T(8,128)S(1)} %get-tuple-element.91), channel_id=1, source_target_pairs={{0,28},{4,8},{8,4},{12,16},{16,12},{20,24},{24,20},{28,0},{1,29},{... | collective-permute-start | bytes 98312 | tf_op jit(solution)/shard_map/ppermute | solution.py:567
  6.2 3.0 %collective-permute-start = (f32[16,512]{1,0:T(8,128)S(1)}, f32[16,512]{1,0:T(8,128)S(1)}, u32[]{:S(2)}, u32[]{:S(2)}) collective-permute-start(f32[16,512]{1,0:T(8,128)S(1)} %get-tuple-element.92), channel_id=1, source_target_pairs={{0,4},{4,0},{8,12},{12,8},{16,20},{20,16},{24,28},{28,24},{1,5},{5... | collective-permute-start | bytes 98312 | tf_op jit(solution)/shard_map/ppermute | solution.py:566
  9.6 4.9 %collective-permute-start.3 = (f32[72,128]{1,0:T(8,128)S(1)}, f32[72,128]{1,0:T(8,128)S(1)}, u32[]{:S(2)}, u32[]{:S(2)}) collective-permute-start(f32[72,128]{1,0:T(8,128)S(1)} %get-tuple-element.52), channel_id=1, source_target_pairs={{0,3},{1,2},{2,1},{3,0},{4,7},{5,6},{6,5},{7,4},{8,11},{9,10},{10,... | collective-permute-start | bytes 110600 | tf_op jit(solution)/shard_map/ppermute | solution.py:567
  12.1 4.0 %collective-permute-start.2 = (f32[72,128]{1,0:T(8,128)S(1)}, f32[72,128]{1,0:T(8,128)S(1)}, u32[]{:S(2)}, u32[]{:S(2)}) collective-permute-start(f32[72,128]{1,0:T(8,128)S(1)} %get-tuple-element.51.after), channel_id=1, source_target_pairs={{0,1},{1,0},{2,3},{3,2},{4,5},{5,4},{6,7},{7,6},{8,9},{9,8},{10,11... | collective-permute-start | bytes 110600 | tf_op jit(solution)/shard_map/ppermute | solution.py:566

commit v7 on v6

--- a/solution.py
+++ b/solution.py
@@ -416,8 +416,8 @@
         for t in range(1, tiles - 1):
             repeat_sides(ref, t)
     sweep(2, tiles - 2,
-          lambda r: first_vector(f_ref, c_ref, v1_ref, w_ref, faces_ref, center_ref, r, own), 15)
-    second_vector(v1_ref, v2_ref, w_ref, center_ref, [own], 14, 3, tiles - 3)
+          lambda r: first_vector(f_ref, c_ref, v1_ref, w_ref, faces_ref, center_ref, r, own), 30)
+    second_vector(v1_ref, v2_ref, w_ref, center_ref, [own], 28, 3, tiles - 3)
 
 
 def inner_rest_kernel(after, near_ref, far_ref, f_in, c_in, p_in, v1_in, v2_in, w_in, faces_in, center_in,

time: 40.3 us -> 40.2 us (level)
  no operation moved by 1% of the time
where the time goes in v7:
time: 40.2 us; the launch traced here: 40 us
  blocking collectives  18.1 us (45%)
  Pallas kernels  9.41 us (23%)
  starting transfers between devices  7.63 us (19%)
  other arithmetic  2.47 us (6%)
  waiting for transfers between devices  1.57 us (4%)
  between operations  0.77 us (2%)
    all_to_all x2, blocking collectives, everyone(): return lax.all_to_all(row, BOTH, 0, 0, tiled=True)  18.1 us
    pallas_call x6, Pallas kernels, call(): pl.pallas_call(kernel, in_specs=[VM] * len(ins), out_specs=[pl.BlockSpec(...  9.41 us
    ppermute x2, starting transfers between devices, exchange(): lax.ppermute(far, axis, [(i, (((i + 1) % n ^ 1) - 1) % n) for i in range(...  7.09 us
    add x2, other arithmetic, fields_of(): return (rc + control_cost, 1.0 + control_cost)  2.44 us
    ppermute x2, waiting for transfers between devices, exchange(): near = lax.ppermute(near, axis, [(i, i ^ 1) for i in range(n)])  1.55 us
  transfers between devices with their start and end apart: 4, of which 1 were waited for; matrix products, arithmetic and copies ran while one was open for 4% of the time, Pallas kernels for 8%

profile of v7, /device:TPU:0, one launch (start us, length us, event | category | flops | bytes accessed | tf_op | source)
XLA Modules:
  0.0 40.0 jit_solution(8057437717668443372)
XLA Ops:
  0.6 0.0 copy-start
  0.6 0.9 %broadcast_add_fusion.1 = (f32[8,512]{1,0:T(8,128)S(1)}, f32[8,512]{1,0:T(8,128)S(1)}, f32[8,512]{1,0:T(8,128)S(1)}, f32[8,512]{1,0:T(8,128)S(1)}, f32[8,512]{1,0:T(8,128)S(1)}, /*index=5*/f32[8,512]{1,0:T(8,128)S(1)}) fusion(f32[256,512]{1,0:T(8,128)} %param.6, f32[256,512]{1,0:T(8,128)} %param.5, f32[256,512]{1,0:T(8,128)} %param.4, f32[256,512]{1,0:T(8,128)} %p_in.1), kind=kLoop, calls=%fused_computation.11 | loop fusion | flops 49152 | bytes 229376 | tf_op jit(solution)/shard_map/add | solution.py:163
  1.6 4.6 %collective-permute-start.1 = (f32[16,512]{1,0:T(8,128)S(1)}, f32[16,512]{1,0:T(8,128)S(1)}, u32[]{:S(2)}, u32[]{:S(2)}) collective-permute-start(f32[16,512]{1,0:T(8,128)S(1)} %get-tuple-element.91), channel_id=1, source_target_pairs={{0,28},{4,8},{8,4},{12,16},{16,12},{20,24},{24,20},{28,0},{1,29},{... | collective-permute-start | bytes 98312 | tf_op jit(solution)/shard_map/ppermute | solution.py:567
  6.2 0.0 collective-permute-start
  6.2 1.5 %broadcast_add_fusion = (f32[256,512]{1,0:T(8,128)S(1)}, f32[256,512]{1,0:T(8,128)S(1)}) fusion(f32[256,512]{1,0:T(8,128)} %param.6, f32[256,512]{1,0:T(8,128)} %param.5, f32[256,512]{1,0:T(8,128)} %param.4), kind=kLoop, calls=%fused_computation.1 | loop fusion | flops 786432 | bytes 2621440 | tf_op jit(solution)/shard_map/add | solution.py:163
  7.8 0.0 copy-done
  7.8 1.2 %shard_map.67 = (f32[5,288,128]{2,1,0:T(8,128)S(1)}, f32[5,288,128]{2,1,0:T(8,128)S(1)}, f32[5,288,128]{2,1,0:T(8,128)S(1)}, f32[5,288,128]{2,1,0:T(8,128)S(1)},...) custom-call(f32[256,512]{1,0:T(8,128)S(1)} %get-tuple-element.88.f_i, ...), custom_call_target="tpu_custom_call" | custom-call | bytes 3000000 | tf_op jit(solution)/shard_map/pallas_call | solution.py:586
  9.0 0.0 collective-permute-done.1.far_ref
  9.0 0.0 collective-permute-done.near_ref
  9.0 0.3 shard_map.68
  9.3 2.5 %collective-permute-start.3 = (f32[72,128]{1,0:T(8,128)S(1)}, f32[72,128]{1,0:T(8,128)S(1)}, u32[]{:S(2)}, u32[]{:S(2)}) collective-permute-start(f32[72,128]{1,0:T(8,128)S(1)} %get-tuple-element.52), channel_id=1, source_target_pairs={{0,3},{1,2},{2,1},{3,0},{4,7},{5,6},{6,5},{7,4},{8,11},{9,10},{10,... | collective-permute-start | bytes 110600 | tf_op jit(solution)/shard_map/ppermute | solution.py:567
  11.8 0.5 %collective-permute-start.2 = (f32[72,128]{1,0:T(8,128)S(1)}, f32[72,128]{1,0:T(8,128)S(1)}, u32[]{:S(2)}, u32[]{:S(2)}) collective-permute-start(f32[72,128]{1,0:T(8,128)S(1)} %get-tuple-element.51.after), channel_id=1, source_target_pairs={{0,1},{1,0},{2,3},{3,2},{4,5},{5,4},{6,7},{7,6},{8,9},{9,8},{10,11... | collective-permute-start | bytes 110600 | tf_op jit(solution)/shard_map/ppermute | solution.py:566
  12.3 1.9 %shard_map.69 = (f32[5,288,128]{2,1,0:T(8,128)S(1)}, f32[5,288,128]{2,1,0:T(8,128)S(1)}, f32[5,288,128]{2,1,0:T(8,128)S(1)}, f32[5,288,128]{2,1,0:T(8,128)S(1)},...) custom-call(f32[72,128]{1,0:T(8,128)S(1)} %get-tuple-element.51.afte, ...), custom_call_target="tpu_custom_call", output_to_operand_aliasing={{0}: (3, {}), {1}: (4, {}), {2}: (5, {}), {3}: (6, {}), {4}... | custom-call | bytes 8000000 | tf_op jit(solution)/shard_map/pallas_call | solution.py:586
  14.2 0.0 collective-permute-done.3.far_ref
  14.2 1.5 %collective-permute-done.2.near_ref = f32[72,128]{1,0:T(8,128)S(1)} collective-permute-done((f32[72,128]{1,0:T(8,128)S(1)}, f32[72,128]{1,0:T(8,128)S(1)}, u32[]{:S(2)}, u32[]{:S(2)}) %collective-permute-start.2) | collective-permute-done | bytes 36896 | tf_op jit(solution)/shard_map/ppermute | solution.py:566
  15.8 1.1 %shard_map.70 = (f32[5,288,128]{2,1,0:T(8,128)S(1)}, f32[5,288,128]{2,1,0:T(8,128)S(1)}, f32[5,288,128]{2,1,0:T(8,128)S(1)}, f32[5,288,128]{2,1,0:T(8,128)S(1)},...) custom-call(f32[72,128]{1,0:T(8,128)S(1)} %collective-permute-done.2, ...), custom_call_target="tpu_custom_call", output_to_operand_aliasing={{0}: (3, {}), {1}: (4, {}), {2}: (5, {}), {3}: (6, {}), {4}... | custom-call | tf_op jit(solution)/shard_map/pallas_call | solution.py:586
  16.9 9.2 %all_to_all.10.rows_ref = f32[32,1,128]{2,1,0:T(1,128)S(1)} all-to-all(f32[32,1,128]{2,1,0:T(1,128)S(1)} %get-tuple-element.67), channel_id=1, replica_groups=mesh['row'=8,'col'=4] {'row','col'}, dimensions={0} | all-to-all | bytes 32768 | tf_op jit(solution)/shard_map/all_to_all | solution.py:572
  26.1 3.8 %shard_map.71 = (f32[256,512]{1,0:T(8,128)}, f32[5,288,128]{2,1,0:T(8,128)S(1)}, f32[5,288,128]{2,1,0:T(8,128)S(1)}, f32[32,1,128]{2,1,0:T(1,128)S(1)}) custom-call(f32[32,1,128]{2,1,0:T(1,128)S(1)} %all_to_all.10.rows_ref, f32[5,288,128]{2,1,0:T(8,128)S(1)} %get-tuple-element.68.f_ref, f32[5,288,128]{2,1,0:T(8,128)S(1)} %get-tuple-element.69.c_ref, ...), custom_call_target="tpu_custom_call" | custom-call | tf_op jit(solution)/shard_map/pallas_call | solution.py:586
  29.9 8.9 %all_to_all.11.rows_ref = f32[32,1,128]{2,1,0:T(1,128)S(1)} all-to-all(f32[32,1,128]{2,1,0:T(1,128)S(1)} %get-tuple-element.76), channel_id=1, replica_groups=mesh['row'=8,'col'=4] {'row','col'}, dimensions={0} | all-to-all | bytes 32768 | tf_op jit(solution)/shard_map/all_to_all | solution.py:572
  38.8 1.2 %shard_map.72 = (f32[256,512]{1,0:T(8,128)}, f32[1,1]{1,0:T(1,128)}) custom-call(f32[32,1,128]{2,1,0:T(1,128)S(1)} %all_to_all.11.rows_ref, f32[5,288,128]{2,1,0:T(8,128)S(1)} %get-tuple-element.70.p_ref, f32[5,288,128]{2,1,0:T(8,128)S(1)} %get-tuple-element.77.u1_ref, f32[5,288,128]{2,1,0:T(8,128)S(1)} %get-tuple-element.78.u2_ref), custom_call_target="tpu_custom_call" | custom-call | tf_op jit(solution)/shard_map/pallas_call | solution.py:586
  (6 shorter events, 0.0 us)
Async XLA Ops:
  0.6 7.2 %copy-start = (f32[256,512]{1,0:T(8,128)S(1)}, f32[256,512]{1,0:T(8,128)}, u32[]{:S(2)}) copy-start(f32[256,512]{1,0:T(8,128)} %p_in.1) | copy-start | bytes 1572868
  1.6 7.3 %collective-permute-start.1 = (f32[16,512]{1,0:T(8,128)S(1)}, f32[16,512]{1,0:T(8,128)S(1)}, u32[]{:S(2)}, u32[]{:S(2)}) collective-permute-start(f32[16,512]{1,0:T(8,128)S(1)} %get-tuple-element.91), channel_id=1, source_target_pairs={{0,28},{4,8},{8,4},{12,16},{16,12},{20,24},{24,20},{28,0},{1,29},{... | collective-permute-start | bytes 98312 | tf_op jit(solution)/shard_map/ppermute | solution.py:567
  6.2 2.8 %collective-permute-start = (f32[16,512]{1,0:T(8,128)S(1)}, f32[16,512]{1,0:T(8,128)S(1)}, u32[]{:S(2)}, u32[]{:S(2)}) collective-permute-start(f32[16,512]{1,0:T(8,128)S(1)} %get-tuple-element.92), channel_id=1, source_target_pairs={{0,4},{4,0},{8,12},{12,8},{16,20},{20,16},{24,28},{28,24},{1,5},{5... | collective-permute-start | bytes 98312 | tf_op jit(solution)/shard_map/ppermute | solution.py:566
  9.3 4.9 %collective-permute-start.3 = (f32[72,128]{1,0:T(8,128)S(1)}, f32[72,128]{1,0:T(8,128)S(1)}, u32[]{:S(2)}, u32[]{:S(2)}) collective-permute-start(f32[72,128]{1,0:T(8,128)S(1)} %get-tuple-element.52), channel_id=1, source_target_pairs={{0,3},{1,2},{2,1},{3,0},{4,7},{5,6},{6,5},{7,4},{8,11},{9,10},{10,... | collective-permute-start | bytes 110600 | tf_op jit(solution)/shard_map/ppermute | solution.py:567
  11.8 4.0 %collective-permute-start.2 = (f32[72,128]{1,0:T(8,128)S(1)}, f32[72,128]{1,0:T(8,128)S(1)}, u32[]{:S(2)}, u32[]{:S(2)}) collective-permute-start(f32[72,128]{1,0:T(8,128)S(1)} %get-tuple-element.51.after), channel_id=1, source_target_pairs={{0,1},{1,0},{2,3},{3,2},{4,5},{5,4},{6,7},{7,6},{8,9},{9,8},{10,11... | collective-permute-start | bytes 110600 | tf_op jit(solution)/shard_map/ppermute | solution.py:566

commit v8 on v6

--- a/solution.py
+++ b/solution.py
@@ -333,7 +333,7 @@
     return (jnp.zeros((SUB, LANES), jnp.float32),) * (2 * len(PAIRS))
 
 
-def own_products(v0_ref, v1_ref, v2_ref, w_ref, center_ref, sums, most=8):
+def own_products(v0_ref, v1_ref, v2_ref, w_ref, center_ref, sums, most=16):
     own = list(range(v0_ref.shape[0] - 1))
     lane = lanes()
     unroll = even_share(row_tiles(v0_ref) - 2, most)

time: 40.3 us -> 40.2 us (level)
  no operation moved by 1% of the time
where the time goes in v8:
time: 40.2 us; the launch traced here: 40 us
  blocking collectives  17.9 us (45%)
  Pallas kernels  9.64 us (24%)
  starting transfers between devices  7.63 us (19%)
  other arithmetic  2.47 us (6%)
  waiting for transfers between devices  1.59 us (4%)
  between operations  0.77 us (2%)
    all_to_all x2, blocking collectives, everyone(): return lax.all_to_all(row, BOTH, 0, 0, tiled=True)  17.9 us
    pallas_call x6, Pallas kernels, call(): pl.pallas_call(kernel, in_specs=[VM] * len(ins), out_specs=[pl.BlockSpec(...  9.64 us
    ppermute x2, starting transfers between devices, exchange(): lax.ppermute(far, axis, [(i, (((i + 1) % n ^ 1) - 1) % n) for i in range(...  7.09 us
    add x2, other arithmetic, fields_of(): return (rc + control_cost, 1.0 + control_cost)  2.44 us
    ppermute x2, waiting for transfers between devices, exchange(): near = lax.ppermute(near, axis, [(i, i ^ 1) for i in range(n)])  1.55 us
  transfers between devices with their start and end apart: 4, of which 1 were waited for; matrix products, arithmetic and copies ran while one was open for 4% of the time, Pallas kernels for 8%

profile of v8, /device:TPU:0, one launch (start us, length us, event | category | flops | bytes accessed | tf_op | source)
XLA Modules:
  0.0 40.0 jit_solution(1453895412717352842)
XLA Ops:
  0.6 0.0 copy-start
  0.6 0.9 %broadcast_add_fusion.1 = (f32[8,512]{1,0:T(8,128)S(1)}, f32[8,512]{1,0:T(8,128)S(1)}, f32[8,512]{1,0:T(8,128)S(1)}, f32[8,512]{1,0:T(8,128)S(1)}, f32[8,512]{1,0:T(8,128)S(1)}, /*index=5*/f32[8,512]{1,0:T(8,128)S(1)}) fusion(f32[256,512]{1,0:T(8,128)} %param.6, f32[256,512]{1,0:T(8,128)} %param.5, f32[256,512]{1,0:T(8,128)} %param.4, f32[256,512]{1,0:T(8,128)} %p_in.1), kind=kLoop, calls=%fused_computation.11 | loop fusion | flops 49152 | bytes 229376 | tf_op jit(solution)/shard_map/add | solution.py:163
  1.6 4.6 %collective-permute-start.1 = (f32[16,512]{1,0:T(8,128)S(1)}, f32[16,512]{1,0:T(8,128)S(1)}, u32[]{:S(2)}, u32[]{:S(2)}) collective-permute-start(f32[16,512]{1,0:T(8,128)S(1)} %get-tuple-element.91), channel_id=1, source_target_pairs={{0,28},{4,8},{8,4},{12,16},{16,12},{20,24},{24,20},{28,0},{1,29},{... | collective-permute-start | bytes 98312 | tf_op jit(solution)/shard_map/ppermute | solution.py:567
  6.2 0.0 collective-permute-start
  6.2 1.5 %broadcast_add_fusion = (f32[256,512]{1,0:T(8,128)S(1)}, f32[256,512]{1,0:T(8,128)S(1)}) fusion(f32[256,512]{1,0:T(8,128)} %param.6, f32[256,512]{1,0:T(8,128)} %param.5, f32[256,512]{1,0:T(8,128)} %param.4), kind=kLoop, calls=%fused_computation.1 | loop fusion | flops 786432 | bytes 2621440 | tf_op jit(solution)/shard_map/add | solution.py:163
  7.8 0.0 copy-done
  7.8 1.5 %shard_map.67 = (f32[5,288,128]{2,1,0:T(8,128)S(1)}, f32[5,288,128]{2,1,0:T(8,128)S(1)}, f32[5,288,128]{2,1,0:T(8,128)S(1)}, f32[5,288,128]{2,1,0:T(8,128)S(1)},...) custom-call(f32[256,512]{1,0:T(8,128)S(1)} %get-tuple-element.88.f_i, ...), custom_call_target="tpu_custom_call" | custom-call | bytes 3000000 | tf_op jit(solution)/shard_map/pallas_call | solution.py:586
  9.3 0.0 collective-permute-done.1.far_ref
  9.3 0.0 collective-permute-done.near_ref
  9.3 0.3 shard_map.68
  9.6 2.5 %collective-permute-start.3 = (f32[72,128]{1,0:T(8,128)S(1)}, f32[72,128]{1,0:T(8,128)S(1)}, u32[]{:S(2)}, u32[]{:S(2)}) collective-permute-start(f32[72,128]{1,0:T(8,128)S(1)} %get-tuple-element.52), channel_id=1, source_target_pairs={{0,3},{1,2},{2,1},{3,0},{4,7},{5,6},{6,5},{7,4},{8,11},{9,10},{10,... | collective-permute-start | bytes 110600 | tf_op jit(solution)/shard_map/ppermute | solution.py:567
  12.1 0.5 %collective-permute-start.2 = (f32[72,128]{1,0:T(8,128)S(1)}, f32[72,128]{1,0:T(8,128)S(1)}, u32[]{:S(2)}, u32[]{:S(2)}) collective-permute-start(f32[72,128]{1,0:T(8,128)S(1)} %get-tuple-element.51.after), channel_id=1, source_target_pairs={{0,1},{1,0},{2,3},{3,2},{4,5},{5,4},{6,7},{7,6},{8,9},{9,8},{10,11... | collective-permute-start | bytes 110600 | tf_op jit(solution)/shard_map/ppermute | solution.py:566
  12.6 1.8 %shard_map.69 = (f32[5,288,128]{2,1,0:T(8,128)S(1)}, f32[5,288,128]{2,1,0:T(8,128)S(1)}, f32[5,288,128]{2,1,0:T(8,128)S(1)}, f32[5,288,128]{2,1,0:T(8,128)S(1)},...) custom-call(f32[72,128]{1,0:T(8,128)S(1)} %get-tuple-element.51.afte, ...), custom_call_target="tpu_custom_call", output_to_operand_aliasing={{0}: (3, {}), {1}: (4, {}), {2}: (5, {}), {3}: (6, {}), {4}... | custom-call | bytes 8000000 | tf_op jit(solution)/shard_map/pallas_call | solution.py:586
  14.4 0.0 collective-permute-done.3.far_ref
  14.5 1.5 %collective-permute-done.2.near_ref = f32[72,128]{1,0:T(8,128)S(1)} collective-permute-done((f32[72,128]{1,0:T(8,128)S(1)}, f32[72,128]{1,0:T(8,128)S(1)}, u32[]{:S(2)}, u32[]{:S(2)}) %collective-permute-start.2) | collective-permute-done | bytes 36896 | tf_op jit(solution)/shard_map/ppermute | solution.py:566
  16.0 1.1 %shard_map.70 = (f32[5,288,128]{2,1,0:T(8,128)S(1)}, f32[5,288,128]{2,1,0:T(8,128)S(1)}, f32[5,288,128]{2,1,0:T(8,128)S(1)}, f32[5,288,128]{2,1,0:T(8,128)S(1)},...) custom-call(f32[72,128]{1,0:T(8,128)S(1)} %collective-permute-done.2, ...), custom_call_target="tpu_custom_call", output_to_operand_aliasing={{0}: (3, {}), {1}: (4, {}), {2}: (5, {}), {3}: (6, {}), {4}... | custom-call | tf_op jit(solution)/shard_map/pallas_call | solution.py:586
  17.2 9.0 %all_to_all.10.rows_ref = f32[32,1,128]{2,1,0:T(1,128)S(1)} all-to-all(f32[32,1,128]{2,1,0:T(1,128)S(1)} %get-tuple-element.67), channel_id=1, replica_groups=mesh['row'=8,'col'=4] {'row','col'}, dimensions={0} | all-to-all | bytes 32768 | tf_op jit(solution)/shard_map/all_to_all | solution.py:572
  26.1 3.7 %shard_map.71 = (f32[256,512]{1,0:T(8,128)}, f32[5,288,128]{2,1,0:T(8,128)S(1)}, f32[5,288,128]{2,1,0:T(8,128)S(1)}, f32[32,1,128]{2,1,0:T(1,128)S(1)}) custom-call(f32[32,1,128]{2,1,0:T(1,128)S(1)} %all_to_all.10.rows_ref, f32[5,288,128]{2,1,0:T(8,128)S(1)} %get-tuple-element.68.f_ref, f32[5,288,128]{2,1,0:T(8,128)S(1)} %get-tuple-element.69.c_ref, ...), custom_call_target="tpu_custom_call" | custom-call | tf_op jit(solution)/shard_map/pallas_call | solution.py:586
  29.9 8.9 %all_to_all.11.rows_ref = f32[32,1,128]{2,1,0:T(1,128)S(1)} all-to-all(f32[32,1,128]{2,1,0:T(1,128)S(1)} %get-tuple-element.76), channel_id=1, replica_groups=mesh['row'=8,'col'=4] {'row','col'}, dimensions={0} | all-to-all | bytes 32768 | tf_op jit(solution)/shard_map/all_to_all | solution.py:572
  38.8 1.2 %shard_map.72 = (f32[256,512]{1,0:T(8,128)}, f32[1,1]{1,0:T(1,128)}) custom-call(f32[32,1,128]{2,1,0:T(1,128)S(1)} %all_to_all.11.rows_ref, f32[5,288,128]{2,1,0:T(8,128)S(1)} %get-tuple-element.70.p_ref, f32[5,288,128]{2,1,0:T(8,128)S(1)} %get-tuple-element.77.u1_ref, f32[5,288,128]{2,1,0:T(8,128)S(1)} %get-tuple-element.78.u2_ref), custom_call_target="tpu_custom_call" | custom-call | tf_op jit(solution)/shard_map/pallas_call | solution.py:586
  (6 shorter events, 0.0 us)
Async XLA Ops:
  0.6 7.2 %copy-start = (f32[256,512]{1,0:T(8,128)S(1)}, f32[256,512]{1,0:T(8,128)}, u32[]{:S(2)}) copy-start(f32[256,512]{1,0:T(8,128)} %p_in.1) | copy-start | bytes 1572868
  1.6 7.6 %collective-permute-start.1 = (f32[16,512]{1,0:T(8,128)S(1)}, f32[16,512]{1,0:T(8,128)S(1)}, u32[]{:S(2)}, u32[]{:S(2)}) collective-permute-start(f32[16,512]{1,0:T(8,128)S(1)} %get-tuple-element.91), channel_id=1, source_target_pairs={{0,28},{4,8},{8,4},{12,16},{16,12},{20,24},{24,20},{28,0},{1,29},{... | collective-permute-start | bytes 98312 | tf_op jit(solution)/shard_map/ppermute | solution.py:567
  6.2 3.0 %collective-permute-start = (f32[16,512]{1,0:T(8,128)S(1)}, f32[16,512]{1,0:T(8,128)S(1)}, u32[]{:S(2)}, u32[]{:S(2)}) collective-permute-start(f32[16,512]{1,0:T(8,128)S(1)} %get-tuple-element.92), channel_id=1, source_target_pairs={{0,4},{4,0},{8,12},{12,8},{16,20},{20,16},{24,28},{28,24},{1,5},{5... | collective-permute-start | bytes 98312 | tf_op jit(solution)/shard_map/ppermute | solution.py:566
  9.6 4.9 %collective-permute-start.3 = (f32[72,128]{1,0:T(8,128)S(1)}, f32[72,128]{1,0:T(8,128)S(1)}, u32[]{:S(2)}, u32[]{:S(2)}) collective-permute-start(f32[72,128]{1,0:T(8,128)S(1)} %get-tuple-element.52), channel_id=1, source_target_pairs={{0,3},{1,2},{2,1},{3,0},{4,7},{5,6},{6,5},{7,4},{8,11},{9,10},{10,... | collective-permute-start | bytes 110600 | tf_op jit(solution)/shard_map/ppermute | solution.py:567
  12.1 4.0 %collective-permute-start.2 = (f32[72,128]{1,0:T(8,128)S(1)}, f32[72,128]{1,0:T(8,128)S(1)}, u32[]{:S(2)}, u32[]{:S(2)}) collective-permute-start(f32[72,128]{1,0:T(8,128)S(1)} %get-tuple-element.51.after), channel_id=1, source_target_pairs={{0,1},{1,0},{2,3},{3,2},{4,5},{5,4},{6,7},{7,6},{8,9},{9,8},{10,11... | collective-permute-start | bytes 110600 | tf_op jit(solution)/shard_map/ppermute | solution.py:566
